TPU v7x, 128 devices: a whole 4x4x4 slice. The times are simulated.
128 devices in a mesh: inline: 8 (over y, core), xline: 16 (over x, z).
Axes of the slice: x: 4, y: 4, z: 4, core: 2. Of those that a mesh axis runs over, the one named last changes fastest.
Arguments:
- traces: bfloat16 [32768, 1024], P(('inline', 'xline')), may hold values from -6 to 6
- owner: int32 [32768, 1], P(('inline', 'xline')), may hold values from 0 to 127; in each aligned block of 256 rows (0 to 255, 256 to 511, ...) at most 8 rows name the same one
- bin_ids: int32 [32768], P(('inline', 'xline')), may hold values from 0 to 323
- fold: int32 [128, 256], P('inline', 'xline'), may hold values from 1 to 8
- w_first: bfloat16 [32, 3], replicated, may hold values from -3.5 to 3.5
- w_second: bfloat16 [3, 32, 32], replicated, may hold values from -0.625 to 0.625
- w_noise: bfloat16 [32], replicated, may hold values from -1 to 1
- w_volume: bfloat16 [16, 27], replicated, may hold values from -1.25 to 1.25
Outputs:
- features: bfloat16 [128, 16, 256, 1024], P('inline', None, 'xline')
Inputs may be any that keep to these rules, and one draw needn't show every extreme that they name: Of one device's 256 traces at most 8 name the same owner, and in every draw some device sends exactly 8 to some owner.
All inputs are finite; a program needn't handle non-finite values.
Results may differ from a plain program's by a relative error of at most 0.0062.
Values may be sent and summed in bfloat16 or wider, within the bound.
No kernel may reach another device: no remote copies, remote signals or barrier semaphores. Data moves between devices by JAX's collectives and lax.ppermute only.
A program may use at most 192 MiB of HBM per device.

v0:
```python
import jax
import jax.numpy as jnp
from jax import lax
from jax.sharding import PartitionSpec as P


def with_halo(value, sides, width):
    for axis, dim in sides:
        size, length = (lax.axis_size(axis), value.shape[dim])
        up = [(i, (i + 1) % size) for i in range(size - 1)]
        down = [(j, i) for i, j in up]
        last = lax.slice_in_dim(value, length - width, length, axis=dim)
        first = lax.slice_in_dim(value, 0, width, axis=dim)
        before = lax.ppermute(last, axis, up)
        after = lax.ppermute(first, axis, down)
        value = jnp.concatenate([before, value, after], axis=dim)
    return value


def denoise(block, w_first, w_second, w_noise):
    first = lax.conv_general_dilated(
        block[:, None, :],
        w_first[:, None, :],
        (1,),
        ((1, 1),),
        dimension_numbers=("NCH", "OIH", "NCH"),
        preferred_element_type=jnp.float32,
    )
    hidden = jax.nn.relu(first).astype(jnp.bfloat16)
    kernel = jnp.transpose(w_second, (1, 2, 0))
    total = lax.conv_general_dilated(
        hidden,
        kernel,
        (1,),
        ((4, 4),),
        rhs_dilation=(4,),
        dimension_numbers=("NCH", "OIH", "NCH"),
        preferred_element_type=jnp.float32,
    )
    second = jax.nn.relu(total)
    noise = jnp.einsum(
        "c,nct->nt", w_noise.astype(jnp.float32), second, precision=lax.Precision.HIGHEST
    )
    return (block.astype(jnp.float32) - noise).astype(jnp.bfloat16)


def body(traces, owner, bin_ids, fold, w_first, w_second, w_noise, w_volume):
    n_inline = lax.axis_size("inline")
    n_xline = lax.axis_size("xline")
    devices = n_inline * n_xline
    tr_count, samples = traces.shape
    capacity = 4 * tr_count // devices
    tile_x, tile_y = fold.shape
    out_channels = w_volume.shape[0]
    blocks = traces.reshape(tr_count // 64, 64, samples)
    denoised = lax.map(lambda blk: denoise(blk, w_first, w_second, w_noise), blocks).reshape(
        tr_count, samples
    )
    target = owner[:, 0]
    chosen = (target[:, None] == jnp.arange(devices, dtype=jnp.int32)[None, :]).astype(jnp.int32)
    before = jnp.cumsum(chosen, axis=0) - chosen
    rank = jnp.sum(before * chosen, axis=1)
    slot = target * capacity + rank
    placing = slot[None, :] == jnp.arange(devices * capacity, dtype=jnp.int32)[:, None]
    outgoing = jnp.dot(
        placing.astype(jnp.bfloat16), denoised, preferred_element_type=jnp.float32
    ).astype(jnp.bfloat16)
    out_bins = jnp.sum(jnp.where(placing, bin_ids[None, :], 0), axis=1)
    received, recv_bins = (
        lax.all_to_all(
            outgoing.reshape(devices, capacity, samples),
            ("inline", "xline"),
            split_axis=0,
            concat_axis=0,
            tiled=True,
        ),
        lax.all_to_all(
            out_bins.reshape(devices, capacity),
            ("inline", "xline"),
            split_axis=0,
            concat_axis=0,
            tiled=True,
        ),
    )
    received = received.reshape(devices * capacity, samples)
    recv_bins = recv_bins.reshape(devices * capacity)
    extended = (tile_x + 2) * (tile_y + 2)
    selector = (jnp.arange(extended, dtype=jnp.int32)[:, None] == recv_bins[None, :]).astype(
        jnp.bfloat16
    )
    partial_stack = jnp.dot(selector, received, preferred_element_type=jnp.float32)
    partial_stack = partial_stack.reshape(tile_x + 2, tile_y + 2, samples)
    framed = with_halo(partial_stack, (("inline", 0), ("xline", 1)), 1)
    rows_done = (
        framed[2:-2]
        + jnp.pad(framed[0:1], ((0, tile_x - 1), (0, 0), (0, 0)))
        + jnp.pad(framed[-1:], ((tile_x - 1, 0), (0, 0), (0, 0)))
    )
    stack = (
        rows_done[:, 2:-2]
        + jnp.pad(rows_done[:, 0:1], ((0, 0), (0, tile_y - 1), (0, 0)))
        + jnp.pad(rows_done[:, -1:], ((0, 0), (tile_y - 1, 0), (0, 0)))
    )
    volume = (stack / fold[:, :, None].astype(jnp.float32)).astype(jnp.bfloat16)
    bordered = with_halo(volume, (("inline", 0), ("xline", 1)), 1)
    layered = jnp.stack([bordered[0:tile_x], bordered[1 : tile_x + 1], bordered[2 : tile_x + 2]], 1)
    kernel = w_volume.reshape(out_channels, 3, 3, 3)
    result = lax.conv_general_dilated(
        layered,
        kernel,
        (1, 1),
        ((0, 0), (1, 1)),
        dimension_numbers=("NCHW", "OIHW", "NCHW"),
        preferred_element_type=jnp.float32,
    )
    return result.astype(jnp.bfloat16)


def solution(mesh):
    placed = (
        P(("inline", "xline"), None),
        P(("inline", "xline"), None),
        P(("inline", "xline")),
        P("inline", "xline"),
        P(),
        P(),
        P(),
        P(),
    )
    return jax.shard_map(
        body,
        mesh=mesh,
        in_specs=placed,
        out_specs=P("inline", None, "xline", None),
        check_vma=False,
    )
```

profile of v0, /device:TPU:1, one launch (start us, length us, event | category | flops | bytes accessed | tf_op | source)
XLA Modules:
  0.0 349.1 jit_solution(7142819789819713080)
XLA Ops:
  4.3 11.5 %all-to-all-start = ((s32[128,1,8]{2,1,0:T(1,128)}), s32[128,1,8]{2,1,0:T(1,128)S(1)}, u32[]{:S(2)}, u32[]{:S(2)}) async-start(s32[128,1,8]{2,1,0:T(1,128)} %bitcast.11), calls=%async_computation | async-start | bytes 131072 | tf_op jit(solution)/shard_map/all_to_all | solution.py:77
  15.8 128.8 %while.10 = (s32[]{:T(128)}, bf16[4,64,1024]{2,1,0:T(8,128)(2,1)S(1)}, bf16[4,64,1024]{2,1,0:T(8,128)(2,1)}, bf16[32,3]{0,1:T(4,128)(2,1)}, bf16[3,32,32]{2,1,0:T(8,128)(2,1)}, /*index=5*/bf16[32]{0:T(256)(128)(2,1)}, s32[]{:T(128)}) while((s32[]{:T(128)}, bf16[4,64,1024]{2,1,0:T(8,128)(2,1)S(1)}, bf16[4,64,1024]{2,1,0:T(8,128)(2,1)}, ...), condition=%wide.region_5.6_spmd, body=%wide.region_4.5_spmd.sunk | while | flops 445833216 | bytes 35003000 | solution.py:56
  17.1 9.9 %convolution_maximum_fusion.2 = f32[64,32,1024]{0,1,2:T(8,128)} fusion(bf16[3,32,32]{2,1,0:T(8,128)(2,1)} %get-tuple-element.116, bf16[64,1,1024]{0,1,2:T(2,128)(2,1)S(1)} %copy.106, bf16[32,1,3]{0,2,1:T(4,128)(2,1)} %bitcast.85), kind=kOutput, calls=%fused_computation.1.clone.1 | convolution fusion | flops 420470784 | bytes 8526016 | tf_op jit(solution)/shard_map/while/body/eval_jaxpr/conv_general_dilated | solution.py:31
  27.0 13.8 %copy.107 = f32[64,32,1024]{2,1,0:T(8,128)} copy(f32[64,32,1024]{0,1,2:T(8,128)} %convolution_maximum_fusion.2) | data formatting | bytes 16777216 | tf_op jit(solution)/shard_map/while/body/eval_jaxpr/jit(relu)/max | solution.py:40
  40.8 6.2 %fusion.47 = f32[1,64,1024]{2,0,1:T(1,128)S(1)} fusion(f32[64,32,1024]{2,1,0:T(8,128)} %copy.107, bf16[32]{0:T(256)(128)(2,1)S(1)} %copy-done.1), kind=kOutput, calls=%fused_computation.8.clone.1 | convolution fusion | flops 25165824 | bytes 8650816 | tf_op jit(solution)/shard_map/while/body/eval_jaxpr/c,nct->nt/dot_general | solution.py:41
  49.3 9.9 %convolution_maximum_fusion.2 = f32[64,32,1024]{0,1,2:T(8,128)} fusion(bf16[3,32,32]{2,1,0:T(8,128)(2,1)} %get-tuple-element.116, bf16[64,1,1024]{0,1,2:T(2,128)(2,1)S(1)} %copy.106, bf16[32,1,3]{0,2,1:T(4,128)(2,1)} %bitcast.85), kind=kOutput, calls=%fused_computation.1.clone.1 | convolution fusion | flops 420470784 | bytes 8526016 | tf_op jit(solution)/shard_map/while/body/eval_jaxpr/conv_general_dilated | solution.py:31
  59.2 13.8 %copy.107 = f32[64,32,1024]{2,1,0:T(8,128)} copy(f32[64,32,1024]{0,1,2:T(8,128)} %convolution_maximum_fusion.2) | data formatting | bytes 16777216 | tf_op jit(solution)/shard_map/while/body/eval_jaxpr/jit(relu)/max | solution.py:40
  73.0 6.2 %fusion.47 = f32[1,64,1024]{2,0,1:T(1,128)S(1)} fusion(f32[64,32,1024]{2,1,0:T(8,128)} %copy.107, bf16[32]{0:T(256)(128)(2,1)S(1)} %copy-done.1), kind=kOutput, calls=%fused_computation.8.clone.1 | convolution fusion | flops 25165824 | bytes 8650816 | tf_op jit(solution)/shard_map/while/body/eval_jaxpr/c,nct->nt/dot_general | solution.py:41
  81.5 9.9 %convolution_maximum_fusion.2 = f32[64,32,1024]{0,1,2:T(8,128)} fusion(bf16[3,32,32]{2,1,0:T(8,128)(2,1)} %get-tuple-element.116, bf16[64,1,1024]{0,1,2:T(2,128)(2,1)S(1)} %copy.106, bf16[32,1,3]{0,2,1:T(4,128)(2,1)} %bitcast.85), kind=kOutput, calls=%fused_computation.1.clone.1 | convolution fusion | flops 420470784 | bytes 8526016 | tf_op jit(solution)/shard_map/while/body/eval_jaxpr/conv_general_dilated | solution.py:31
  91.4 13.8 %copy.107 = f32[64,32,1024]{2,1,0:T(8,128)} copy(f32[64,32,1024]{0,1,2:T(8,128)} %convolution_maximum_fusion.2) | data formatting | bytes 16777216 | tf_op jit(solution)/shard_map/while/body/eval_jaxpr/jit(relu)/max | solution.py:40
  105.2 6.2 %fusion.47 = f32[1,64,1024]{2,0,1:T(1,128)S(1)} fusion(f32[64,32,1024]{2,1,0:T(8,128)} %copy.107, bf16[32]{0:T(256)(128)(2,1)S(1)} %copy-done.1), kind=kOutput, calls=%fused_computation.8.clone.1 | convolution fusion | flops 25165824 | bytes 8650816 | tf_op jit(solution)/shard_map/while/body/eval_jaxpr/c,nct->nt/dot_general | solution.py:41
  113.7 9.9 %convolution_maximum_fusion.2 = f32[64,32,1024]{0,1,2:T(8,128)} fusion(bf16[3,32,32]{2,1,0:T(8,128)(2,1)} %get-tuple-element.116, bf16[64,1,1024]{0,1,2:T(2,128)(2,1)S(1)} %copy.106, bf16[32,1,3]{0,2,1:T(4,128)(2,1)} %bitcast.85), kind=kOutput, calls=%fused_computation.1.clone.1 | convolution fusion | flops 420470784 | bytes 8526016 | tf_op jit(solution)/shard_map/while/body/eval_jaxpr/conv_general_dilated | solution.py:31
  123.6 13.8 %copy.107 = f32[64,32,1024]{2,1,0:T(8,128)} copy(f32[64,32,1024]{0,1,2:T(8,128)} %convolution_maximum_fusion.2) | data formatting | bytes 16777216 | tf_op jit(solution)/shard_map/while/body/eval_jaxpr/jit(relu)/max | solution.py:40
  137.5 6.2 %fusion.47 = f32[1,64,1024]{2,0,1:T(1,128)S(1)} fusion(f32[64,32,1024]{2,1,0:T(8,128)} %copy.107, bf16[32]{0:T(256)(128)(2,1)S(1)} %copy-done.1), kind=kOutput, calls=%fused_computation.8.clone.1 | convolution fusion | flops 25165824 | bytes 8650816 | tf_op jit(solution)/shard_map/while/body/eval_jaxpr/c,nct->nt/dot_general | solution.py:41
  144.6 2.0 convert_bitcast_fusion
  146.7 9.8 %all-to-all-start.1 = ((bf16[128,8,1024]{2,1,0:T(8,128)(2,1)}), bf16[128,8,1024]{2,1,0:T(8,128)(2,1)S(1)}, u32[]{:S(2)}, u32[]{:S(2)}) async-start(bf16[128,8,1024]{2,1,0:T(8,128)(2,1)} %convert_bitcast_fusion), calls=%async_computation.1 | async-start | bytes 4194304 | tf_op jit(solution)/shard_map/all_to_all | solution.py:70
  157.9 28.1 %all-to-all-done.1 = bf16[128,8,1024]{2,1,0:T(8,128)(2,1)S(1)} async-done(((bf16[128,8,1024]{2,1,0:T(8,128)(2,1)}), bf16[128,8,1024]{2,1,0:T(8,128)(2,1)S(1)}, u32[]{:S(2)}, u32[]{:S(2)}) %all-to-all-start.1) | async-done | bytes 2097184 | tf_op jit(solution)/shard_map/all_to_all | solution.py:70
  187.7 3.3 collective-permute-start
  191.0 2.1 collective-permute-start.1
  193.1 1.5 reshape.61
  198.2 2.8 collective-permute-start.2
  201.1 1.3 collective-permute-start.3
  202.7 3.8 %collective-permute-done.3 = f32[20,1,1024]{2,0,1:T(8,128)S(1)} collective-permute-done((f32[20,1,1024]{2,0,1:T(8,128)S(1)}, f32[20,1,1024]{2,0,1:T(8,128)S(1)}, u32[]{:S(2)}, u32[]{:S(2)}) %collective-permute-start.3) | collective-permute-done | bytes 81952 | tf_op jit(solution)/shard_map/ppermute | solution.py:15
  207.8 4.2 %collective-permute-start.4 = (bf16[1,16,1024]{2,0,1:T(2,128)(2,1)S(1)}, bf16[1,16,1024]{2,0,1:T(2,128)(2,1)S(1)}, u32[]{:S(2)}, u32[]{:S(2)}) collective-permute-start(bf16[1,16,1024]{2,0,1:T(2,128)(2,1)S(1)} %get-tuple-element.59), channel_id=1, source_target_pairs={{0,16},{16,32},{32,48},{48,64},{64,80},{80,96},{96,112},{1,17},{17... | collective-permute-start | bytes 98312 | tf_op jit(solution)/shard_map/ppermute | solution.py:14
  211.9 1.9 collective-permute-start.5
  213.9 3.6 %collective-permute-done.5 = bf16[1,16,1024]{2,0,1:T(2,128)(2,1)S(1)} collective-permute-done((bf16[1,16,1024]{2,0,1:T(2,128)(2,1)S(1)}, bf16[1,16,1024]{2,0,1:T(2,128)(2,1)S(1)}, u32[]{:S(2)}, u32[]{:S(2)}) %collective-permute-start.5) | collective-permute-done | bytes 32800 | tf_op jit(solution)/shard_map/ppermute | solution.py:15
  217.6 1.6 collective-permute-start.6
  219.2 1.3 collective-permute-start.7
  220.7 3.4 collective-permute-done.7
  225.0 19.2 %copy.85 = bf16[16,3,18,1024]{0,1,3,2:T(4,128)(2,1)} copy(bf16[16,3,18,1024]{3,0,2,1:T(8,128)(2,1)S(1)} %pad_maximum_fusion.1) | data formatting | bytes 3538944 | tf_op jit(solution)/shard_map/stack | solution.py:106
  244.2 52.6 %convolution_convert_fusion = bf16[16,16,16,1024]{1,0,3,2:T(8,128)(2,1)} fusion(bf16[16,3,18,1024]{0,1,3,2:T(4,128)(2,1)} %copy.85, bf16[16,3,3,3]{0,3,2,1:T(4,128)(2,1)S(1)} %reshape.62), kind=kOutput, calls=%fused_computation.11 | convolution fusion | flops 230539264 | bytes 10158944 | tf_op jit(solution)/shard_map/conv_general_dilated | solution.py:108
  296.8 52.3 %copy.87 = bf16[16,16,16,1024]{3,2,1,0:T(8,128)(2,1)} copy(bf16[16,16,16,1024]{1,0,3,2:T(8,128)(2,1)} %convolution_convert_fusion) | data formatting | bytes 16777216 | tf_op jit(solution)/shard_map/convert_element_type | solution.py:116
  (69 shorter events, 22.7 us)
Async XLA Ops:
  4.3 142.4 %all-to-all-start = ((s32[128,1,8]{2,1,0:T(1,128)}), s32[128,1,8]{2,1,0:T(1,128)S(1)}, u32[]{:S(2)}, u32[]{:S(2)}) async-start(s32[128,1,8]{2,1,0:T(1,128)} %bitcast.11), calls=%async_computation | async-start | bytes 131072 | tf_op jit(solution)/shard_map/all_to_all | solution.py:77
  27.0 13.8 %copy-start.1 = (bf16[32]{0:T(256)(128)(2,1)S(1)}, bf16[32]{0:T(256)(128)(2,1)}, u32[]{:S(2)}) copy-start(bf16[32]{0:T(256)(128)(2,1)} %get-tuple-element.117) | copy-start | bytes 196 | tf_op jit(solution)/shard_map/while
  59.2 13.8 %copy-start.1 = (bf16[32]{0:T(256)(128)(2,1)S(1)}, bf16[32]{0:T(256)(128)(2,1)}, u32[]{:S(2)}) copy-start(bf16[32]{0:T(256)(128)(2,1)} %get-tuple-element.117) | copy-start | bytes 196 | tf_op jit(solution)/shard_map/while
  91.4 13.8 %copy-start.1 = (bf16[32]{0:T(256)(128)(2,1)S(1)}, bf16[32]{0:T(256)(128)(2,1)}, u32[]{:S(2)}) copy-start(bf16[32]{0:T(256)(128)(2,1)} %get-tuple-element.117) | copy-start | bytes 196 | tf_op jit(solution)/shard_map/while
  123.6 13.8 %copy-start.1 = (bf16[32]{0:T(256)(128)(2,1)S(1)}, bf16[32]{0:T(256)(128)(2,1)}, u32[]{:S(2)}) copy-start(bf16[32]{0:T(256)(128)(2,1)} %get-tuple-element.117) | copy-start | bytes 196 | tf_op jit(solution)/shard_map/while
  146.7 39.4 %all-to-all-start.1 = ((bf16[128,8,1024]{2,1,0:T(8,128)(2,1)}), bf16[128,8,1024]{2,1,0:T(8,128)(2,1)S(1)}, u32[]{:S(2)}, u32[]{:S(2)}) async-start(bf16[128,8,1024]{2,1,0:T(8,128)(2,1)} %convert_bitcast_fusion), calls=%async_computation.1 | async-start | bytes 4194304 | tf_op jit(solution)/shard_map/all_to_all | solution.py:70
  186.9 4.0 %copy-start = (f32[324,1024]{1,0:T(8,128)}, f32[324,1024]{1,0:T(8,128)S(1)}, u32[]{:S(2)}) copy-start(f32[324,1024]{1,0:T(8,128)S(1)} %fusion.8) | copy-start | bytes 3981316
  187.7 7.7 %collective-permute-start = (f32[1,18,1024]{2,1,0:T(8,128)}, f32[1,18,1024]{2,1,0:T(8,128)}, u32[]{:S(2)}, u32[]{:S(2)}) collective-permute-start(f32[1,18,1024]{2,1,0:T(8,128)} %get-tuple-element.52), channel_id=1, source_target_pairs={{0,16},{16,32},{32,48},{48,64},{64,80},{80,96},{96,112},{1,17},{17... | collective-permute-start | bytes 221192 | tf_op jit(solution)/shard_map/ppermute | solution.py:14
  191.0 6.3 %collective-permute-start.1 = (f32[1,18,1024]{2,1,0:T(8,128)}, f32[1,18,1024]{2,1,0:T(8,128)}, u32[]{:S(2)}, u32[]{:S(2)}) collective-permute-start(f32[1,18,1024]{2,1,0:T(8,128)} %get-tuple-element.53), channel_id=1, source_target_pairs={{16,0},{32,16},{48,32},{64,48},{80,64},{96,80},{112,96},{17,1},{33... | collective-permute-start | bytes 221192 | tf_op jit(solution)/shard_map/ppermute | solution.py:15
  195.4 7.0 %copy-start.2 = (s32[16,16]{1,0:T(8,128)S(1)}, s32[16,16]{1,0:T(8,128)}, u32[]{:S(2)}) copy-start(s32[16,16]{1,0:T(8,128)} %param.13) | copy-start | bytes 3076
  198.2 4.4 %collective-permute-start.2 = (f32[20,1,1024]{2,0,1:T(8,128)S(1)}, f32[20,1,1024]{2,0,1:T(8,128)S(1)}, u32[]{:S(2)}, u32[]{:S(2)}) collective-permute-start(f32[20,1,1024]{2,0,1:T(8,128)S(1)} %get-tuple-element.50), channel_id=1, source_target_pairs={{0,1},{1,2},{2,3},{3,4},{4,5},{5,6},{6,7},{7,8},{8,9},{9,10},{10,1... | collective-permute-start | bytes 245768 | tf_op jit(solution)/shard_map/ppermute | solution.py:14
  201.1 5.4 %collective-permute-start.3 = (f32[20,1,1024]{2,0,1:T(8,128)S(1)}, f32[20,1,1024]{2,0,1:T(8,128)S(1)}, u32[]{:S(2)}, u32[]{:S(2)}) collective-permute-start(f32[20,1,1024]{2,0,1:T(8,128)S(1)} %get-tuple-element.51), channel_id=1, source_target_pairs={{1,0},{2,1},{3,2},{4,3},{5,4},{6,5},{7,6},{8,7},{9,8},{10,9},{11,1... | collective-permute-start | bytes 245768 | tf_op jit(solution)/shard_map/ppermute | solution.py:15
  202.5 4.4 %copy-start.4 = (pred[16]{0:T(512)(128)(4,1)S(1)}, pred[16]{0:T(512)(128)(4,1)}, u32[]{:S(2)}) copy-start(pred[16]{0:T(512)(128)(4,1)} %constant.26.clone.1) | copy-start | bytes 52
  207.4 13.1 %copy-start.3 = (bf16[16,27]{1,0:T(8,128)(2,1)S(1)}, bf16[16,27]{1,0:T(8,128)(2,1)}, u32[]{:S(2)}) copy-start(bf16[16,27]{1,0:T(8,128)(2,1)} %param.17) | copy-start | bytes 2596
  207.8 6.1 %collective-permute-start.4 = (bf16[1,16,1024]{2,0,1:T(2,128)(2,1)S(1)}, bf16[1,16,1024]{2,0,1:T(2,128)(2,1)S(1)}, u32[]{:S(2)}, u32[]{:S(2)}) collective-permute-start(bf16[1,16,1024]{2,0,1:T(2,128)(2,1)S(1)} %get-tuple-element.59), channel_id=1, source_target_pairs={{0,16},{16,32},{32,48},{48,64},{64,80},{80,96},{96,112},{1,17},{17... | collective-permute-start | bytes 98312 | tf_op jit(solution)/shard_map/ppermute | solution.py:14
  211.9 5.6 %collective-permute-start.5 = (bf16[1,16,1024]{2,0,1:T(2,128)(2,1)S(1)}, bf16[1,16,1024]{2,0,1:T(2,128)(2,1)S(1)}, u32[]{:S(2)}, u32[]{:S(2)}) collective-permute-start(bf16[1,16,1024]{2,0,1:T(2,128)(2,1)S(1)} %get-tuple-element.60), channel_id=1, source_target_pairs={{16,0},{32,16},{48,32},{64,48},{80,64},{96,80},{112,96},{17,1},{33... | collective-permute-start | bytes 98312 | tf_op jit(solution)/shard_map/ppermute | solution.py:15
  217.6 3.1 collective-permute-start.6
  219.2 4.8 %collective-permute-start.7 = (bf16[18,1,1024]{2,0,1:T(8,128)(2,1)S(1)}, bf16[18,1,1024]{2,0,1:T(8,128)(2,1)S(1)}, u32[]{:S(2)}, u32[]{:S(2)}) collective-permute-start(bf16[18,1,1024]{2,0,1:T(8,128)(2,1)S(1)} %get-tuple-element.58), channel_id=1, source_target_pairs={{1,0},{2,1},{3,2},{4,3},{5,4},{6,5},{7,6},{8,7},{9,8},{10,9},{11,1... | collective-permute-start | bytes 110600 | tf_op jit(solution)/shard_map/ppermute | solution.py:15
where the time goes:
time: 354 us; the launch traced here: 349 us
  local copies, waits for them, and re-layouts  140 us (40%)
  matrix products  120 us (34%)
  waiting for transfers between devices  40.1 us (11%)
  starting transfers between devices  39.7 us (11%)
  other arithmetic  9.18 us (3%)
    max x4, local copies, waits for them, and re-layouts, denoise(): second = jax.nn.relu(total)  55.3 us
    conv_general_dilated x1, matrix products, body(): lax.conv_general_dilated(layered, kernel, (1, 1), ((0, 0), (1, 1)), dimen...  52.6 us
    convert_element_type x1, local copies, waits for them, and re-layouts, body(): return result.astype(jnp.bfloat16)  52.3 us
    conv_general_dilated x4, matrix products, denoise(): lax.conv_general_dilated(hidden, kernel, (1,), ((4, 4),), rhs_dilation=(4...  39.6 us
    all_to_all x1, waiting for transfers between devices, body(): lax.all_to_all(outgoing.reshape(devices, capacity, samples), ('inline', '...  28.1 us
    dot_general x4, matrix products, denoise(): jnp.einsum('c,nct->nt', w_noise.astype(jnp.float32), second, precision=la...  24.7 us
    another operation x2, local copies, waits for them, and re-layouts, body(): jnp.stack([bordered[0:tile_x], bordered[1:tile_x + 1], bordered[2:tile_x...  19.5 us
    ppermute x4, starting transfers between devices, with_halo(): before = lax.ppermute(last, axis, up)  11.9 us
  transfers between devices with their start and end apart: 10, of which 6 were waited for; matrix products, arithmetic and copies ran while one was open for 39% of the time, Pallas kernels for 0%

commit v1 on v0

v1 whole, which is shorter than its diff:
```python
import jax
import jax.numpy as jnp
from jax import lax
from jax.experimental import pallas as pl
from jax.experimental.pallas import tpu as pltpu
from jax.sharding import PartitionSpec as P

F32 = jnp.float32
BF16 = jnp.bfloat16
WIN = 24
PAD = 8
QP = 24
TAIL = 128


def iota(shape, dim):
    return lax.broadcasted_iota(jnp.int32, shape, dim)


def first_weights(w_first):
    shape = (4, 8, 32, 48)
    delta = iota(shape, 3) - 4 * iota(shape, 1) - iota(shape, 0) - 3
    out = jnp.zeros(shape, BF16)
    for k in range(3):
        out = jnp.where(delta == k, w_first[:, k][None, None, :, None], out)
    return out.reshape(1024, 48)


def second_weights(w_second):
    shape = (3, 8, 2, 4, 256)
    step = iota(shape, 4) // 32 - 2 * iota(shape, 0) - iota(shape, 2)
    out = jnp.zeros(shape, BF16)
    for k in range(3):
        wide = jnp.tile(w_second[k], (1, 8)).reshape(8, 4, 256)
        out = jnp.where(step == k, wide[None, :, None], out)
    return out.reshape(192, 256)


def noise_weights(w_noise):
    w = w_noise.astype(F32).reshape(8, 1, 4)
    return jnp.broadcast_to(jnp.broadcast_to(w, (8, 2, 4)).reshape(64, 1), (64, 256))


def volume_weights(w_volume):
    w = w_volume.reshape(16, 3, 3, 3).transpose(0, 1, 3, 2)
    shape = (16, 16, 3, 3, QP)
    delta = iota(shape, 4) - iota(shape, 1)
    out = jnp.zeros(shape, BF16)
    for k in range(3):
        out = jnp.where(delta == k, w[:, None, :, :, k][..., None], out)
    return jnp.pad(out.reshape(256, 9 * QP), ((0, 0), (0, 8)))


def denoise_kernel(x_ref, own_col_ref, own_row_ref, bins_ref, w1_ref, w2_ref, wn_ref, out_ref, xt, dt):
    traces, samples = x_ref.shape
    slots = out_ref.shape[0]
    rows = xt.shape[0]
    xt[0:PAD, :] = jnp.zeros((PAD, traces), F32)
    xt[PAD + samples : rows, :] = jnp.zeros((rows - PAD - samples, traces), F32)
    for k in range(samples // 128):
        xt[PAD + 128 * k : PAD + 128 * (k + 1), :] = x_ref[:, 128 * k : 128 * (k + 1)].astype(F32).T
    windows = -(-samples // WIN)
    sub = iota((3, 8, traces), 1)

    def window(j, low, high):
        start = WIN * j
        if not isinstance(j, int):
            start = pl.multiple_of(start, 8)
        xs = xt[pl.ds(start, 48), :].astype(BF16)
        parts = []
        for p in range(4):
            h = jnp.dot(w1_ref[256 * p : 256 * (p + 1), :], xs, preferred_element_type=F32)
            h = jnp.maximum(h, 0.0).astype(BF16)
            if low or high < 8:
                row = iota((256, traces), 0)
                h = jnp.where((row >= 32 * low) & (row < 32 * high), h, jnp.zeros_like(h))
            o = jnp.dot(w2_ref[...], h, preferred_element_type=F32)
            o = jnp.maximum(o, 0.0).reshape(3, 64, traces) * wn_ref[...][None]
            parts.append(jnp.sum(o.reshape(3, 8, 8, traces), axis=1))
        even = (sub & 1) == 0

        def pair(a, b, shift, mask):
            return jnp.where(mask, a + pltpu.roll(a, 8 - shift, 1), b + pltpu.roll(b, shift, 1))

        lo = pair(parts[0], parts[1], 1, even)
        hi = pair(parts[2], parts[3], 1, even)
        noise = pair(lo, hi, 2, (sub & 2) == 0)
        x = xt[pl.ds(start + PAD, WIN), :]
        dt[pl.ds(start, WIN), :] = x - noise.reshape(WIN, traces)

    window(0, 1, 8)

    def step(j, carry):
        window(j, 0, 8)
        return carry

    lax.fori_loop(1, windows - 1, step, 0)
    last = windows - 1
    window(last, 0, (samples - WIN * last + 4) // 4)

    same = own_col_ref[...] == own_row_ref[...]
    earlier = same & (iota((traces, traces), 0) < iota((traces, traces), 1))
    rank = jnp.sum(jnp.where(earlier, 1.0, 0.0), axis=0, keepdims=True).astype(jnp.int32)
    slot = own_row_ref[...] * 8 + rank
    placing = jnp.where(iota((slots, traces), 0) == slot, 1.0, 0.0).astype(BF16)
    nt = (((1,), (1,)), ((), ()))
    for k in range(samples // 256):
        block = dt[256 * k : 256 * (k + 1), :].astype(BF16)
        out_ref[:, 256 * k : 256 * (k + 1)] = lax.dot_general(
            placing, block, nt, preferred_element_type=F32
        ).astype(BF16)
    which = iota((TAIL, traces), 0)
    row, col = bins_ref[...] // 18 + 1, bins_ref[...] % 18 + 1
    tail = jnp.where(which == 0, row, jnp.where(which == 1, col, 0)).astype(F32).astype(BF16)
    out_ref[:, samples:] = lax.dot_general(placing, tail, nt, preferred_element_type=F32).astype(BF16)


def stack_kernel(recv_ref, fold_ref, main_ref, up_ref, down_ref, cols_ref):
    slots = recv_ref.shape[0]
    blocks, bins, _ = main_ref.shape
    samples = recv_ref.shape[1] - TAIL
    tail = recv_ref[:, samples:].astype(F32).T
    place = ((tail[0:1] - 1.0) * QP + (tail[1:2] - 1.0)).astype(jnp.int32)
    select = jnp.where(iota((bins, slots), 0) == place, 1.0, 0.0).astype(BF16)
    for c in range(0, blocks - 1, 2):
        both = jnp.dot(select, recv_ref[:, 128 * c : 128 * (c + 2)], preferred_element_type=F32)
        main_ref[c] = both[:, :128]
        main_ref[c + 1] = both[:, 128:]
    main_ref[blocks - 1] = fold_ref[...]
    for c in range(blocks):
        lanes = slice(128 * c, 128 * (c + 1))
        up_ref[:, lanes] = main_ref[c, 0 : 2 * QP, :].astype(BF16)
        down_ref[:, lanes] = main_ref[c, bins - 2 * QP : bins, :].astype(BF16)
        for k, q in enumerate((0, 1, 16, 17)):
            cols_ref[c, 24 * k : 24 * k + 18, :] = main_ref[c, pl.ds(q, 18, stride=QP), :]
            cols_ref[c, 24 * k + 18 : 24 * k + 24, :] = jnp.zeros((6, 128), F32)


def columns_kernel(cols_ref, above_ref, below_ref, left_ref, right_ref, acc):
    blocks = cols_ref.shape[0]
    for c in range(blocks):
        acc[:, 128 * c : 128 * (c + 1)] = cols_ref[c]
    above = above_ref[...].astype(F32)
    below = below_ref[...].astype(F32)
    for k, q in enumerate((0, 1, 16, 17)):
        for r in range(2):
            acc[24 * k + r : 24 * k + r + 1, :] += above[r * QP + q : r * QP + q + 1, :]
            acc[24 * k + 16 + r : 24 * k + 17 + r, :] += below[r * QP + q : r * QP + q + 1, :]
    left_ref[...] = acc[0:48, :].astype(BF16)
    right_ref[...] = acc[48:96, :].astype(BF16)


def volume_kernel(main_ref, above_ref, below_ref, left_ref, right_ref, w_ref, out_ref, acc, vs):
    blocks, bins, _ = acc.shape
    samples = 128 * (blocks - 1)
    planes = bins // QP

    @pl.when(pl.program_id(0) == 0)
    def _():
        acc[...] = main_ref[...]
        for c in range(blocks):
            lanes = slice(128 * c, 128 * (c + 1))
            acc[c, 0 : 2 * QP, :] += above_ref[:, lanes].astype(F32)
            acc[c, bins - 2 * QP : bins, :] += below_ref[:, lanes].astype(F32)
            for ref, first in ((left_ref, 0), (right_ref, 16)):
                strip = ref[:, lanes].astype(F32)
                for k in range(2):
                    acc[c, pl.ds(first + k, planes, stride=QP), :] += strip[24 * k : 24 * k + planes, :]
        vs[planes * 3 * QP :, :] = jnp.zeros((8, samples), F32)
        lane = iota((QP, samples), 1)

        def plane(r, carry):
            rows = pl.ds(pl.multiple_of(r * QP, 8), QP)
            fold = acc[blocks - 1, rows, :]
            inside = fold > 0.0
            fold = jnp.where(inside, fold, 1.0)
            v = jnp.concatenate(
                [jnp.where(inside, acc[c, rows, :] / fold, 0.0) for c in range(blocks - 1)], axis=1
            )
            v = v.astype(BF16).astype(F32)
            before = jnp.where(lane == 0, 0.0, pltpu.roll(v, 1, 1))
            after = jnp.where(lane == samples - 1, 0.0, pltpu.roll(v, samples - 1, 1))
            base = r * 3 * QP
            vs[pl.ds(pl.multiple_of(base, 8), QP), :] = before
            vs[pl.ds(pl.multiple_of(base + QP, 8), QP), :] = v
            vs[pl.ds(pl.multiple_of(base + 2 * QP, 8), QP), :] = after
            return carry

        lax.fori_loop(0, planes, plane, 0)

    base = pl.multiple_of(pl.program_id(0) * 3 * QP, 8)
    taps = vs[pl.ds(base, 9 * QP + 8), :].astype(BF16)
    out = jnp.dot(w_ref[...], taps, preferred_element_type=F32)
    out_ref[...] = out.astype(BF16).reshape(out_ref.shape)


def neighbours(first, last, axis):
    size = lax.axis_size(axis)
    up = [(i, i + 1) for i in range(size - 1)]
    down = [(j, i) for i, j in up]
    return lax.ppermute(last, axis, up), lax.ppermute(first, axis, down)


def body(traces, owner, bin_ids, fold, w_first, w_second, w_noise, w_volume):
    devices = lax.axis_size("inline") * lax.axis_size("xline")
    count, samples = traces.shape
    slots = devices * 8
    width = samples + TAIL
    vmem = pl.BlockSpec(memory_space=pltpu.VMEM)
    params = pltpu.CompilerParams(vmem_limit_bytes=56 << 20)
    rows = WIN * (-(-samples // WIN))
    outgoing = pl.pallas_call(
        denoise_kernel,
        out_shape=jax.ShapeDtypeStruct((slots, width), BF16),
        in_specs=[vmem] * 7,
        out_specs=vmem,
        scratch_shapes=[pltpu.VMEM((rows + 32, count), F32), pltpu.VMEM((rows, count), F32)],
        compiler_params=params,
        name="denoise",
    )(
        traces,
        owner,
        owner.reshape(1, count),
        bin_ids.reshape(1, count),
        first_weights(w_first),
        second_weights(w_second),
        noise_weights(w_noise),
    )
    received = lax.all_to_all(
        outgoing.reshape(devices, 8, width), ("inline", "xline"), split_axis=0, concat_axis=0, tiled=True
    ).reshape(slots, width)
    folds = jnp.pad(fold.astype(F32), ((1, 1), (1, QP - 17)))
    folds = jnp.broadcast_to(folds[:, :, None], (18, QP, TAIL)).reshape(18 * QP, TAIL)
    bins = 18 * QP
    main, up, down, cols = pl.pallas_call(
        stack_kernel,
        out_shape=[
            jax.ShapeDtypeStruct((width // 128, bins, 128), F32),
            jax.ShapeDtypeStruct((2 * QP, width), BF16),
            jax.ShapeDtypeStruct((2 * QP, width), BF16),
            jax.ShapeDtypeStruct((width // 128, 96, 128), F32),
        ],
        in_specs=[vmem] * 2,
        out_specs=[vmem] * 4,
        compiler_params=params,
        name="stack",
    )(received, folds)
    above, below = neighbours(up, down, "inline")
    left, right = pl.pallas_call(
        columns_kernel,
        out_shape=[jax.ShapeDtypeStruct((48, width), BF16)] * 2,
        in_specs=[vmem] * 3,
        out_specs=[vmem] * 2,
        scratch_shapes=[pltpu.VMEM((96, width), F32)],
        compiler_params=params,
        name="columns",
    )(cols, above, below)
    from_left, from_right = neighbours(left, right, "xline")
    whole = lambda *shape: pl.BlockSpec(shape, lambda x: (0,) * len(shape))
    return pl.pallas_call(
        volume_kernel,
        out_shape=jax.ShapeDtypeStruct((16, 16, 16, samples), BF16),
        grid=(16,),
        in_specs=[
            whole(width // 128, bins, 128),
            whole(2 * QP, width),
            whole(2 * QP, width),
            whole(48, width),
            whole(48, width),
            whole(256, 9 * QP + 8),
        ],
        out_specs=pl.BlockSpec((1, 16, 16, samples), lambda x: (x, 0, 0, 0)),
        scratch_shapes=[pltpu.VMEM((width // 128, bins, 128), F32), pltpu.VMEM((bins * 3 + 8, samples), F32)],
        compiler_params=params,
        name="volume",
    )(main, above, below, from_left, from_right, volume_weights(w_volume))


def solution(mesh):
    placed = (
        P(("inline", "xline"), None),
        P(("inline", "xline"), None),
        P(("inline", "xline")),
        P("inline", "xline"),
        P(),
        P(),
        P(),
        P(),
    )
    return jax.shard_map(
        body,
        mesh=mesh,
        in_specs=placed,
        out_specs=P("inline", None, "xline", None),
        check_vma=False,
    )
```

time: 354 us -> 135 us (0.38); the launches traced: 349 us -> 135 us
  local copies, waits for them, and re-layouts: 140 us -> 11.9 us
  matrix products: 120 us -> 0 us
  Pallas kernels: 0 us -> 61.7 us
  starting transfers between devices: 39.7 us -> 20.6 us
  other arithmetic: 9.18 us -> 2.64 us
    conv_general_dilated x5 -> x0, matrix products: 92.2 us -> none  [the longest x1 52.6 us: body(): lax.conv_general_dilated(layered, kernel, (1, 1), ((0, 0), (1, 1)), dimen...]
    pallas_call x0 -> x4, Pallas kernels: none -> 61.7 us  [the longest x1 42.5 us: body(): pl.pallas_call(denoise_kernel, out_shape=jax.ShapeDtypeStruct((slots, wid...]
    max x4 -> x0, local copies, waits for them, and re-layouts: 55.3 us -> none  [denoise(): second = jax.nn.relu(total)]
    convert_element_type x2 -> x0, local copies, waits for them, and re-layouts: 52.3 us -> none  [the longest x1 52.3 us: body(): return result.astype(jnp.bfloat16)]
    dot_general x6 -> x0, matrix products: 27.6 us -> none  [the longest x4 24.7 us: denoise(): jnp.einsum('c,nct->nt', w_noise.astype(jnp.float32), second, precision=la...]
    another operation x5 -> x4, local copies, waits for them, and re-layouts: 19.5 us -> 0.77 us  [second_weights(): wide = jnp.tile(w_second[k], (1, 8)).reshape(8, 4, 256)]
    all_to_all x2 -> x1, starting transfers between devices: 21.3 us -> 11.5 us  [body(): lax.all_to_all(outgoing.reshape(devices, 8, width), ('inline', 'xline'),...]
    ppermute x8 -> x4, starting transfers between devices: 18.5 us -> 9.15 us  [neighbours(): return (lax.ppermute(last, axis, up), lax.ppermute(first, axis, down))]
  transfers between devices with their start and end apart: 10 -> 5, of which waited for: 6 -> 3; matrix products, arithmetic and copies ran while one was open for 39% -> 3% of each run, Pallas kernels for 0% -> 0%
where the time goes in v1:
time: 135 us
  Pallas kernels  61.7 us (46%)
  waiting for transfers between devices  37.6 us (28%)
  starting transfers between devices  20.6 us (15%)
  local copies, waits for them, and re-layouts  11.9 us (9%)
  other arithmetic  2.64 us (2%)
    pallas_call x1, Pallas kernels, body(): pl.pallas_call(denoise_kernel, out_shape=jax.ShapeDtypeStruct((slots, wid...  42.5 us
    all_to_all x1, waiting for transfers between devices, body(): lax.all_to_all(outgoing.reshape(devices, 8, width), ('inline', 'xline'),...  32.1 us
    pallas_call x1, Pallas kernels, body(): pl.pallas_call(volume_kernel, out_shape=jax.ShapeDtypeStruct((16, 16, 16,...  12.9 us
    all_to_all x1, starting transfers between devices, body(): lax.all_to_all(outgoing.reshape(devices, 8, width), ('inline', 'xline'),...  11.5 us
    ppermute x4, starting transfers between devices, neighbours(): return (lax.ppermute(last, axis, up), lax.ppermute(first, axis, down))  9.15 us
    ppermute x4, waiting for transfers between devices, neighbours(): return (lax.ppermute(last, axis, up), lax.ppermute(first, axis, down))  5.49 us
    pallas_call x1, Pallas kernels, body(): pl.pallas_call(stack_kernel, out_shape=[jax.ShapeDtypeStruct((width // 12...  4.33 us
    unnamed x16, local copies, waits for them, and re-layouts  3.37 us
  transfers between devices with their start and end apart: 5, of which 3 were waited for; matrix products, arithmetic and copies ran while one was open for 3% of the time, Pallas kernels for 0%

profile of v1, /device:TPU:1, one launch (start us, length us, event | category | flops | bytes accessed | tf_op | source)
XLA Modules:
  0.0 134.7 jit_solution(673275215544948796)
XLA Ops:
  0.0 0.8 slice_bitcast_fusion.8
  0.8 0.7 reshape.74
  2.2 0.1 iota.194
  2.5 0.7 slice_bitcast_fusion
  3.8 1.5 %copy.10.own_col_ref = s32[256,1]{1,0:T(8,128)} copy(s32[256,1]{0,1:T(1,128)} %param.9) | data formatting | bytes 2048 | tf_op args[1]
  5.3 1.7 %fusion.3.w1_ref = bf16[1024,48]{1,0:T(8,128)(2,1)} fusion(s32[1024]{0:T(1024)S(1)} %iota.186, s32[1024]{0:T(1024)S(1)} %iota.183, bf16[1024]{0:T(1024)(128)(2,1)S(1)} %broadcast_in_dim.140, bf16[1024]{0:T(1024)(128)(2,1)S(1)} %broadcast_in_dim.136, bf16[1024]{0:T(1024)(128)(2,1)S(1)} %broadcast_in_dim.132), kind=kLoop, calls=%fused_computation.4 | loop fusion | flops 442368 | bytes 112640 | tf_op jit(solution)/shard_map/jit(_where)/select_n | solution.py:25
  6.9 0.8 fusion.12.w2_ref
  7.7 0.7 broadcast_in_dim.157.wn_ref
  8.4 42.5 %denoise.1 = bf16[1024,1152]{1,0:T(8,128)(2,1)} custom-call(bf16[256,1024]{1,0:T(8,128)(2,1)} %x_ref.1, s32[256,1]{1,0:T(8,128)} %copy.10.own_col_ref, s32[1,256]{1,0:T(1,128)} %bitcast.28, s32[1,256]{1,0:T(1,128)} %bitcast.29, bf16[1024,48]{1,0:T(8,128)(2,1)} %fusion.3.w1_ref, bf16[192,256]{1,0:T(8,128)(2,1)} %fusion.12.w2_ref, ...), custom_call_target="tpu_custom_call" | custom-call | tf_op jit(solution)/shard_map/denoise/pallas_call | solution.py:212
  51.0 11.5 %all-to-all-start = ((bf16[128,8,1152]{2,1,0:T(8,128)(2,1)}), bf16[128,8,1152]{2,1,0:T(8,128)(2,1)S(1)}, u32[]{:S(2)}, u32[]{:S(2)}) async-start(bf16[128,8,1152]{2,1,0:T(8,128)(2,1)} %bitcast.26), calls=%async_computation | async-start | bytes 4718592 | tf_op jit(solution)/shard_map/all_to_all | solution.py:229
  62.8 32.1 %all-to-all-done = bf16[128,8,1152]{2,1,0:T(8,128)(2,1)S(1)} async-done(((bf16[128,8,1152]{2,1,0:T(8,128)(2,1)}), bf16[128,8,1152]{2,1,0:T(8,128)(2,1)S(1)}, u32[]{:S(2)}, u32[]{:S(2)}) %all-to-all-start) | async-done | bytes 2359328 | tf_op jit(solution)/shard_map/all_to_all | solution.py:229
  94.9 1.0 broadcast_in_dim.159.fold_ref
  95.9 0.5 copy-done
  96.4 4.3 %stack.1 = (f32[9,432,128]{2,1,0:T(8,128)}, bf16[48,1152]{1,0:T(8,128)(2,1)}, bf16[48,1152]{1,0:T(8,128)(2,1)}, f32[9,96,128]{2,1,0:T(8,128)}) custom-call(bf16[1024,1152]{1,0:T(8,128)(2,1)} %bitcast.25, f32[432,128]{1,0:T(8,128)} %broadcast_in_dim.159.fold_ref), custom_call_target="tpu_custom_call" | custom-call | tf_op jit(solution)/shard_map/stack/pallas_call | solution.py:235
  100.7 3.1 %collective-permute-start = (bf16[48,1152]{1,0:T(8,128)(2,1)}, bf16[48,1152]{1,0:T(8,128)(2,1)S(1)}, u32[]{:S(2)}, u32[]{:S(2)}) collective-permute-start(bf16[48,1152]{1,0:T(8,128)(2,1)} %get-tuple-element.12), channel_id=1, source_target_pairs={{0,16},{16,32},{32,48},{48,64},{64,80},{80,96},{96,112},{1,17},{17... | collective-permute-start | bytes 331784 | tf_op jit(solution)/shard_map/ppermute | solution.py:201
  103.8 1.9 %collective-permute-start.1 = (bf16[48,1152]{1,0:T(8,128)(2,1)}, bf16[48,1152]{1,0:T(8,128)(2,1)S(1)}, u32[]{:S(2)}, u32[]{:S(2)}) collective-permute-start(bf16[48,1152]{1,0:T(8,128)(2,1)} %get-tuple-element.13), channel_id=1, source_target_pairs={{16,0},{32,16},{48,32},{64,48},{80,64},{96,80},{112,96},{17,1},{33... | collective-permute-start | bytes 331784 | tf_op jit(solution)/shard_map/ppermute | solution.py:201
  106.3 0.3 broadcast_in_dim.161
  106.6 0.3 broadcast_in_dim.162
  106.9 0.3 broadcast_in_dim.164
  107.2 0.3 broadcast_in_dim.165
  107.5 0.3 broadcast_in_dim.167
  107.8 0.3 broadcast_in_dim.168
  108.2 1.9 %collective-permute-done.1.below_ref = bf16[48,1152]{1,0:T(8,128)(2,1)S(1)} collective-permute-done((bf16[48,1152]{1,0:T(8,128)(2,1)}, bf16[48,1152]{1,0:T(8,128)(2,1)S(1)}, u32[]{:S(2)}, u32[]{:S(2)}) %collective-permute-start.1) | collective-permute-done | bytes 110624 | tf_op jit(solution)/shard_map/ppermute | solution.py:201
  110.1 0.6 copy-done.2
  110.7 1.9 %columns.1 = (bf16[48,1152]{1,0:T(8,128)(2,1)}, bf16[48,1152]{1,0:T(8,128)(2,1)}) custom-call(f32[9,96,128]{2,1,0:T(8,128)} %get-tuple-element.14.cols_ref, bf16[48,1152]{1,0:T(8,128)(2,1)} %copy-done.1, bf16[48,1152]{1,0:T(8,128)(2,1)} %copy-done.2), custom_call_target="tpu_custom_call" | custom-call | tf_op jit(solution)/shard_map/columns/pallas_call | solution.py:249
  112.6 2.8 %collective-permute-start.2 = (bf16[48,1152]{1,0:T(8,128)(2,1)}, bf16[48,1152]{1,0:T(8,128)(2,1)S(1)}, u32[]{:S(2)}, u32[]{:S(2)}) collective-permute-start(bf16[48,1152]{1,0:T(8,128)(2,1)} %get-tuple-element.15), channel_id=1, source_target_pairs={{0,1},{1,2},{2,3},{3,4},{4,5},{5,6},{6,7},{7,8},{8,9},{9,10},{10,1... | collective-permute-start | bytes 331784 | tf_op jit(solution)/shard_map/ppermute | solution.py:201
  115.5 1.3 collective-permute-start.3
  116.8 0.2 fusion.6
  116.9 0.7 pad.9.w_ref
  117.6 3.6 %collective-permute-done.3.right_ref = bf16[48,1152]{1,0:T(8,128)(2,1)S(1)} collective-permute-done((bf16[48,1152]{1,0:T(8,128)(2,1)}, bf16[48,1152]{1,0:T(8,128)(2,1)S(1)}, u32[]{:S(2)}, u32[]{:S(2)}) %collective-permute-start.3) | collective-permute-done | bytes 110624 | tf_op jit(solution)/shard_map/ppermute | solution.py:201
  121.2 0.6 copy-done.4
  121.8 12.9 %volume.1 = bf16[16,16,16,1024]{3,2,1,0:T(8,128)(2,1)} custom-call(f32[9,432,128]{2,1,0:T(8,128)} %get-tuple-element.11.main_ref, bf16[48,1152]{1,0:T(8,128)(2,1)} %copy-done.1, bf16[48,1152]{1,0:T(8,128)(2,1)} %copy-done.2, bf16[48,1152]{1,0:T(8,128)(2,1)} %copy-done.3, bf16[48,1152]{1,0:T(8,128)(2,1)} %copy-done.4, bf16[256,224]{1,0:T(8,128)(2,1)} %pad.9.w_ref), custom_call_target="tpu_custom_call" | custom-call | tf_op jit(solution)/shard_map/volume/pallas_call | solution.py:260
  (57 shorter events, 2.2 us)
Async XLA Ops:
  51.0 11.5 %copy-start.5 = (s32[16,16]{1,0:T(8,128)S(1)}, s32[16,16]{1,0:T(8,128)}, u32[]{:S(2)}) copy-start(s32[16,16]{1,0:T(8,128)} %param.11) | copy-start | bytes 3076
  51.0 11.7 %copy-start.6 = (bf16[16,27]{1,0:T(8,128)(2,1)S(1)}, bf16[16,27]{1,0:T(8,128)(2,1)}, u32[]{:S(2)}) copy-start(bf16[16,27]{1,0:T(8,128)(2,1)} %param.15) | copy-start | bytes 2596
  51.0 43.9 %all-to-all-start = ((bf16[128,8,1152]{2,1,0:T(8,128)(2,1)}), bf16[128,8,1152]{2,1,0:T(8,128)(2,1)S(1)}, u32[]{:S(2)}, u32[]{:S(2)}) async-start(bf16[128,8,1152]{2,1,0:T(8,128)(2,1)} %bitcast.26), calls=%async_computation | async-start | bytes 4718592 | tf_op jit(solution)/shard_map/all_to_all | solution.py:229
  94.9 1.5 %copy-start = (bf16[128,8,1152]{2,1,0:T(8,128)(2,1)}, bf16[128,8,1152]{2,1,0:T(8,128)(2,1)S(1)}, u32[]{:S(2)}) copy-start(bf16[128,8,1152]{2,1,0:T(8,128)(2,1)S(1)} %all-to-all-done) | copy-start | bytes 7077892
  100.7 7.4 %collective-permute-start = (bf16[48,1152]{1,0:T(8,128)(2,1)}, bf16[48,1152]{1,0:T(8,128)(2,1)S(1)}, u32[]{:S(2)}, u32[]{:S(2)}) collective-permute-start(bf16[48,1152]{1,0:T(8,128)(2,1)} %get-tuple-element.12), channel_id=1, source_target_pairs={{0,16},{16,32},{32,48},{48,64},{64,80},{80,96},{96,112},{1,17},{17... | collective-permute-start | bytes 331784 | tf_op jit(solution)/shard_map/ppermute | solution.py:201
  103.8 6.3 %collective-permute-start.1 = (bf16[48,1152]{1,0:T(8,128)(2,1)}, bf16[48,1152]{1,0:T(8,128)(2,1)S(1)}, u32[]{:S(2)}, u32[]{:S(2)}) collective-permute-start(bf16[48,1152]{1,0:T(8,128)(2,1)} %get-tuple-element.13), channel_id=1, source_target_pairs={{16,0},{32,16},{48,32},{64,48},{80,64},{96,80},{112,96},{17,1},{33... | collective-permute-start | bytes 331784 | tf_op jit(solution)/shard_map/ppermute | solution.py:201
  108.2 1.9 %copy-start.1 = (bf16[48,1152]{1,0:T(8,128)(2,1)}, bf16[48,1152]{1,0:T(8,128)(2,1)S(1)}, u32[]{:S(2)}) copy-start(bf16[48,1152]{1,0:T(8,128)(2,1)S(1)} %collective-permute-done.above_ref) | copy-start | bytes 331780
  110.1 0.6 copy-start.2
  112.6 5.0 %collective-permute-start.2 = (bf16[48,1152]{1,0:T(8,128)(2,1)}, bf16[48,1152]{1,0:T(8,128)(2,1)S(1)}, u32[]{:S(2)}, u32[]{:S(2)}) collective-permute-start(bf16[48,1152]{1,0:T(8,128)(2,1)} %get-tuple-element.15), channel_id=1, source_target_pairs={{0,1},{1,2},{2,3},{3,4},{4,5},{5,6},{6,7},{7,8},{8,9},{9,10},{10,1... | collective-permute-start | bytes 331784 | tf_op jit(solution)/shard_map/ppermute | solution.py:201
  115.5 5.7 %collective-permute-start.3 = (bf16[48,1152]{1,0:T(8,128)(2,1)}, bf16[48,1152]{1,0:T(8,128)(2,1)S(1)}, u32[]{:S(2)}, u32[]{:S(2)}) collective-permute-start(bf16[48,1152]{1,0:T(8,128)(2,1)} %get-tuple-element.16), channel_id=1, source_target_pairs={{1,0},{2,1},{3,2},{4,3},{5,4},{6,5},{7,6},{8,7},{9,8},{10,9},{11,1... | collective-permute-start | bytes 331784 | tf_op jit(solution)/shard_map/ppermute | solution.py:201
  117.6 3.6 %copy-start.3 = (bf16[48,1152]{1,0:T(8,128)(2,1)}, bf16[48,1152]{1,0:T(8,128)(2,1)S(1)}, u32[]{:S(2)}) copy-start(bf16[48,1152]{1,0:T(8,128)(2,1)S(1)} %collective-permute-done.2.left_ref) | copy-start | bytes 331780
  121.2 0.6 copy-start.4

commit v2 on v1

v2 whole, which is shorter than its diff:
```python
import jax
import jax.numpy as jnp
from jax import lax
from jax.experimental import pallas as pl
from jax.experimental.pallas import tpu as pltpu
from jax.sharding import PartitionSpec as P

F32 = jnp.float32
BF16 = jnp.bfloat16
WIN = 24
PAD = 24
QP = 24
TAIL = 128


def iota(shape, dim):
    return lax.broadcasted_iota(jnp.int32, shape, dim)


def picks(shape, row, col):
    return jnp.where(jnp.broadcast_to(row == col, shape), 1.0, 0.0).astype(BF16)


def column(vector, size):
    eye = iota((size, size), 0) == iota((size, size), 1)
    return jnp.sum(jnp.where(eye, vector, 0.0), axis=1, keepdims=True)


def denoise_kernel(x_ref, own_ref, bins_ref, wf_ref, ws_ref, wn_ref, out_ref, xt, dt, ha, hb, w1, w2, wn):
    traces, samples = x_ref.shape
    slots = out_ref.shape[0]
    rows = xt.shape[0]
    windows = -(-samples // WIN)
    hidden_bufs = (ha, hb)

    wf = wf_ref[...].astype(F32)
    taps = [jnp.broadcast_to(column(wf[k : k + 1], 32), (32, 32)) for k in range(3)]
    lane = iota((32, 32), 1)
    for p in range(4):
        for u in range(6):
            block = jnp.zeros((32, 32), F32)
            for k in range(3):
                block = jnp.where(lane == 4 * u + p + k + 3, taps[k], block)
            w1[192 * p + 32 * u : 192 * p + 32 * (u + 1), :] = block.astype(BF16)
    wide = jnp.dot(
        ws_ref[...], picks((32, 256), iota((32, 256), 0), iota((32, 256), 1) % 32), preferred_element_type=F32
    ).astype(BF16)
    row = iota((192, 32), 0)
    channel = picks((192, 32), row % 64 // 8 * 4 + row % 4, iota((192, 32), 1))
    row = iota((192, 256), 0)
    apart = iota((192, 256), 1) // 32 - 2 * (row // 64) - row % 8 // 4
    total = jnp.zeros((192, 256), F32)
    for k in range(3):
        part = jnp.dot(channel, wide[32 * k : 32 * (k + 1)], preferred_element_type=F32)
        total = jnp.where(apart == k, part, total)
    w2[...] = total.astype(BF16)
    row = iota((64, 32), 0)
    of_row = jnp.where(row // 8 * 4 + row % 4 == iota((64, 32), 1), wn_ref[...].astype(F32), 0.0)
    wn[...] = jnp.broadcast_to(jnp.sum(of_row, axis=1, keepdims=True), wn.shape)

    xt[0:PAD, :] = jnp.zeros((PAD, traces), F32)
    xt[PAD + samples : rows, :] = jnp.zeros((rows - PAD - samples, traces), F32)
    for k in range(samples // 128):
        xt[PAD + 128 * k : PAD + 128 * (k + 1), :] = x_ref[:, 128 * k : 128 * (k + 1)].astype(F32).T

    def relu(value):
        return jnp.maximum(value.astype(BF16), jnp.zeros((), BF16))

    def hidden(j, h_ref, before):
        xs = xt[PAD + WIN * j : PAD + WIN * j + 32, :].astype(BF16)
        for p in range(4):
            h_ref[p, 0:64, :] = before[p, 192:256, :]
            h_ref[p, 64:256, :] = relu(
                jnp.dot(w1[192 * p : 192 * (p + 1), :], xs, preferred_element_type=F32)
            )

    sub = iota((3, 8, traces), 1)
    even = (sub & 1) == 0
    low = (sub & 2) == 0

    def pair(a, b, shift, mask):
        return jnp.where(mask, a + pltpu.roll(a, 8 - shift, 1), b + pltpu.roll(b, shift, 1))

    def second(j, h_ref):
        parts = []
        for p in range(4):
            o = jnp.dot(w2[...], h_ref[p], preferred_element_type=F32)
            o = jnp.maximum(o, 0.0).reshape(3, 64, traces) * wn[...][None]
            parts.append(jnp.sum(o.reshape(3, 8, 8, traces), axis=1))
        noise = pair(pair(parts[0], parts[1], 1, even), pair(parts[2], parts[3], 1, even), 2, low)
        x = xt[PAD + WIN * j : PAD + WIN * (j + 1), :]
        dt[WIN * j : WIN * (j + 1), :] = x - noise.reshape(WIN, traces)

    xs = xt[PAD - WIN : PAD - WIN + 32, :].astype(BF16)
    for p in range(4):
        hb[p, 192:224, :] = jnp.zeros((32, traces), BF16)
        hb[p, 224:256, :] = relu(
            jnp.dot(w1[192 * p + 160 : 192 * (p + 1), :], xs, preferred_element_type=F32)
        )
    hidden(0, ha, hb)
    for j in range(windows):
        this, other = hidden_bufs[j % 2], hidden_bufs[1 - j % 2]
        if j + 1 < windows:
            hidden(j + 1, other, this)
        else:
            inside = 32 * ((samples - WIN * j + 4) // 4)
            for p in range(4):
                this[p, inside:, :] = jnp.zeros((256 - inside, traces), BF16)
        second(j, this)

    own = own_ref[...]
    own_col = column(own.astype(F32), traces).astype(jnp.int32)
    earlier = (own_col == own) & (iota((traces, traces), 0) < iota((traces, traces), 1))
    rank = jnp.sum(jnp.where(earlier, 1.0, 0.0), axis=0, keepdims=True).astype(jnp.int32)
    placing = picks((slots, traces), iota((slots, traces), 0), own * 8 + rank)
    nt = (((1,), (1,)), ((), ()))
    for k in range(samples // 256):
        block = dt[256 * k : 256 * (k + 1), :].astype(BF16)
        out_ref[:, 256 * k : 256 * (k + 1)] = lax.dot_general(
            placing, block, nt, preferred_element_type=F32
        ).astype(BF16)
    which = iota((TAIL, traces), 0)
    row, col = bins_ref[...] // 18 + 1, bins_ref[...] % 18 + 1
    tail = jnp.where(which == 0, row, jnp.where(which == 1, col, 0)).astype(F32).astype(BF16)
    out_ref[:, samples:] = lax.dot_general(placing, tail, nt, preferred_element_type=F32).astype(BF16)


def prepare_kernel(fold_ref, wv_ref, fold_out, w_out):
    bins = fold_out.shape[0]
    row = iota((bins, 16), 0)
    of_x = jnp.dot(
        picks((bins, 16), row // QP - 1, iota((bins, 16), 1)),
        fold_ref[...].astype(F32).astype(BF16),
        preferred_element_type=F32,
    )
    own = jnp.sum(jnp.where(row % QP - 1 == iota((bins, 16), 1), of_x, 0.0), axis=1, keepdims=True)
    fold_out[...] = jnp.broadcast_to(own, fold_out.shape)
    cols = w_out.shape[1]
    by_row = jnp.dot(
        picks((256, 16), iota((256, 16), 0) // 16, iota((256, 16), 1)), wv_ref[...], preferred_element_type=F32
    ).astype(BF16)
    col = iota((27, cols), 1)
    tap = col // (3 * QP) * 9 + col // QP % 3
    apart = iota((256, cols), 1) % QP - iota((256, cols), 0) % 16
    total = jnp.zeros((256, cols), F32)
    for k in range(3):
        part = jnp.dot(by_row, picks((27, cols), tap + 3 * k, iota((27, cols), 0)), preferred_element_type=F32)
        total = jnp.where(apart == k, part, total)
    w_out[...] = jnp.where(iota((256, cols), 1) < 9 * QP, total, 0.0).astype(BF16)


def stack_kernel(recv_ref, fold_ref, main_ref, up_ref, down_ref, cols_ref):
    slots = recv_ref.shape[0]
    blocks, bins, _ = main_ref.shape
    samples = recv_ref.shape[1] - TAIL
    tail = recv_ref[:, samples:].astype(F32).T
    place = ((tail[0:1] - 1.0) * QP + (tail[1:2] - 1.0)).astype(jnp.int32)
    select = jnp.where(iota((bins, slots), 0) == place, 1.0, 0.0).astype(BF16)
    for c in range(0, blocks - 1, 2):
        both = jnp.dot(select, recv_ref[:, 128 * c : 128 * (c + 2)], preferred_element_type=F32)
        main_ref[c] = both[:, :128]
        main_ref[c + 1] = both[:, 128:]
    main_ref[blocks - 1] = fold_ref[...]
    for c in range(blocks):
        lanes = slice(128 * c, 128 * (c + 1))
        up_ref[:, lanes] = main_ref[c, 0 : 2 * QP, :].astype(BF16)
        down_ref[:, lanes] = main_ref[c, bins - 2 * QP : bins, :].astype(BF16)
        for k, q in enumerate((0, 1, 16, 17)):
            cols_ref[c, 24 * k : 24 * k + 18, :] = main_ref[c, pl.ds(q, 18, stride=QP), :]
            cols_ref[c, 24 * k + 18 : 24 * k + 24, :] = jnp.zeros((6, 128), F32)


def columns_kernel(cols_ref, above_ref, below_ref, left_ref, right_ref, acc):
    blocks = cols_ref.shape[0]
    for c in range(blocks):
        acc[:, 128 * c : 128 * (c + 1)] = cols_ref[c]
    above = above_ref[...].astype(F32)
    below = below_ref[...].astype(F32)
    for k, q in enumerate((0, 1, 16, 17)):
        for r in range(2):
            acc[24 * k + r : 24 * k + r + 1, :] += above[r * QP + q : r * QP + q + 1, :]
            acc[24 * k + 16 + r : 24 * k + 17 + r, :] += below[r * QP + q : r * QP + q + 1, :]
    left_ref[...] = acc[0:48, :].astype(BF16)
    right_ref[...] = acc[48:96, :].astype(BF16)


def volume_kernel(main_ref, above_ref, below_ref, left_ref, right_ref, w_ref, out_ref, acc, vs):
    blocks, bins, _ = acc.shape
    samples = 128 * (blocks - 1)
    planes = bins // QP

    @pl.when(pl.program_id(0) == 0)
    def _():
        acc[...] = main_ref[...]
        for c in range(blocks):
            lanes = slice(128 * c, 128 * (c + 1))
            acc[c, 0 : 2 * QP, :] += above_ref[:, lanes].astype(F32)
            acc[c, bins - 2 * QP : bins, :] += below_ref[:, lanes].astype(F32)
            for ref, first in ((left_ref, 0), (right_ref, 16)):
                strip = ref[:, lanes].astype(F32)
                for k in range(2):
                    acc[c, pl.ds(first + k, planes, stride=QP), :] += strip[24 * k : 24 * k + planes, :]
        vs[planes * 3 * QP :, :] = jnp.zeros((8, samples), F32)

    lane = iota((QP, samples), 1)

    def plane(r):
        rows = pl.ds(pl.multiple_of(r * QP, 8), QP)
        fold = acc[blocks - 1, rows, :]
        inside = fold > 0.0
        fold = jnp.where(inside, fold, 1.0)
        v = jnp.concatenate(
            [jnp.where(inside, acc[c, rows, :] / fold, 0.0) for c in range(blocks - 1)], axis=1
        )
        v = v.astype(BF16).astype(F32)
        before = jnp.where(lane == 0, 0.0, pltpu.roll(v, 1, 1))
        after = jnp.where(lane == samples - 1, 0.0, pltpu.roll(v, samples - 1, 1))
        base = r * 3 * QP
        vs[pl.ds(pl.multiple_of(base, 8), QP), :] = before
        vs[pl.ds(pl.multiple_of(base + QP, 8), QP), :] = v
        vs[pl.ds(pl.multiple_of(base + 2 * QP, 8), QP), :] = after

    count = out_ref.shape[0]
    at = pl.program_id(0) * count

    @pl.when(pl.program_id(0) == 0)
    def _():
        plane(0)
        plane(1)

    for k in range(count):
        plane(at + 2 + k)
    for k in range(count):
        base = pl.multiple_of((at + k) * 3 * QP, 8)
        taps = vs[pl.ds(base, 9 * QP + 8), :].astype(BF16)
        for c in range(0, samples, 256):
            out = jnp.dot(w_ref[...], taps[:, c : c + 256], preferred_element_type=F32)
            out_ref[k, :, :, c : c + 256] = out.astype(BF16).reshape(16, 16, 256)


def neighbours(first, last, axis):
    size = lax.axis_size(axis)
    up = [(i, i + 1) for i in range(size - 1)]
    down = [(j, i) for i, j in up]
    return lax.ppermute(last, axis, up), lax.ppermute(first, axis, down)


def body(traces, owner, bin_ids, fold, w_first, w_second, w_noise, w_volume):
    devices = lax.axis_size("inline") * lax.axis_size("xline")
    count, samples = traces.shape
    slots = devices * 8
    width = samples + TAIL
    vmem = pl.BlockSpec(memory_space=pltpu.VMEM)
    params = pltpu.CompilerParams(vmem_limit_bytes=24 << 20)
    rows = WIN * (-(-samples // WIN))
    outgoing = pl.pallas_call(
        denoise_kernel,
        out_shape=jax.ShapeDtypeStruct((slots, width), BF16),
        in_specs=[vmem] * 6,
        out_specs=vmem,
        scratch_shapes=[
            pltpu.VMEM((PAD + rows + 8, count), F32),
            pltpu.VMEM((rows, count), F32),
            pltpu.VMEM((4, 256, count), BF16),
            pltpu.VMEM((4, 256, count), BF16),
            pltpu.VMEM((768, 32), BF16),
            pltpu.VMEM((192, 256), BF16),
            pltpu.VMEM((64, count), F32),
        ],
        compiler_params=params,
        name="denoise",
    )(
        traces,
        owner.reshape(1, count),
        bin_ids.reshape(1, count),
        w_first.T,
        w_second.reshape(96, 32),
        w_noise.reshape(1, 32),
    )
    bins = 18 * QP
    folds, w_taps = pl.pallas_call(
        prepare_kernel,
        out_shape=[jax.ShapeDtypeStruct((bins, TAIL), F32), jax.ShapeDtypeStruct((256, 9 * QP + 8), BF16)],
        in_specs=[vmem] * 2,
        out_specs=[vmem] * 2,
        compiler_params=params,
        name="prepare",
    )(fold, w_volume)
    received = lax.all_to_all(
        outgoing.reshape(devices, 8, width), ("inline", "xline"), split_axis=0, concat_axis=0, tiled=True
    ).reshape(slots, width)
    main, up, down, cols = pl.pallas_call(
        stack_kernel,
        out_shape=[
            jax.ShapeDtypeStruct((width // 128, bins, 128), F32),
            jax.ShapeDtypeStruct((2 * QP, width), BF16),
            jax.ShapeDtypeStruct((2 * QP, width), BF16),
            jax.ShapeDtypeStruct((width // 128, 96, 128), F32),
        ],
        in_specs=[vmem] * 2,
        out_specs=[vmem] * 4,
        compiler_params=params,
        name="stack",
    )(received, folds)
    above, below = neighbours(up, down, "inline")
    left, right = pl.pallas_call(
        columns_kernel,
        out_shape=[jax.ShapeDtypeStruct((48, width), BF16)] * 2,
        in_specs=[vmem] * 3,
        out_specs=[vmem] * 2,
        scratch_shapes=[pltpu.VMEM((96, width), F32)],
        compiler_params=params,
        name="columns",
    )(cols, above, below)
    from_left, from_right = neighbours(left, right, "xline")
    whole = lambda *shape: pl.BlockSpec(shape, lambda x: (0,) * len(shape))
    return pl.pallas_call(
        volume_kernel,
        out_shape=jax.ShapeDtypeStruct((16, 16, 16, samples), BF16),
        grid=(8,),
        in_specs=[
            whole(width // 128, bins, 128),
            whole(2 * QP, width),
            whole(2 * QP, width),
            whole(48, width),
            whole(48, width),
            whole(256, 9 * QP + 8),
        ],
        out_specs=pl.BlockSpec((2, 16, 16, samples), lambda x: (x, 0, 0, 0)),
        scratch_shapes=[pltpu.VMEM((width // 128, bins, 128), F32), pltpu.VMEM((bins * 3 + 8, samples), F32)],
        compiler_params=params,
        name="volume",
    )(main, above, below, from_left, from_right, w_taps)


def solution(mesh):
    placed = (
        P(("inline", "xline"), None),
        P(("inline", "xline"), None),
        P(("inline", "xline")),
        P("inline", "xline"),
        P(),
        P(),
        P(),
        P(),
    )
    return jax.shard_map(
        body,
        mesh=mesh,
        in_specs=placed,
        out_specs=P("inline", None, "xline", None),
        check_vma=False,
    )
```

time: 135 us -> 86.5 us (0.64)
  Pallas kernels: 61.7 us -> 19.1 us
  local copies, waits for them, and re-layouts: 11.9 us -> 5.88 us
  waiting for transfers between devices: 37.6 us -> 40.3 us
  other arithmetic: 2.64 us -> 0 us
    pallas_call x1, Pallas kernels: 42.5 us -> 10.2 us  [body(): pl.pallas_call(denoise_kernel, out_shape=jax.ShapeDtypeStruct((slots, wid...]
    broadcast_in_dim x32 -> x0, local copies, waits for them, and re-layouts: 6.32 us -> none  [the longest x10 2.16 us: volume_weights(): out = jnp.where(delta == k, w[:, None, :, :, k][..., None], out)]
    pallas_call x1, Pallas kernels: 12.9 us -> 7.18 us  [body(): pl.pallas_call(volume_kernel, out_shape=jax.ShapeDtypeStruct((16, 16, 16,...]
    pallas_call x1, Pallas kernels: 4.33 us -> 1.16 us  [body(): pl.pallas_call(stack_kernel, out_shape=[jax.ShapeDtypeStruct((width // 12...]
    ppermute x4, waiting for transfers between devices: 5.49 us -> 8.32 us  [neighbours(): return (lax.ppermute(last, axis, up), lax.ppermute(first, axis, down))]
    select_n x3 -> x0, other arithmetic: 2.62 us -> none  [the longest x1 1.67 us: first_weights(): out = jnp.where(delta == k, w_first[:, k][None, None, :, None], out)]
    unnamed x16 -> x18, local copies, waits for them, and re-layouts: 3.37 us -> 5.88 us
    pallas_call x1, Pallas kernels: 1.85 us -> 0.09 us  [body(): pl.pallas_call(columns_kernel, out_shape=[jax.ShapeDtypeStruct((48, width...]
  transfers between devices with their start and end apart: 5 -> 5, of which waited for: 3 -> 4; matrix products, arithmetic and copies ran while one was open for 3% -> 0% of each run, Pallas kernels for 0% -> 0%
where the time goes in v2:
time: 86.5 us; the launch traced here: 86.1 us
  waiting for transfers between devices  40.3 us (47%)
  starting transfers between devices  20.7 us (24%)
  Pallas kernels  19.1 us (22%)
  local copies, waits for them, and re-layouts  5.88 us (7%)
    all_to_all x1, waiting for transfers between devices, body(): lax.all_to_all(outgoing.reshape(devices, 8, width), ('inline', 'xline'),...  32 us
    all_to_all x1, starting transfers between devices, body(): lax.all_to_all(outgoing.reshape(devices, 8, width), ('inline', 'xline'),...  11.5 us
    pallas_call x1, Pallas kernels, body(): pl.pallas_call(denoise_kernel, out_shape=jax.ShapeDtypeStruct((slots, wid...  10.2 us
    ppermute x4, starting transfers between devices, neighbours(): return (lax.ppermute(last, axis, up), lax.ppermute(first, axis, down))  9.18 us
    ppermute x4, waiting for transfers between devices, neighbours(): return (lax.ppermute(last, axis, up), lax.ppermute(first, axis, down))  8.32 us
    pallas_call x1, Pallas kernels, body(): pl.pallas_call(volume_kernel, out_shape=jax.ShapeDtypeStruct((16, 16, 16,...  7.18 us
    unnamed x18, local copies, waits for them, and re-layouts  5.88 us
  transfers between devices with their start and end apart: 5, of which 4 were waited for; matrix products, arithmetic and copies ran while one was open for 0% of the time, Pallas kernels for 0%

profile of v2, /device:TPU:1, one launch (start us, length us, event | category | flops | bytes accessed | tf_op | source)
XLA Modules:
  0.0 86.1 jit_solution(14559213886553663928)
XLA Ops:
  0.0 0.0 copy-start.1
  0.0 1.0 %copy-done.1 = bf16[256,1024]{1,0:T(8,128)(2,1)S(1)} copy-done((bf16[256,1024]{1,0:T(8,128)(2,1)S(1)}, bf16[256,1024]{1,0:T(8,128)(2,1)}, u32[]{:S(2)}) %copy-start.1) | copy-done | bytes 524312
  1.0 0.0 copy-start.2
  1.0 0.7 copy-done.2
  1.8 0.0 copy-start.5
  1.8 0.7 copy-done.5
  2.5 0.7 copy-done.6
  3.1 0.0 copy-start.7
  3.1 0.7 copy-done.7
  3.8 0.0 copy-start.8
  3.8 0.7 copy-done.8
  4.5 10.2 %denoise.1 = bf16[1024,1152]{1,0:T(8,128)(2,1)S(1)} custom-call(bf16[256,1024]{1,0:T(8,128)(2,1)S(1)} %copy-done.1, s32[1,256]{1,0:T(1,128)S(1)} %bitcast.10, s32[1,256]{1,0:T(1,128)S(1)} %bitcast.11, bf16[3,32]{1,0:T(4,128)(2,1)S(1)} %bitcast.12, bf16[96,32]{1,0:T(8,128)(2,1)S(1)} %bitcast.9, bf16[1,32]{1,0:T(2,128)(2,1)S(1)} %bitcast.13), custom_call_target="tpu_custom_call" | custom-call | tf_op jit(solution)/shard_map/denoise/pallas_call | solution.py:256
  14.7 0.0 copy-start
  14.7 1.4 %copy-done = bf16[1024,1152]{1,0:T(8,128)(2,1)} copy-done((bf16[1024,1152]{1,0:T(8,128)(2,1)}, bf16[1024,1152]{1,0:T(8,128)(2,1)S(1)}, u32[]{:S(2)}) %copy-start) | copy-done | bytes 2359320
  16.1 0.0 copy-start.3
  16.1 0.0 copy-start.4
  16.1 11.5 %all-to-all-start = ((bf16[128,8,1152]{2,1,0:T(8,128)(2,1)}), bf16[128,8,1152]{2,1,0:T(8,128)(2,1)S(1)}, u32[]{:S(2)}, u32[]{:S(2)}) async-start(bf16[128,8,1152]{2,1,0:T(8,128)(2,1)} %bitcast.8), calls=%async_computation | async-start | bytes 4718592 | tf_op jit(solution)/shard_map/all_to_all | solution.py:289
  27.6 0.0 copy-done.3
  27.6 0.0 copy-done.4
  27.6 0.4 prepare.1
  28.1 32.0 %all-to-all-done = bf16[128,8,1152]{2,1,0:T(8,128)(2,1)S(1)} async-done(((bf16[128,8,1152]{2,1,0:T(8,128)(2,1)}), bf16[128,8,1152]{2,1,0:T(8,128)(2,1)S(1)}, u32[]{:S(2)}, u32[]{:S(2)}) %all-to-all-start) | async-done | bytes 2359328 | tf_op jit(solution)/shard_map/all_to_all | solution.py:289
  60.1 1.2 %stack.1 = (f32[9,432,128]{2,1,0:T(8,128)S(1)}, bf16[48,1152]{1,0:T(8,128)(2,1)S(1)}, bf16[48,1152]{1,0:T(8,128)(2,1)S(1)}, f32[9,96,128]{2,1,0:T(8,128)S(1)}) custom-call(bf16[1024,1152]{1,0:T(8,128)(2,1)S(1)} %bitcast.7, f32[432,128]{1,0:T(8,128)S(1)} %get-tuple-element.13.fold_ref), custom_call_target="tpu_custom_call" | custom-call | tf_op jit(solution)/shard_map/stack/pallas_call | solution.py:292
  61.2 3.1 %collective-permute-start = (bf16[48,1152]{1,0:T(8,128)(2,1)S(1)}, bf16[48,1152]{1,0:T(8,128)(2,1)S(1)}, u32[]{:S(2)}, u32[]{:S(2)}) collective-permute-start(bf16[48,1152]{1,0:T(8,128)(2,1)S(1)} %get-tuple-element.15), channel_id=1, source_target_pairs={{0,16},{16,32},{32,48},{48,64},{64,80},{80,96},{96,112},{1,17},{17... | collective-permute-start | bytes 331784 | tf_op jit(solution)/shard_map/ppermute | solution.py:245
  64.3 1.9 %collective-permute-start.1 = (bf16[48,1152]{1,0:T(8,128)(2,1)S(1)}, bf16[48,1152]{1,0:T(8,128)(2,1)S(1)}, u32[]{:S(2)}, u32[]{:S(2)}) collective-permute-start(bf16[48,1152]{1,0:T(8,128)(2,1)S(1)} %get-tuple-element.16), channel_id=1, source_target_pairs={{16,0},{32,16},{48,32},{64,48},{80,64},{96,80},{112,96},{17,1},{33... | collective-permute-start | bytes 331784 | tf_op jit(solution)/shard_map/ppermute | solution.py:245
  66.3 0.0 collective-permute-done.above_ref
  66.3 4.1 %collective-permute-done.1.below_ref = bf16[48,1152]{1,0:T(8,128)(2,1)S(1)} collective-permute-done((bf16[48,1152]{1,0:T(8,128)(2,1)S(1)}, bf16[48,1152]{1,0:T(8,128)(2,1)S(1)}, u32[]{:S(2)}, u32[]{:S(2)}) %collective-permute-start.1) | collective-permute-done | bytes 110624 | tf_op jit(solution)/shard_map/ppermute | solution.py:245
  70.4 0.1 columns.1
  70.5 2.9 %collective-permute-start.2 = (bf16[48,1152]{1,0:T(8,128)(2,1)S(1)}, bf16[48,1152]{1,0:T(8,128)(2,1)S(1)}, u32[]{:S(2)}, u32[]{:S(2)}) collective-permute-start(bf16[48,1152]{1,0:T(8,128)(2,1)S(1)} %get-tuple-element.18), channel_id=1, source_target_pairs={{0,1},{1,2},{2,3},{3,4},{4,5},{5,6},{6,7},{7,8},{8,9},{9,10},{10,1... | collective-permute-start | bytes 331784 | tf_op jit(solution)/shard_map/ppermute | solution.py:245
  73.4 1.3 %collective-permute-start.3 = (bf16[48,1152]{1,0:T(8,128)(2,1)S(1)}, bf16[48,1152]{1,0:T(8,128)(2,1)S(1)}, u32[]{:S(2)}, u32[]{:S(2)}) collective-permute-start(bf16[48,1152]{1,0:T(8,128)(2,1)S(1)} %get-tuple-element.19), channel_id=1, source_target_pairs={{1,0},{2,1},{3,2},{4,3},{5,4},{6,5},{7,6},{8,7},{9,8},{10,9},{11,1... | collective-permute-start | bytes 331784 | tf_op jit(solution)/shard_map/ppermute | solution.py:245
  74.7 0.4 collective-permute-done.2.left_ref
  75.1 3.8 %collective-permute-done.3.right_ref = bf16[48,1152]{1,0:T(8,128)(2,1)S(1)} collective-permute-done((bf16[48,1152]{1,0:T(8,128)(2,1)S(1)}, bf16[48,1152]{1,0:T(8,128)(2,1)S(1)}, u32[]{:S(2)}, u32[]{:S(2)}) %collective-permute-start.3) | collective-permute-done | bytes 110624 | tf_op jit(solution)/shard_map/ppermute | solution.py:245
  78.9 7.2 %volume.1 = bf16[16,16,16,1024]{3,2,1,0:T(8,128)(2,1)} custom-call(f32[9,432,128]{2,1,0:T(8,128)S(1)} %get-tuple-element.14.main_ref, bf16[48,1152]{1,0:T(8,128)(2,1)S(1)} %collective-permute-done.above_ref, bf16[48,1152]{1,0:T(8,128)(2,1)S(1)} %collective-permute-done.1.below_ref, bf16[48,1152]{1,0:T(8,128)(2,1)S(1)} %collective-permute-done.2.left_ref, ...), custom_call_target="tpu_custom_call" | custom-call | tf_op jit(solution)/shard_map/volume/pallas_call | solution.py:317
  (1 shorter events, 0.0 us)
Async XLA Ops:
  0.0 1.0 %copy-start.1 = (bf16[256,1024]{1,0:T(8,128)(2,1)S(1)}, bf16[256,1024]{1,0:T(8,128)(2,1)}, u32[]{:S(2)}) copy-start(bf16[256,1024]{1,0:T(8,128)(2,1)} %x_ref.1) | copy-start | bytes 1572868
  1.0 0.7 copy-start.2
  1.8 0.7 copy-start.5
  2.5 0.7 copy-start.6
  3.1 0.7 copy-start.7
  3.8 0.7 copy-start.8
  14.7 1.4 %copy-start = (bf16[1024,1152]{1,0:T(8,128)(2,1)}, bf16[1024,1152]{1,0:T(8,128)(2,1)S(1)}, u32[]{:S(2)}) copy-start(bf16[1024,1152]{1,0:T(8,128)(2,1)S(1)} %denoise.1) | copy-start | bytes 7077892
  16.1 11.5 %copy-start.3 = (s32[16,16]{1,0:T(8,128)S(1)}, s32[16,16]{1,0:T(8,128)}, u32[]{:S(2)}) copy-start(s32[16,16]{1,0:T(8,128)} %fold_ref.1) | copy-start | bytes 3076
  16.1 11.5 %copy-start.4 = (bf16[16,27]{1,0:T(8,128)(2,1)S(1)}, bf16[16,27]{1,0:T(8,128)(2,1)}, u32[]{:S(2)}) copy-start(bf16[16,27]{1,0:T(8,128)(2,1)} %wv_ref.1) | copy-start | bytes 2596
  16.1 44.0 %all-to-all-start = ((bf16[128,8,1152]{2,1,0:T(8,128)(2,1)}), bf16[128,8,1152]{2,1,0:T(8,128)(2,1)S(1)}, u32[]{:S(2)}, u32[]{:S(2)}) async-start(bf16[128,8,1152]{2,1,0:T(8,128)(2,1)} %bitcast.8), calls=%async_computation | async-start | bytes 4718592 | tf_op jit(solution)/shard_map/all_to_all | solution.py:289
  61.2 5.0 %collective-permute-start = (bf16[48,1152]{1,0:T(8,128)(2,1)S(1)}, bf16[48,1152]{1,0:T(8,128)(2,1)S(1)}, u32[]{:S(2)}, u32[]{:S(2)}) collective-permute-start(bf16[48,1152]{1,0:T(8,128)(2,1)S(1)} %get-tuple-element.15), channel_id=1, source_target_pairs={{0,16},{16,32},{32,48},{48,64},{64,80},{80,96},{96,112},{1,17},{17... | collective-permute-start | bytes 331784 | tf_op jit(solution)/shard_map/ppermute | solution.py:245
  64.3 6.1 %collective-permute-start.1 = (bf16[48,1152]{1,0:T(8,128)(2,1)S(1)}, bf16[48,1152]{1,0:T(8,128)(2,1)S(1)}, u32[]{:S(2)}, u32[]{:S(2)}) collective-permute-start(bf16[48,1152]{1,0:T(8,128)(2,1)S(1)} %get-tuple-element.16), channel_id=1, source_target_pairs={{16,0},{32,16},{48,32},{64,48},{80,64},{96,80},{112,96},{17,1},{33... | collective-permute-start | bytes 331784 | tf_op jit(solution)/shard_map/ppermute | solution.py:245
  70.5 4.6 %collective-permute-start.2 = (bf16[48,1152]{1,0:T(8,128)(2,1)S(1)}, bf16[48,1152]{1,0:T(8,128)(2,1)S(1)}, u32[]{:S(2)}, u32[]{:S(2)}) collective-permute-start(bf16[48,1152]{1,0:T(8,128)(2,1)S(1)} %get-tuple-element.18), channel_id=1, source_target_pairs={{0,1},{1,2},{2,3},{3,4},{4,5},{5,6},{6,7},{7,8},{8,9},{9,10},{10,1... | collective-permute-start | bytes 331784 | tf_op jit(solution)/shard_map/ppermute | solution.py:245
  73.4 5.5 %collective-permute-start.3 = (bf16[48,1152]{1,0:T(8,128)(2,1)S(1)}, bf16[48,1152]{1,0:T(8,128)(2,1)S(1)}, u32[]{:S(2)}, u32[]{:S(2)}) collective-permute-start(bf16[48,1152]{1,0:T(8,128)(2,1)S(1)} %get-tuple-element.19), channel_id=1, source_target_pairs={{1,0},{2,1},{3,2},{4,3},{5,4},{6,5},{7,6},{8,7},{9,8},{10,9},{11,1... | collective-permute-start | bytes 331784 | tf_op jit(solution)/shard_map/ppermute | solution.py:245

commit v3 on v2

v3 whole, which is shorter than its diff:
```python
import jax
import jax.numpy as jnp
from jax import lax
from jax.experimental import pallas as pl
from jax.experimental.pallas import tpu as pltpu
from jax.sharding import PartitionSpec as P

F32 = jnp.float32
BF16 = jnp.bfloat16
WIN = 24
PAD = 24
SIDE = 18
BINS = 328
EDGE = 2 * SIDE
STRIP = 40
TAIL = 128


def iota(shape, dim):
    return lax.broadcasted_iota(jnp.int32, shape, dim)


def picks(shape, row, col):
    return jnp.where(jnp.broadcast_to(row == col, shape), 1.0, 0.0).astype(BF16)


def column(vector, size):
    eye = iota((size, size), 0) == iota((size, size), 1)
    return jnp.sum(jnp.where(eye, vector, 0.0), axis=1, keepdims=True)


def denoise_kernel(*refs):
    ins, out_hbm, bufs = refs[:6], refs[6], refs[7:13]
    xt, dt, ha, hb, w1, w2, wn, out_ref, in_sems, out_sems = refs[13:]
    x_ref, own_ref, bins_ref, wf_ref, ws_ref, wn_ref = bufs
    loads = [pltpu.make_async_copy(src, dst, in_sems.at[k]) for k, (src, dst) in enumerate(zip(ins, bufs))]
    for load in loads:
        load.start()
    traces, samples = x_ref.shape
    slots = out_ref.shape[0]
    rows = xt.shape[0]
    windows = -(-samples // WIN)
    hidden_bufs = (ha, hb)

    for load in loads[1:]:
        load.wait()

    own = own_ref[...]
    own_col = column(own.astype(F32), traces).astype(jnp.int32)
    earlier = (own_col == own) & (iota((traces, traces), 0) < iota((traces, traces), 1))
    rank = jnp.sum(jnp.where(earlier, 1.0, 0.0), axis=0, keepdims=True).astype(jnp.int32)
    placing = picks((slots, traces), iota((slots, traces), 0), own * 8 + rank)
    stores = []

    def place(start, width, rows):
        out_ref[:, start : start + width] = lax.dot_general(
            placing, rows, (((1,), (1,)), ((), ())), preferred_element_type=F32
        ).astype(BF16)
        store = pltpu.make_async_copy(
            out_ref.at[:, pl.ds(start, width)], out_hbm.at[:, pl.ds(start, width)], out_sems.at[len(stores)]
        )
        store.start()
        stores.append(store)

    which = iota((TAIL, traces), 0)
    row, col = bins_ref[...] // 18 + 1, bins_ref[...] % 18 + 1
    tail = jnp.where(which == 0, row, jnp.where(which == 1, col, 0)).astype(F32).astype(BF16)
    place(samples, TAIL, tail)

    wf = wf_ref[...].astype(F32)
    taps = [jnp.broadcast_to(column(wf[k : k + 1], 32), (32, 32)) for k in range(3)]
    lane = iota((32, 32), 1)
    for p in range(4):
        for u in range(6):
            block = jnp.zeros((32, 32), F32)
            for k in range(3):
                block = jnp.where(lane == 4 * u + p + k + 3, taps[k], block)
            w1[192 * p + 32 * u : 192 * p + 32 * (u + 1), :] = block.astype(BF16)
    wide = jnp.dot(
        ws_ref[...], picks((32, 256), iota((32, 256), 0), iota((32, 256), 1) % 32), preferred_element_type=F32
    ).astype(BF16)
    row = iota((192, 32), 0)
    channel = picks((192, 32), row % 64 // 8 * 4 + row % 4, iota((192, 32), 1))
    row = iota((192, 256), 0)
    apart = iota((192, 256), 1) // 32 - 2 * (row // 64) - row % 8 // 4
    total = jnp.zeros((192, 256), F32)
    for k in range(3):
        part = jnp.dot(channel, wide[32 * k : 32 * (k + 1)], preferred_element_type=F32)
        total = jnp.where(apart == k, part, total)
    w2[...] = total.astype(BF16)
    row = iota((64, 32), 0)
    of_row = jnp.where(row // 8 * 4 + row % 4 == iota((64, 32), 1), wn_ref[...].astype(F32), 0.0)
    wn[...] = jnp.broadcast_to(jnp.sum(of_row, axis=1, keepdims=True), wn.shape)

    loads[0].wait()
    xt[0:PAD, :] = jnp.zeros((PAD, traces), F32)
    xt[PAD + samples : rows, :] = jnp.zeros((rows - PAD - samples, traces), F32)
    for k in range(samples // 128):
        xt[PAD + 128 * k : PAD + 128 * (k + 1), :] = x_ref[:, 128 * k : 128 * (k + 1)].astype(F32).T

    def relu(value):
        return jnp.maximum(value.astype(BF16), jnp.zeros((), BF16))

    def hidden(j, h_ref, before):
        xs = xt[PAD + WIN * j : PAD + WIN * j + 32, :].astype(BF16)
        for p in range(4):
            h_ref[p, 0:64, :] = before[p, 192:256, :]
            h_ref[p, 64:256, :] = relu(
                jnp.dot(w1[192 * p : 192 * (p + 1), :], xs, preferred_element_type=F32)
            )

    sub = iota((3, 8, traces), 1)
    even = (sub & 1) == 0
    low = (sub & 2) == 0

    def pair(a, b, shift, mask):
        return jnp.where(mask, a + pltpu.roll(a, 8 - shift, 1), b + pltpu.roll(b, shift, 1))

    def second(j, h_ref):
        parts = []
        for p in range(4):
            o = jnp.dot(w2[...], h_ref[p], preferred_element_type=F32)
            o = jnp.maximum(o, 0.0).reshape(3, 64, traces) * wn[...][None]
            parts.append(jnp.sum(o.reshape(3, 8, 8, traces), axis=1))
        noise = pair(pair(parts[0], parts[1], 1, even), pair(parts[2], parts[3], 1, even), 2, low)
        x = xt[PAD + WIN * j : PAD + WIN * (j + 1), :]
        dt[WIN * j : WIN * (j + 1), :] = x - noise.reshape(WIN, traces)

    xs = xt[PAD - WIN : PAD - WIN + 32, :].astype(BF16)
    for p in range(4):
        hb[p, 192:224, :] = jnp.zeros((32, traces), BF16)
        hb[p, 224:256, :] = relu(
            jnp.dot(w1[192 * p + 160 : 192 * (p + 1), :], xs, preferred_element_type=F32)
        )
    hidden(0, ha, hb)
    for j in range(windows):
        this, other = hidden_bufs[j % 2], hidden_bufs[1 - j % 2]
        if j + 1 < windows:
            hidden(j + 1, other, this)
        else:
            inside = 32 * ((samples - WIN * j + 4) // 4)
            for p in range(4):
                this[p, inside:, :] = jnp.zeros((256 - inside, traces), BF16)
        second(j, this)
        while len(stores) - 1 < min(WIN * (j + 1), samples) // 256:
            start = 256 * (len(stores) - 1)
            place(start, 256, dt[start : start + 256, :].astype(BF16))
    for store in stores:
        store.wait()


def prepare_kernel(fold_ref, wv_ref, fold_out, w_out):
    bins = fold_out.shape[0]
    row = iota((bins, 16), 0)
    of_x = jnp.dot(
        picks((bins, 16), row // SIDE - 1, iota((bins, 16), 1)),
        fold_ref[...].astype(F32).astype(BF16),
        preferred_element_type=F32,
    )
    own = jnp.sum(jnp.where(row % SIDE - 1 == iota((bins, 16), 1), of_x, 0.0), axis=1, keepdims=True)
    fold_out[...] = jnp.broadcast_to(own, fold_out.shape)
    rows, cols = w_out.shape
    by_row = jnp.dot(
        picks((rows, 16), iota((rows, 16), 0) // 16 % 16, iota((rows, 16), 1)),
        wv_ref[...],
        preferred_element_type=F32,
    ).astype(BF16)
    row, col = iota((rows, cols), 0), iota((rows, cols), 1)
    dx = col // SIDE % 4 - row // 256
    dy = col % SIDE - row % 16
    near = (dx >= 0) & (dx < 3)
    dt = iota((27, cols), 1) // (4 * SIDE)
    total = jnp.zeros((rows, cols), F32)
    for k in range(9):
        taps = picks((27, cols), 3 * k + dt, iota((27, cols), 0))
        part = jnp.dot(by_row, taps, preferred_element_type=F32)
        total = jnp.where(near & (dx == k // 3) & (dy == k % 3), part, total)
    w_out[...] = total.astype(BF16)


def stack_kernel(recv_ref, fold_ref, main_ref, up_ref, down_ref, cols_ref):
    slots = recv_ref.shape[0]
    blocks, bins, _ = main_ref.shape
    samples = recv_ref.shape[1] - TAIL
    tail = recv_ref[:, samples:].astype(F32).T
    place = ((tail[0:1] - 1.0) * SIDE + (tail[1:2] - 1.0)).astype(jnp.int32)
    select = picks((bins, slots), iota((bins, slots), 0), place)
    for c in range(0, blocks - 1, 2):
        both = jnp.dot(select, recv_ref[:, 128 * c : 128 * (c + 2)], preferred_element_type=F32)
        main_ref[c] = both[:, :128]
        main_ref[c + 1] = both[:, 128:]
    main_ref[blocks - 1] = fold_ref[...]
    edge = iota((STRIP, 128), 0) < EDGE
    for c in range(blocks):
        lanes = slice(128 * c, 128 * (c + 1))
        up_ref[:, lanes] = jnp.where(edge, main_ref[c, 0:STRIP, :], 0.0).astype(BF16)
        down_ref[:, lanes] = main_ref[c, bins - STRIP : bins, :].astype(BF16)
        for k, q in enumerate((0, 1, 16, 17)):
            cols_ref[c, 24 * k : 24 * k + SIDE, :] = main_ref[c, pl.ds(q, SIDE, stride=SIDE), :]
            cols_ref[c, 24 * k + SIDE : 24 * (k + 1), :] = jnp.zeros((24 - SIDE, 128), F32)


def columns_kernel(cols_ref, above_ref, below_ref, left_ref, right_ref, acc):
    blocks = cols_ref.shape[0]
    for c in range(blocks):
        acc[:, 128 * c : 128 * (c + 1)] = cols_ref[c]
    above = above_ref[...].astype(F32)
    below = below_ref[...].astype(F32)
    for k, q in enumerate((0, 1, 16, 17)):
        for r in range(2):
            at = r * SIDE + q
            acc[24 * k + r : 24 * k + r + 1, :] += above[at : at + 1, :]
            acc[24 * k + 16 + r : 24 * k + 17 + r, :] += below[at : at + 1, :]
    left_ref[...] = acc[0:48, :].astype(BF16)
    right_ref[...] = acc[48:96, :].astype(BF16)


def volume_kernel(main_ref, above_ref, below_ref, left_ref, right_ref, w_ref, out_hbm, acc, vs, out, sems):
    blocks, bins, _ = acc.shape
    samples = 128 * (blocks - 1)
    acc[...] = main_ref[...]
    for c in range(blocks):
        lanes = slice(128 * c, 128 * (c + 1))
        acc[c, 0:STRIP, :] += above_ref[:, lanes].astype(F32)
        acc[c, bins - STRIP : bins, :] += below_ref[:, lanes].astype(F32)
        for ref, first in ((left_ref, 0), (right_ref, 16)):
            strip = ref[:, lanes].astype(F32)
            for k in range(2):
                acc[c, pl.ds(first + k, SIDE, stride=SIDE), :] += strip[24 * k : 24 * k + SIDE, :]

    def taps_of(start, stop):
        lane = iota((stop - start, samples), 1)
        fold = acc[blocks - 1, start:stop, :]
        inside = fold > 0.0
        fold = jnp.where(inside, fold, 1.0)
        v = jnp.concatenate(
            [jnp.where(inside, acc[c, start:stop, :] / fold, 0.0) for c in range(blocks - 1)], axis=1
        )
        v = v.astype(BF16).astype(F32)
        vs[0, start:stop, :] = jnp.where(lane == 0, 0.0, pltpu.roll(v, 1, 1))
        vs[1, start:stop, :] = v
        vs[2, start:stop, :] = jnp.where(lane == samples - 1, 0.0, pltpu.roll(v, samples - 1, 1))

    done, slots = 0, out.shape[0]
    stores = []
    for m in range(8):
        first, last = EDGE * m, EDGE * m + 2 * EDGE
        needed = min(bins, -(-last // 8) * 8)
        taps_of(done, needed)
        done = needed
        taps = jnp.concatenate([vs[dt, first:last, :] for dt in range(3)], axis=0).astype(BF16)
        if m >= slots:
            stores[m - slots].wait()
        for c in range(0, samples, 256):
            part = jnp.dot(w_ref[...], taps[:, c : c + 256], preferred_element_type=F32)
            out[m % slots, :, :, :, c : c + 256] = part.astype(BF16).reshape(2, 16, 16, 256)
        store = pltpu.make_async_copy(
            out.at[m % slots], out_hbm.at[pl.ds(2 * m, 2)], sems.at[m % slots]
        )
        store.start()
        stores.append(store)
    for store in stores[8 - slots :]:
        store.wait()


def neighbours(first, last, axis):
    size = lax.axis_size(axis)
    up = [(i, i + 1) for i in range(size - 1)]
    down = [(j, i) for i, j in up]
    return lax.ppermute(last, axis, up), lax.ppermute(first, axis, down)


def body(traces, owner, bin_ids, fold, w_first, w_second, w_noise, w_volume):
    devices = lax.axis_size("inline") * lax.axis_size("xline")
    count, samples = traces.shape
    slots = devices * 8
    width = samples + TAIL
    vmem = pl.BlockSpec(memory_space=pltpu.VMEM)
    hbm = pl.BlockSpec(memory_space=pltpu.HBM)
    params = pltpu.CompilerParams(vmem_limit_bytes=24 << 20)
    rows = WIN * (-(-samples // WIN))
    outgoing = pl.pallas_call(
        denoise_kernel,
        out_shape=jax.ShapeDtypeStruct((slots, width), BF16),
        in_specs=[hbm] * 6,
        out_specs=hbm,
        scratch_shapes=[
            pltpu.VMEM((count, samples), BF16),
            pltpu.VMEM((1, count), jnp.int32),
            pltpu.VMEM((1, count), jnp.int32),
            pltpu.VMEM((3, 32), BF16),
            pltpu.VMEM((96, 32), BF16),
            pltpu.VMEM((1, 32), BF16),
            pltpu.VMEM((PAD + rows + 8, count), F32),
            pltpu.VMEM((rows, count), F32),
            pltpu.VMEM((4, 256, count), BF16),
            pltpu.VMEM((4, 256, count), BF16),
            pltpu.VMEM((768, 32), BF16),
            pltpu.VMEM((192, 256), BF16),
            pltpu.VMEM((64, count), F32),
            pltpu.VMEM((slots, width), BF16),
            pltpu.SemaphoreType.DMA((6,)),
            pltpu.SemaphoreType.DMA((samples // 256 + 1,)),
        ],
        compiler_params=pltpu.CompilerParams(vmem_limit_bytes=60 << 20),
        name="denoise",
    )(
        traces,
        owner.reshape(1, count),
        bin_ids.reshape(1, count),
        w_first.T,
        w_second.reshape(96, 32),
        w_noise.reshape(1, 32),
    )
    bins = BINS
    folds, w_taps = pl.pallas_call(
        prepare_kernel,
        out_shape=[jax.ShapeDtypeStruct((bins, TAIL), F32), jax.ShapeDtypeStruct((512, 12 * SIDE), BF16)],
        in_specs=[vmem] * 2,
        out_specs=[vmem] * 2,
        compiler_params=params,
        name="prepare",
    )(fold, w_volume)
    received = lax.all_to_all(
        outgoing.reshape(devices, 8, width), ("inline", "xline"), split_axis=0, concat_axis=0, tiled=True
    ).reshape(slots, width)
    main, up, down, cols = pl.pallas_call(
        stack_kernel,
        out_shape=[
            jax.ShapeDtypeStruct((width // 128, bins, 128), F32),
            jax.ShapeDtypeStruct((STRIP, width), BF16),
            jax.ShapeDtypeStruct((STRIP, width), BF16),
            jax.ShapeDtypeStruct((width // 128, 96, 128), F32),
        ],
        in_specs=[vmem] * 2,
        out_specs=[vmem] * 4,
        compiler_params=params,
        name="stack",
    )(received, folds)
    above, below = neighbours(up, down, "inline")
    left, right = pl.pallas_call(
        columns_kernel,
        out_shape=[jax.ShapeDtypeStruct((48, width), BF16)] * 2,
        in_specs=[vmem] * 3,
        out_specs=[vmem] * 2,
        scratch_shapes=[pltpu.VMEM((96, width), F32)],
        compiler_params=params,
        name="columns",
    )(cols, above, below)
    from_left, from_right = neighbours(left, right, "xline")
    return pl.pallas_call(
        volume_kernel,
        out_shape=jax.ShapeDtypeStruct((16, 16, 16, samples), BF16),
        in_specs=[vmem] * 6,
        out_specs=hbm,
        scratch_shapes=[
            pltpu.VMEM((width // 128, bins, 128), F32),
            pltpu.VMEM((3, bins, samples), F32),
            pltpu.VMEM((3, 2, 16, 16, samples), BF16),
            pltpu.SemaphoreType.DMA((3,)),
        ],
        compiler_params=params,
        name="volume",
    )(main, above, below, from_left, from_right, w_taps)


def solution(mesh):
    placed = (
        P(("inline", "xline"), None),
        P(("inline", "xline"), None),
        P(("inline", "xline")),
        P("inline", "xline"),
        P(),
        P(),
        P(),
        P(),
    )
    return jax.shard_map(
        body,
        mesh=mesh,
        in_specs=placed,
        out_specs=P("inline", None, "xline", None),
        check_vma=False,
    )
```

time: 86.5 us -> 80.7 us (0.933)
  local copies, waits for them, and re-layouts: 5.88 us -> 0.01 us
  Pallas kernels: 19.1 us -> 20.3 us
  waiting for transfers between devices: 40.3 us -> 39.1 us
    unnamed x18 -> x4, local copies, waits for them, and re-layouts: 5.88 us -> 0.01 us
    pallas_call x1, Pallas kernels: 10.2 us -> 12.8 us  [body(): pl.pallas_call(denoise_kernel, out_shape=jax.ShapeDtypeStruct((slots, wid...]
    pallas_call x1, Pallas kernels: 7.18 us -> 4.98 us  [body(): pl.pallas_call(volume_kernel, out_shape=jax.ShapeDtypeStruct((16, 16, 16,...]
    pallas_call x1, Pallas kernels: 0.42 us -> 1.39 us  [body(): pl.pallas_call(prepare_kernel, out_shape=[jax.ShapeDtypeStruct((bins, TAI...]
    all_to_all x1, waiting for transfers between devices: 32 us -> 31 us  [body(): lax.all_to_all(outgoing.reshape(devices, 8, width), ('inline', 'xline'),...]
  transfers between devices with their start and end apart: 5 -> 5, of which waited for: 4 -> 4; matrix products, arithmetic and copies ran while one was open for 0% -> 0% of each run, Pallas kernels for 0% -> 2%
where the time goes in v3:
time: 80.7 us; the launch traced here: 80.4 us
  waiting for transfers between devices  39.1 us (48%)
  starting transfers between devices  20.7 us (26%)
  Pallas kernels  20.3 us (25%)
    all_to_all x1, waiting for transfers between devices, body(): lax.all_to_all(outgoing.reshape(devices, 8, width), ('inline', 'xline'),...  31 us
    pallas_call x1, Pallas kernels, body(): pl.pallas_call(denoise_kernel, out_shape=jax.ShapeDtypeStruct((slots, wid...  12.8 us
    all_to_all x1, starting transfers between devices, body(): lax.all_to_all(outgoing.reshape(devices, 8, width), ('inline', 'xline'),...  11.5 us
    ppermute x4, starting transfers between devices, neighbours(): return (lax.ppermute(last, axis, up), lax.ppermute(first, axis, down))  9.17 us
    ppermute x4, waiting for transfers between devices, neighbours(): return (lax.ppermute(last, axis, up), lax.ppermute(first, axis, down))  8.13 us
    pallas_call x1, Pallas kernels, body(): pl.pallas_call(volume_kernel, out_shape=jax.ShapeDtypeStruct((16, 16, 16,...  4.98 us
  transfers between devices with their start and end apart: 5, of which 4 were waited for; matrix products, arithmetic and copies ran while one was open for 0% of the time, Pallas kernels for 2%

profile of v3, /device:TPU:1, one launch (start us, length us, event | category | flops | bytes accessed | tf_op | source)
XLA Modules:
  0.0 80.4 jit_solution(12907418817706868264)
XLA Ops:
  0.0 12.8 %denoise.1 = bf16[1024,1152]{1,0:T(8,128)(2,1)} custom-call(bf16[256,1024]{1,0:T(8,128)(2,1)} %refs_0_.1, s32[1,256]{1,0:T(1,128)} %bitcast.10, s32[1,256]{1,0:T(1,128)} %bitcast.11, bf16[3,32]{1,0:T(4,128)(2,1)} %bitcast.12, bf16[96,32]{1,0:T(8,128)(2,1)} %bitcast.9, bf16[1,32]{1,0:T(2,128)(2,1)} %bitcast.13), custom_call_target="tpu_custom_call" | custom-call | tf_op jit(solution)/shard_map/denoise/pallas_call | solution.py:282
  12.8 0.0 copy-start
  12.9 0.0 copy-start.1
  12.9 11.5 %all-to-all-start = ((bf16[128,8,1152]{2,1,0:T(8,128)(2,1)}), bf16[128,8,1152]{2,1,0:T(8,128)(2,1)S(1)}, u32[]{:S(2)}, u32[]{:S(2)}) async-start(bf16[128,8,1152]{2,1,0:T(8,128)(2,1)} %bitcast.8), calls=%async_computation | async-start | bytes 4718592 | tf_op jit(solution)/shard_map/all_to_all | solution.py:324
  24.4 0.0 copy-done
  24.4 0.0 copy-done.1
  24.4 1.4 %prepare.1 = (f32[328,128]{1,0:T(8,128)S(1)}, bf16[512,216]{1,0:T(8,128)(2,1)S(1)}) custom-call(s32[16,16]{1,0:T(8,128)S(1)} %copy-done, bf16[16,27]{1,0:T(8,128)(2,1)S(1)} %copy-done.1), custom_call_target="tpu_custom_call" | custom-call | tf_op jit(solution)/shard_map/prepare/pallas_call | solution.py:316
  25.8 31.0 %all-to-all-done = bf16[128,8,1152]{2,1,0:T(8,128)(2,1)S(1)} async-done(((bf16[128,8,1152]{2,1,0:T(8,128)(2,1)}), bf16[128,8,1152]{2,1,0:T(8,128)(2,1)S(1)}, u32[]{:S(2)}, u32[]{:S(2)}) %all-to-all-start) | async-done | bytes 2359328 | tf_op jit(solution)/shard_map/all_to_all | solution.py:324
  56.8 1.0 %stack.1 = (f32[9,328,128]{2,1,0:T(8,128)S(1)}, bf16[40,1152]{1,0:T(8,128)(2,1)S(1)}, bf16[40,1152]{1,0:T(8,128)(2,1)S(1)}, f32[9,96,128]{2,1,0:T(8,128)S(1)}) custom-call(bf16[1024,1152]{1,0:T(8,128)(2,1)S(1)} %bitcast.7, f32[328,128]{1,0:T(8,128)S(1)} %get-tuple-element.13.fold_ref), custom_call_target="tpu_custom_call" | custom-call | tf_op jit(solution)/shard_map/stack/pallas_call | solution.py:327
  57.8 3.1 %collective-permute-start = (bf16[40,1152]{1,0:T(8,128)(2,1)S(1)}, bf16[40,1152]{1,0:T(8,128)(2,1)S(1)}, u32[]{:S(2)}, u32[]{:S(2)}) collective-permute-start(bf16[40,1152]{1,0:T(8,128)(2,1)S(1)} %get-tuple-element.15), channel_id=1, source_target_pairs={{0,16},{16,32},{32,48},{48,64},{64,80},{80,96},{96,112},{1,17},{17... | collective-permute-start | bytes 276488 | tf_op jit(solution)/shard_map/ppermute | solution.py:270
  60.9 1.9 %collective-permute-start.1 = (bf16[40,1152]{1,0:T(8,128)(2,1)S(1)}, bf16[40,1152]{1,0:T(8,128)(2,1)S(1)}, u32[]{:S(2)}, u32[]{:S(2)}) collective-permute-start(bf16[40,1152]{1,0:T(8,128)(2,1)S(1)} %get-tuple-element.16), channel_id=1, source_target_pairs={{16,0},{32,16},{48,32},{64,48},{80,64},{96,80},{112,96},{17,1},{33... | collective-permute-start | bytes 276488 | tf_op jit(solution)/shard_map/ppermute | solution.py:270
  62.8 0.0 collective-permute-done.above_ref
  62.8 3.9 %collective-permute-done.1.below_ref = bf16[40,1152]{1,0:T(8,128)(2,1)S(1)} collective-permute-done((bf16[40,1152]{1,0:T(8,128)(2,1)S(1)}, bf16[40,1152]{1,0:T(8,128)(2,1)S(1)}, u32[]{:S(2)}, u32[]{:S(2)}) %collective-permute-start.1) | collective-permute-done | bytes 92192 | tf_op jit(solution)/shard_map/ppermute | solution.py:270
  66.8 0.1 columns.1
  66.9 2.9 %collective-permute-start.2 = (bf16[48,1152]{1,0:T(8,128)(2,1)S(1)}, bf16[48,1152]{1,0:T(8,128)(2,1)S(1)}, u32[]{:S(2)}, u32[]{:S(2)}) collective-permute-start(bf16[48,1152]{1,0:T(8,128)(2,1)S(1)} %get-tuple-element.18), channel_id=1, source_target_pairs={{0,1},{1,2},{2,3},{3,4},{4,5},{5,6},{6,7},{7,8},{8,9},{9,10},{10,1... | collective-permute-start | bytes 331784 | tf_op jit(solution)/shard_map/ppermute | solution.py:270
  69.7 1.3 %collective-permute-start.3 = (bf16[48,1152]{1,0:T(8,128)(2,1)S(1)}, bf16[48,1152]{1,0:T(8,128)(2,1)S(1)}, u32[]{:S(2)}, u32[]{:S(2)}) collective-permute-start(bf16[48,1152]{1,0:T(8,128)(2,1)S(1)} %get-tuple-element.19), channel_id=1, source_target_pairs={{1,0},{2,1},{3,2},{4,3},{5,4},{6,5},{7,6},{8,7},{9,8},{10,9},{11,1... | collective-permute-start | bytes 331784 | tf_op jit(solution)/shard_map/ppermute | solution.py:270
  71.0 0.4 collective-permute-done.2.left_ref
  71.5 3.8 %collective-permute-done.3.right_ref = bf16[48,1152]{1,0:T(8,128)(2,1)S(1)} collective-permute-done((bf16[48,1152]{1,0:T(8,128)(2,1)S(1)}, bf16[48,1152]{1,0:T(8,128)(2,1)S(1)}, u32[]{:S(2)}, u32[]{:S(2)}) %collective-permute-start.3) | collective-permute-done | bytes 110624 | tf_op jit(solution)/shard_map/ppermute | solution.py:270
  75.2 5.0 %volume.1 = bf16[16,16,16,1024]{3,2,1,0:T(8,128)(2,1)} custom-call(f32[9,328,128]{2,1,0:T(8,128)S(1)} %get-tuple-element.14.main_ref, bf16[40,1152]{1,0:T(8,128)(2,1)S(1)} %collective-permute-done.above_ref, bf16[40,1152]{1,0:T(8,128)(2,1)S(1)} %collective-permute-done.1.below_ref, bf16[48,1152]{1,0:T(8,128)(2,1)S(1)} %collective-permute-done.2.left_ref, ...), custom_call_target="tpu_custom_call" | custom-call | tf_op jit(solution)/shard_map/volume/pallas_call | solution.py:351
Async XLA Ops:
  12.8 11.5 %copy-start = (s32[16,16]{1,0:T(8,128)S(1)}, s32[16,16]{1,0:T(8,128)}, u32[]{:S(2)}) copy-start(s32[16,16]{1,0:T(8,128)} %fold_ref.1) | copy-start | bytes 3076
  12.9 11.5 %copy-start.1 = (bf16[16,27]{1,0:T(8,128)(2,1)S(1)}, bf16[16,27]{1,0:T(8,128)(2,1)}, u32[]{:S(2)}) copy-start(bf16[16,27]{1,0:T(8,128)(2,1)} %wv_ref.1) | copy-start | bytes 2596
  12.9 44.0 %all-to-all-start = ((bf16[128,8,1152]{2,1,0:T(8,128)(2,1)}), bf16[128,8,1152]{2,1,0:T(8,128)(2,1)S(1)}, u32[]{:S(2)}, u32[]{:S(2)}) async-start(bf16[128,8,1152]{2,1,0:T(8,128)(2,1)} %bitcast.8), calls=%async_computation | async-start | bytes 4718592 | tf_op jit(solution)/shard_map/all_to_all | solution.py:324
  57.8 5.0 %collective-permute-start = (bf16[40,1152]{1,0:T(8,128)(2,1)S(1)}, bf16[40,1152]{1,0:T(8,128)(2,1)S(1)}, u32[]{:S(2)}, u32[]{:S(2)}) collective-permute-start(bf16[40,1152]{1,0:T(8,128)(2,1)S(1)} %get-tuple-element.15), channel_id=1, source_target_pairs={{0,16},{16,32},{32,48},{48,64},{64,80},{80,96},{96,112},{1,17},{17... | collective-permute-start | bytes 276488 | tf_op jit(solution)/shard_map/ppermute | solution.py:270
  60.9 5.9 %collective-permute-start.1 = (bf16[40,1152]{1,0:T(8,128)(2,1)S(1)}, bf16[40,1152]{1,0:T(8,128)(2,1)S(1)}, u32[]{:S(2)}, u32[]{:S(2)}) collective-permute-start(bf16[40,1152]{1,0:T(8,128)(2,1)S(1)} %get-tuple-element.16), channel_id=1, source_target_pairs={{16,0},{32,16},{48,32},{64,48},{80,64},{96,80},{112,96},{17,1},{33... | collective-permute-start | bytes 276488 | tf_op jit(solution)/shard_map/ppermute | solution.py:270
  66.9 4.6 %collective-permute-start.2 = (bf16[48,1152]{1,0:T(8,128)(2,1)S(1)}, bf16[48,1152]{1,0:T(8,128)(2,1)S(1)}, u32[]{:S(2)}, u32[]{:S(2)}) collective-permute-start(bf16[48,1152]{1,0:T(8,128)(2,1)S(1)} %get-tuple-element.18), channel_id=1, source_target_pairs={{0,1},{1,2},{2,3},{3,4},{4,5},{5,6},{6,7},{7,8},{8,9},{9,10},{10,1... | collective-permute-start | bytes 331784 | tf_op jit(solution)/shard_map/ppermute | solution.py:270
  69.7 5.5 %collective-permute-start.3 = (bf16[48,1152]{1,0:T(8,128)(2,1)S(1)}, bf16[48,1152]{1,0:T(8,128)(2,1)S(1)}, u32[]{:S(2)}, u32[]{:S(2)}) collective-permute-start(bf16[48,1152]{1,0:T(8,128)(2,1)S(1)} %get-tuple-element.19), channel_id=1, source_target_pairs={{1,0},{2,1},{3,2},{4,3},{5,4},{6,5},{7,6},{8,7},{9,8},{10,9},{11,1... | collective-permute-start | bytes 331784 | tf_op jit(solution)/shard_map/ppermute | solution.py:270

commit v4 on v3

--- a/solution.py
+++ b/solution.py
@@ -178,7 +178,7 @@
     w_out[...] = total.astype(BF16)
 
 
-def stack_kernel(recv_ref, fold_ref, main_ref, up_ref, down_ref, cols_ref):
+def stack_kernel(recv_ref, fold_ref, main_ref, left_ref, right_ref):
     slots = recv_ref.shape[0]
     blocks, bins, _ = main_ref.shape
     samples = recv_ref.shape[1] - TAIL
@@ -190,76 +190,100 @@
         main_ref[c] = both[:, :128]
         main_ref[c + 1] = both[:, 128:]
     main_ref[blocks - 1] = fold_ref[...]
-    edge = iota((STRIP, 128), 0) < EDGE
+    pad = jnp.zeros((24 - SIDE, 128), F32)
     for c in range(blocks):
         lanes = slice(128 * c, 128 * (c + 1))
-        up_ref[:, lanes] = jnp.where(edge, main_ref[c, 0:STRIP, :], 0.0).astype(BF16)
-        down_ref[:, lanes] = main_ref[c, bins - STRIP : bins, :].astype(BF16)
-        for k, q in enumerate((0, 1, 16, 17)):
-            cols_ref[c, 24 * k : 24 * k + SIDE, :] = main_ref[c, pl.ds(q, SIDE, stride=SIDE), :]
-            cols_ref[c, 24 * k + SIDE : 24 * (k + 1), :] = jnp.zeros((24 - SIDE, 128), F32)
-
-
-def columns_kernel(cols_ref, above_ref, below_ref, left_ref, right_ref, acc):
-    blocks = cols_ref.shape[0]
-    for c in range(blocks):
-        acc[:, 128 * c : 128 * (c + 1)] = cols_ref[c]
-    above = above_ref[...].astype(F32)
-    below = below_ref[...].astype(F32)
-    for k, q in enumerate((0, 1, 16, 17)):
-        for r in range(2):
-            at = r * SIDE + q
-            acc[24 * k + r : 24 * k + r + 1, :] += above[at : at + 1, :]
-            acc[24 * k + 16 + r : 24 * k + 17 + r, :] += below[at : at + 1, :]
-    left_ref[...] = acc[0:48, :].astype(BF16)
-    right_ref[...] = acc[48:96, :].astype(BF16)
-
-
-def volume_kernel(main_ref, above_ref, below_ref, left_ref, right_ref, w_ref, out_hbm, acc, vs, out, sems):
-    blocks, bins, _ = acc.shape
-    samples = 128 * (blocks - 1)
-    acc[...] = main_ref[...]
+        for ref, first in ((left_ref, 0), (right_ref, 16)):
+            cols = [main_ref[c, pl.ds(first + k, SIDE, stride=SIDE), :] for k in range(2)]
+            ref[:, lanes] = jnp.concatenate([cols[0], pad, cols[1], pad], axis=0).astype(BF16)
+
+
+def edges_kernel(main_ref, left_ref, right_ref, up_ref, down_ref, up, down):
+    blocks, bins, _ = main_ref.shape
     for c in range(blocks):
         lanes = slice(128 * c, 128 * (c + 1))
-        acc[c, 0:STRIP, :] += above_ref[:, lanes].astype(F32)
-        acc[c, bins - STRIP : bins, :] += below_ref[:, lanes].astype(F32)
+        up[:, lanes] = main_ref[c, 0:STRIP, :]
+        down[:, lanes] = main_ref[c, bins - STRIP : bins, :]
+    for ref, first in ((left_ref, 0), (right_ref, 16)):
+        strip = ref[...].astype(F32)
+        for k in range(2):
+            for r in range(2):
+                at = r * SIDE + first + k
+                up[at : at + 1, :] += strip[24 * k + r : 24 * k + r + 1, :]
+                down[at : at + 1, :] += strip[24 * k + 16 + r : 24 * k + 17 + r, :]
+    up_ref[...] = jnp.where(iota(up.shape, 0) < EDGE, up[...], 0.0).astype(BF16)
+    down_ref[...] = down[...].astype(BF16)
+
+
+def add_sides(acc, left_ref, right_ref, start, count):
+    for c in range(acc.shape[0]):
+        lanes = slice(128 * c, 128 * (c + 1))
         for ref, first in ((left_ref, 0), (right_ref, 16)):
             strip = ref[:, lanes].astype(F32)
             for k in range(2):
-                acc[c, pl.ds(first + k, SIDE, stride=SIDE), :] += strip[24 * k : 24 * k + SIDE, :]
-
-    def taps_of(start, stop):
-        lane = iota((stop - start, samples), 1)
-        fold = acc[blocks - 1, start:stop, :]
-        inside = fold > 0.0
-        fold = jnp.where(inside, fold, 1.0)
-        v = jnp.concatenate(
-            [jnp.where(inside, acc[c, start:stop, :] / fold, 0.0) for c in range(blocks - 1)], axis=1
-        )
-        v = v.astype(BF16).astype(F32)
-        vs[0, start:stop, :] = jnp.where(lane == 0, 0.0, pltpu.roll(v, 1, 1))
-        vs[1, start:stop, :] = v
-        vs[2, start:stop, :] = jnp.where(lane == samples - 1, 0.0, pltpu.roll(v, samples - 1, 1))
-
-    done, slots = 0, out.shape[0]
+                rows = pl.ds(start * SIDE + first + k, count, stride=SIDE)
+                acc[c, rows, :] += strip[24 * k + start : 24 * k + start + count, :]
+
+
+def make_taps(acc, vs, start, stop):
+    blocks = acc.shape[0]
+    samples = 128 * (blocks - 1)
+    lane = iota((stop - start, samples), 1)
+    fold = acc[blocks - 1, start:stop, :]
+    inside = fold > 0.0
+    fold = jnp.where(inside, fold, 1.0)
+    v = jnp.concatenate([jnp.where(inside, acc[c, start:stop, :] / fold, 0.0) for c in range(blocks - 1)], axis=1)
+    v = v.astype(BF16).astype(F32)
+    vs[0, start:stop, :] = jnp.where(lane == 0, 0.0, pltpu.roll(v, 1, 1))
+    vs[1, start:stop, :] = v
+    vs[2, start:stop, :] = jnp.where(lane == samples - 1, 0.0, pltpu.roll(v, samples - 1, 1))
+
+
+def convolve(m, vs, w_ref, block):
+    taps = jnp.concatenate([vs[dt, EDGE * m : EDGE * (m + 2), :] for dt in range(3)], axis=0).astype(BF16)
+    for c in range(0, vs.shape[2], 256):
+        part = jnp.dot(w_ref[...], taps[:, c : c + 256], preferred_element_type=F32)
+        block[:, :, :, c : c + 256] = part.astype(BF16).reshape(2, 16, 16, 256)
+
+
+def inner_kernel(main_ref, left_ref, right_ref, w_ref, out_hbm, acc, vs, out, sems):
+    acc[...] = main_ref[...]
+    add_sides(acc, left_ref, right_ref, 2, 14)
+    done, slots = EDGE // 8 * 8, out.shape[0]
     stores = []
-    for m in range(8):
-        first, last = EDGE * m, EDGE * m + 2 * EDGE
-        needed = min(bins, -(-last // 8) * 8)
-        taps_of(done, needed)
+    for m in range(1, 7):
+        needed = EDGE * (m + 2) // 8 * 8 + 8 * (EDGE * (m + 2) % 8 > 0)
+        make_taps(acc, vs, done, needed)
         done = needed
-        taps = jnp.concatenate([vs[dt, first:last, :] for dt in range(3)], axis=0).astype(BF16)
-        if m >= slots:
-            stores[m - slots].wait()
-        for c in range(0, samples, 256):
-            part = jnp.dot(w_ref[...], taps[:, c : c + 256], preferred_element_type=F32)
-            out[m % slots, :, :, :, c : c + 256] = part.astype(BF16).reshape(2, 16, 16, 256)
-        store = pltpu.make_async_copy(
-            out.at[m % slots], out_hbm.at[pl.ds(2 * m, 2)], sems.at[m % slots]
-        )
+        k = m - 1
+        if k >= slots:
+            stores[k - slots].wait()
+        convolve(m, vs, w_ref, out.at[k % slots])
+        store = pltpu.make_async_copy(out.at[k % slots], out_hbm.at[pl.ds(2 * m, 2)], sems.at[k % slots])
         store.start()
         stores.append(store)
-    for store in stores[8 - slots :]:
+    for store in stores[6 - slots :]:
+        store.wait()
+
+
+def outer_kernel(main_ref, left_ref, right_ref, above_ref, below_ref, w_ref, _, out_hbm, acc, vs, out, sems):
+    blocks, bins, _ = acc.shape
+    top, bottom = 2 * EDGE, (bins - 2 * EDGE) // 8 * 8 - 8
+    for c in range(blocks):
+        lanes = slice(128 * c, 128 * (c + 1))
+        acc[c, 0:top, :] = main_ref[c, 0:top, :]
+        acc[c, bottom:bins, :] = main_ref[c, bottom:bins, :]
+        acc[c, 0:STRIP, :] += above_ref[:, lanes].astype(F32)
+        acc[c, bins - STRIP : bins, :] += below_ref[:, lanes].astype(F32)
+    stores = []
+    for k, (m, start, stop, row) in enumerate(((0, 0, top, 0), (7, bottom, bins, 14))):
+        add_sides(acc, left_ref, right_ref, row, 4)
+        make_taps(acc, vs, start, stop)
+        convolve(m, vs, w_ref, out.at[k])
+        store = pltpu.make_async_copy(out.at[k], out_hbm.at[pl.ds(2 * m, 2)], sems.at[k])
+        store.start()
+        stores.append(store)
+    for store in stores:
         store.wait()
 
 
@@ -324,44 +348,57 @@
     received = lax.all_to_all(
         outgoing.reshape(devices, 8, width), ("inline", "xline"), split_axis=0, concat_axis=0, tiled=True
     ).reshape(slots, width)
-    main, up, down, cols = pl.pallas_call(
+    strip = jax.ShapeDtypeStruct((48, width), BF16)
+    edge = jax.ShapeDtypeStruct((STRIP, width), BF16)
+    main, left, right = pl.pallas_call(
         stack_kernel,
-        out_shape=[
-            jax.ShapeDtypeStruct((width // 128, bins, 128), F32),
-            jax.ShapeDtypeStruct((STRIP, width), BF16),
-            jax.ShapeDtypeStruct((STRIP, width), BF16),
-            jax.ShapeDtypeStruct((width // 128, 96, 128), F32),
-        ],
+        out_shape=[jax.ShapeDtypeStruct((width // 128, bins, 128), F32), strip, strip],
         in_specs=[vmem] * 2,
-        out_specs=[vmem] * 4,
+        out_specs=[vmem] * 3,
         compiler_params=params,
         name="stack",
     )(received, folds)
-    above, below = neighbours(up, down, "inline")
-    left, right = pl.pallas_call(
-        columns_kernel,
-        out_shape=[jax.ShapeDtypeStruct((48, width), BF16)] * 2,
+    from_left, from_right = neighbours(left, right, "xline")
+    up, down = pl.pallas_call(
+        edges_kernel,
+        out_shape=[edge, edge],
         in_specs=[vmem] * 3,
         out_specs=[vmem] * 2,
-        scratch_shapes=[pltpu.VMEM((96, width), F32)],
+        scratch_shapes=[pltpu.VMEM((STRIP, width), F32)] * 2,
         compiler_params=params,
-        name="columns",
-    )(cols, above, below)
-    from_left, from_right = neighbours(left, right, "xline")
-    return pl.pallas_call(
-        volume_kernel,
-        out_shape=jax.ShapeDtypeStruct((16, 16, 16, samples), BF16),
-        in_specs=[vmem] * 6,
-        out_specs=hbm,
-        scratch_shapes=[
+        name="edges",
+    )(main, from_left, from_right)
+    above, below = neighbours(up, down, "inline")
+
+    def scratch(slots):
+        return [
             pltpu.VMEM((width // 128, bins, 128), F32),
             pltpu.VMEM((3, bins, samples), F32),
-            pltpu.VMEM((3, 2, 16, 16, samples), BF16),
-            pltpu.SemaphoreType.DMA((3,)),
-        ],
+            pltpu.VMEM((slots, 2, 16, 16, samples), BF16),
+            pltpu.SemaphoreType.DMA((slots,)),
+        ]
+
+    features = jax.ShapeDtypeStruct((16, 16, 16, samples), BF16)
+    inner = pl.pallas_call(
+        inner_kernel,
+        out_shape=features,
+        in_specs=[vmem] * 4,
+        out_specs=hbm,
+        scratch_shapes=scratch(3),
         compiler_params=params,
-        name="volume",
-    )(main, above, below, from_left, from_right, w_taps)
+        cost_estimate=pl.CostEstimate(flops=1 << 32, transcendentals=0, bytes_accessed=8 << 20),
+        name="inner",
+    )(main, from_left, from_right, w_taps)
+    return pl.pallas_call(
+        outer_kernel,
+        out_shape=features,
+        in_specs=[vmem] * 6 + [hbm],
+        out_specs=hbm,
+        scratch_shapes=scratch(2),
+        input_output_aliases={6: 0},
+        compiler_params=params,
+        name="outer",
+    )(main, from_left, from_right, above, below, w_taps, inner)
 
 
 def solution(mesh):

time: 80.7 us -> 79.2 us (0.981)
  waiting for transfers between devices: 39.1 us -> 35.2 us
  starting transfers between devices: 20.7 us -> 22.1 us
  Pallas kernels: 20.3 us -> 21.2 us
    ppermute x4, waiting for transfers between devices: 8.13 us -> 4.2 us  [neighbours(): return (lax.ppermute(last, axis, up), lax.ppermute(first, axis, down))]
    ppermute x4, starting transfers between devices: 9.17 us -> 10.6 us  [neighbours(): return (lax.ppermute(last, axis, up), lax.ppermute(first, axis, down))]
    pallas_call x2 -> x3, Pallas kernels: 5.06 us -> 6.07 us  [the longest x1 3.96 us: body(): pl.pallas_call(inner_kernel, out_shape=features, in_specs=[vmem] * 4, out...]
  transfers between devices with their start and end apart: 5 -> 5, of which waited for: 4 -> 3; matrix products, arithmetic and copies ran while one was open for 0% -> 0% of each run, Pallas kernels for 2% -> 7%
where the time goes in v4:
time: 79.2 us; the launch traced here: 78.9 us
  waiting for transfers between devices  35.2 us (44%)
  starting transfers between devices  22.1 us (28%)
  Pallas kernels  21.2 us (27%)
    all_to_all x1, waiting for transfers between devices, body(): lax.all_to_all(outgoing.reshape(devices, 8, width), ('inline', 'xline'),...  31 us
    pallas_call x1, Pallas kernels, body(): pl.pallas_call(denoise_kernel, out_shape=jax.ShapeDtypeStruct((slots, wid...  12.8 us
    all_to_all x1, starting transfers between devices, body(): lax.all_to_all(outgoing.reshape(devices, 8, width), ('inline', 'xline'),...  11.5 us
    ppermute x4, starting transfers between devices, neighbours(): return (lax.ppermute(last, axis, up), lax.ppermute(first, axis, down))  10.6 us
    ppermute x4, waiting for transfers between devices, neighbours(): return (lax.ppermute(last, axis, up), lax.ppermute(first, axis, down))  4.2 us
    pallas_call x1, Pallas kernels, body(): pl.pallas_call(inner_kernel, out_shape=features, in_specs=[vmem] * 4, out...  3.96 us
    pallas_call x1, Pallas kernels, body(): pl.pallas_call(outer_kernel, out_shape=features, in_specs=[vmem] * 6 + [h...  2.03 us
  transfers between devices with their start and end apart: 5, of which 3 were waited for; matrix products, arithmetic and copies ran while one was open for 0% of the time, Pallas kernels for 7%

profile of v4, /device:TPU:1, one launch (start us, length us, event | category | flops | bytes accessed | tf_op | source)
XLA Modules:
  0.0 78.9 jit_solution(15215866758053441661)
XLA Ops:
  0.0 12.8 %denoise.1 = bf16[1024,1152]{1,0:T(8,128)(2,1)} custom-call(bf16[256,1024]{1,0:T(8,128)(2,1)} %refs_0_.1, s32[1,256]{1,0:T(1,128)} %bitcast.10, s32[1,256]{1,0:T(1,128)} %bitcast.11, bf16[3,32]{1,0:T(4,128)(2,1)} %bitcast.12, bf16[96,32]{1,0:T(8,128)(2,1)} %bitcast.9, bf16[1,32]{1,0:T(2,128)(2,1)} %bitcast.13), custom_call_target="tpu_custom_call" | custom-call | tf_op jit(solution)/shard_map/denoise/pallas_call | solution.py:306
  12.8 0.0 copy-start
  12.9 0.0 copy-start.1
  12.9 11.5 %all-to-all-start = ((bf16[128,8,1152]{2,1,0:T(8,128)(2,1)}), bf16[128,8,1152]{2,1,0:T(8,128)(2,1)S(1)}, u32[]{:S(2)}, u32[]{:S(2)}) async-start(bf16[128,8,1152]{2,1,0:T(8,128)(2,1)} %bitcast.8), calls=%async_computation | async-start | bytes 4718592 | tf_op jit(solution)/shard_map/all_to_all | solution.py:348
  24.4 0.0 copy-done
  24.4 0.0 copy-done.1
  24.4 1.4 %prepare.1 = (f32[328,128]{1,0:T(8,128)S(1)}, bf16[512,216]{1,0:T(8,128)(2,1)S(1)}) custom-call(s32[16,16]{1,0:T(8,128)S(1)} %copy-done, bf16[16,27]{1,0:T(8,128)(2,1)S(1)} %copy-done.1), custom_call_target="tpu_custom_call" | custom-call | tf_op jit(solution)/shard_map/prepare/pallas_call | solution.py:340
  25.8 31.0 %all-to-all-done = bf16[128,8,1152]{2,1,0:T(8,128)(2,1)S(1)} async-done(((bf16[128,8,1152]{2,1,0:T(8,128)(2,1)}), bf16[128,8,1152]{2,1,0:T(8,128)(2,1)S(1)}, u32[]{:S(2)}, u32[]{:S(2)}) %all-to-all-start) | async-done | bytes 2359328 | tf_op jit(solution)/shard_map/all_to_all | solution.py:348
  56.8 1.0 %stack.1 = (f32[9,328,128]{2,1,0:T(8,128)S(1)}, bf16[48,1152]{1,0:T(8,128)(2,1)S(1)}, bf16[48,1152]{1,0:T(8,128)(2,1)S(1)}) custom-call(bf16[1024,1152]{1,0:T(8,128)(2,1)S(1)} %bitcast.7, f32[328,128]{1,0:T(8,128)S(1)} %get-tuple-element.12.fold_ref), custom_call_target="tpu_custom_call" | custom-call | tf_op jit(solution)/shard_map/stack/pallas_call | solution.py:353
  57.8 2.6 %collective-permute-start = (bf16[48,1152]{1,0:T(8,128)(2,1)S(1)}, bf16[48,1152]{1,0:T(8,128)(2,1)S(1)}, u32[]{:S(2)}, u32[]{:S(2)}) collective-permute-start(bf16[48,1152]{1,0:T(8,128)(2,1)S(1)} %get-tuple-element.14), channel_id=1, source_target_pairs={{0,1},{1,2},{2,3},{3,4},{4,5},{5,6},{6,7},{7,8},{8,9},{9,10},{10,1... | collective-permute-start | bytes 331784 | tf_op jit(solution)/shard_map/ppermute | solution.py:294
  60.4 1.3 %collective-permute-start.1 = (bf16[48,1152]{1,0:T(8,128)(2,1)S(1)}, bf16[48,1152]{1,0:T(8,128)(2,1)S(1)}, u32[]{:S(2)}, u32[]{:S(2)}) collective-permute-start(bf16[48,1152]{1,0:T(8,128)(2,1)S(1)} %get-tuple-element.15), channel_id=1, source_target_pairs={{1,0},{2,1},{3,2},{4,3},{5,4},{6,5},{7,6},{8,7},{9,8},{10,9},{11,1... | collective-permute-start | bytes 331784 | tf_op jit(solution)/shard_map/ppermute | solution.py:294
  61.7 0.4 collective-permute-done.left_ref
  62.1 3.8 %collective-permute-done.1.right_ref = bf16[48,1152]{1,0:T(8,128)(2,1)S(1)} collective-permute-done((bf16[48,1152]{1,0:T(8,128)(2,1)S(1)}, bf16[48,1152]{1,0:T(8,128)(2,1)S(1)}, u32[]{:S(2)}, u32[]{:S(2)}) %collective-permute-start.1) | collective-permute-done | bytes 110624 | tf_op jit(solution)/shard_map/ppermute | solution.py:294
  65.9 0.1 edges.1
  66.0 4.8 %collective-permute-start.2 = (bf16[40,1152]{1,0:T(8,128)(2,1)S(1)}, bf16[40,1152]{1,0:T(8,128)(2,1)S(1)}, u32[]{:S(2)}, u32[]{:S(2)}) collective-permute-start(bf16[40,1152]{1,0:T(8,128)(2,1)S(1)} %get-tuple-element.16), channel_id=1, source_target_pairs={{0,16},{16,32},{32,48},{48,64},{64,80},{80,96},{96,112},{1,17},{17... | collective-permute-start | bytes 276488 | tf_op jit(solution)/shard_map/ppermute | solution.py:294
  70.8 1.9 %collective-permute-start.3 = (bf16[40,1152]{1,0:T(8,128)(2,1)S(1)}, bf16[40,1152]{1,0:T(8,128)(2,1)S(1)}, u32[]{:S(2)}, u32[]{:S(2)}) collective-permute-start(bf16[40,1152]{1,0:T(8,128)(2,1)S(1)} %get-tuple-element.17), channel_id=1, source_target_pairs={{16,0},{32,16},{48,32},{64,48},{80,64},{96,80},{112,96},{17,1},{33... | collective-permute-start | bytes 276488 | tf_op jit(solution)/shard_map/ppermute | solution.py:294
  72.7 4.0 %inner.1._ = bf16[16,16,16,1024]{3,2,1,0:T(8,128)(2,1)} custom-call(f32[9,328,128]{2,1,0:T(8,128)S(1)} %get-tuple-element.13.main_ref, bf16[48,1152]{1,0:T(8,128)(2,1)S(1)} %collective-permute-done.left_ref, bf16[48,1152]{1,0:T(8,128)(2,1)S(1)} %collective-permute-done.1.right_ref, bf16[512,216]{1,0:T(8,128)(2,1)S(1)} %get-tuple-element.18.w_ref), custom_call_target="tpu_custom_call" | custom-call | flops 4294967296 | bytes 8388608 | tf_op jit(solution)/shard_map/inner/pallas_call | solution.py:382
  76.7 0.0 collective-permute-done.2.above_ref
  76.7 0.0 collective-permute-done.3.below_ref
  76.7 2.0 %outer.1 = bf16[16,16,16,1024]{3,2,1,0:T(8,128)(2,1)} custom-call(f32[9,328,128]{2,1,0:T(8,128)S(1)} %get-tuple-element.13.main_ref, bf16[48,1152]{1,0:T(8,128)(2,1)S(1)} %collective-permute-done.left_ref, bf16[48,1152]{1,0:T(8,128)(2,1)S(1)} %collective-permute-done.1.right_ref, ...), custom_call_target="tpu_custom_call", output_to_operand_aliasing={{}: (6, {})} | custom-call | tf_op jit(solution)/shard_map/outer/pallas_call | solution.py:392
Async XLA Ops:
  12.8 11.5 %copy-start = (s32[16,16]{1,0:T(8,128)S(1)}, s32[16,16]{1,0:T(8,128)}, u32[]{:S(2)}) copy-start(s32[16,16]{1,0:T(8,128)} %fold_ref.1) | copy-start | bytes 3076
  12.9 11.5 %copy-start.1 = (bf16[16,27]{1,0:T(8,128)(2,1)S(1)}, bf16[16,27]{1,0:T(8,128)(2,1)}, u32[]{:S(2)}) copy-start(bf16[16,27]{1,0:T(8,128)(2,1)} %wv_ref.1) | copy-start | bytes 2596
  12.9 44.0 %all-to-all-start = ((bf16[128,8,1152]{2,1,0:T(8,128)(2,1)}), bf16[128,8,1152]{2,1,0:T(8,128)(2,1)S(1)}, u32[]{:S(2)}, u32[]{:S(2)}) async-start(bf16[128,8,1152]{2,1,0:T(8,128)(2,1)} %bitcast.8), calls=%async_computation | async-start | bytes 4718592 | tf_op jit(solution)/shard_map/all_to_all | solution.py:348
  57.8 4.3 %collective-permute-start = (bf16[48,1152]{1,0:T(8,128)(2,1)S(1)}, bf16[48,1152]{1,0:T(8,128)(2,1)S(1)}, u32[]{:S(2)}, u32[]{:S(2)}) collective-permute-start(bf16[48,1152]{1,0:T(8,128)(2,1)S(1)} %get-tuple-element.14), channel_id=1, source_target_pairs={{0,1},{1,2},{2,3},{3,4},{4,5},{5,6},{6,7},{7,8},{8,9},{9,10},{10,1... | collective-permute-start | bytes 331784 | tf_op jit(solution)/shard_map/ppermute | solution.py:294
  60.4 5.5 %collective-permute-start.1 = (bf16[48,1152]{1,0:T(8,128)(2,1)S(1)}, bf16[48,1152]{1,0:T(8,128)(2,1)S(1)}, u32[]{:S(2)}, u32[]{:S(2)}) collective-permute-start(bf16[48,1152]{1,0:T(8,128)(2,1)S(1)} %get-tuple-element.15), channel_id=1, source_target_pairs={{1,0},{2,1},{3,2},{4,3},{5,4},{6,5},{7,6},{8,7},{9,8},{10,9},{11,1... | collective-permute-start | bytes 331784 | tf_op jit(solution)/shard_map/ppermute | solution.py:294
  66.0 10.7 %collective-permute-start.2 = (bf16[40,1152]{1,0:T(8,128)(2,1)S(1)}, bf16[40,1152]{1,0:T(8,128)(2,1)S(1)}, u32[]{:S(2)}, u32[]{:S(2)}) collective-permute-start(bf16[40,1152]{1,0:T(8,128)(2,1)S(1)} %get-tuple-element.16), channel_id=1, source_target_pairs={{0,16},{16,32},{32,48},{48,64},{64,80},{80,96},{96,112},{1,17},{17... | collective-permute-start | bytes 276488 | tf_op jit(solution)/shard_map/ppermute | solution.py:294
  70.8 5.9 %collective-permute-start.3 = (bf16[40,1152]{1,0:T(8,128)(2,1)S(1)}, bf16[40,1152]{1,0:T(8,128)(2,1)S(1)}, u32[]{:S(2)}, u32[]{:S(2)}) collective-permute-start(bf16[40,1152]{1,0:T(8,128)(2,1)S(1)} %get-tuple-element.17), channel_id=1, source_target_pairs={{16,0},{32,16},{48,32},{64,48},{80,64},{96,80},{112,96},{17,1},{33... | collective-permute-start | bytes 276488 | tf_op jit(solution)/shard_map/ppermute | solution.py:294

commit v5 on v4

--- a/solution.py
+++ b/solution.py
@@ -191,11 +191,14 @@
         main_ref[c + 1] = both[:, 128:]
     main_ref[blocks - 1] = fold_ref[...]
     pad = jnp.zeros((24 - SIDE, 128), F32)
+    at = lax.axis_index("xline")
+    sides = ((left_ref, 0, at > 0), (right_ref, 16, at < lax.axis_size("xline") - 1))
     for c in range(blocks):
         lanes = slice(128 * c, 128 * (c + 1))
-        for ref, first in ((left_ref, 0), (right_ref, 16)):
+        for ref, first, wanted in sides:
             cols = [main_ref[c, pl.ds(first + k, SIDE, stride=SIDE), :] for k in range(2)]
-            ref[:, lanes] = jnp.concatenate([cols[0], pad, cols[1], pad], axis=0).astype(BF16)
+            strip = jnp.concatenate([cols[0], pad, cols[1], pad], axis=0)
+            ref[:, lanes] = jnp.where(wanted, strip, 0.0).astype(BF16)
 
 
 def edges_kernel(main_ref, left_ref, right_ref, up_ref, down_ref, up, down):
@@ -211,8 +214,10 @@
                 at = r * SIDE + first + k
                 up[at : at + 1, :] += strip[24 * k + r : 24 * k + r + 1, :]
                 down[at : at + 1, :] += strip[24 * k + 16 + r : 24 * k + 17 + r, :]
-    up_ref[...] = jnp.where(iota(up.shape, 0) < EDGE, up[...], 0.0).astype(BF16)
-    down_ref[...] = down[...].astype(BF16)
+    at = lax.axis_index("inline")
+    wanted = (iota(up.shape, 0) < EDGE) & (at > 0)
+    up_ref[...] = jnp.where(wanted, up[...], 0.0).astype(BF16)
+    down_ref[...] = jnp.where(at < lax.axis_size("inline") - 1, down[...], 0.0).astype(BF16)
 
 
 def add_sides(acc, left_ref, right_ref, start, count):
@@ -289,7 +294,7 @@
 
 def neighbours(first, last, axis):
     size = lax.axis_size(axis)
-    up = [(i, i + 1) for i in range(size - 1)]
+    up = [(i, (i + 1) % size) for i in range(size)]
     down = [(j, i) for i, j in up]
     return lax.ppermute(last, axis, up), lax.ppermute(first, axis, down)
 

time: 79.2 us -> 75.1 us (0.948); the launches traced: 78.9 us -> 73.7 us
  starting transfers between devices: 22.1 us -> 18.7 us
  waiting for transfers between devices: 35.2 us -> 33.5 us
    ppermute x4, starting transfers between devices: 10.6 us -> 7.22 us  [neighbours(): return (lax.ppermute(last, axis, up), lax.ppermute(first, axis, down))]
    ppermute x4, waiting for transfers between devices: 4.2 us -> 2.44 us  [neighbours(): return (lax.ppermute(last, axis, up), lax.ppermute(first, axis, down))]
where the time goes in v5:
time: 75.1 us; the launch traced here: 73.7 us
  waiting for transfers between devices  33.5 us (45%)
  Pallas kernels  21.2 us (28%)
  starting transfers between devices  18.7 us (25%)
    all_to_all x1, waiting for transfers between devices, body(): lax.all_to_all(outgoing.reshape(devices, 8, width), ('inline', 'xline'),...  31 us
    pallas_call x1, Pallas kernels, body(): pl.pallas_call(denoise_kernel, out_shape=jax.ShapeDtypeStruct((slots, wid...  12.8 us
    all_to_all x1, starting transfers between devices, body(): lax.all_to_all(outgoing.reshape(devices, 8, width), ('inline', 'xline'),...  11.5 us
    ppermute x4, starting transfers between devices, neighbours(): return (lax.ppermute(last, axis, up), lax.ppermute(first, axis, down))  7.22 us
    pallas_call x1, Pallas kernels, body(): pl.pallas_call(inner_kernel, out_shape=features, in_specs=[vmem] * 4, out...  3.95 us
    ppermute x4, waiting for transfers between devices, neighbours(): return (lax.ppermute(last, axis, up), lax.ppermute(first, axis, down))  2.44 us
    pallas_call x1, Pallas kernels, body(): pl.pallas_call(outer_kernel, out_shape=features, in_specs=[vmem] * 6 + [h...  2.02 us
  transfers between devices with their start and end apart: 5, of which 3 were waited for; matrix products, arithmetic and copies ran while one was open for 0% of the time, Pallas kernels for 7%

profile of v5, /device:TPU:1, one launch (start us, length us, event | category | flops | bytes accessed | tf_op | source)
XLA Modules:
  0.0 73.7 jit_solution(14621848535077304920)
XLA Ops:
  0.0 12.8 %denoise.1 = bf16[1024,1152]{1,0:T(8,128)(2,1)} custom-call(bf16[256,1024]{1,0:T(8,128)(2,1)} %refs_0_.1, s32[1,256]{1,0:T(1,128)} %bitcast.10, s32[1,256]{1,0:T(1,128)} %bitcast.11, bf16[3,32]{1,0:T(4,128)(2,1)} %bitcast.12, bf16[96,32]{1,0:T(8,128)(2,1)} %bitcast.9, bf16[1,32]{1,0:T(2,128)(2,1)} %bitcast.13), custom_call_target="tpu_custom_call" | custom-call | tf_op jit(solution)/shard_map/denoise/pallas_call | solution.py:311
  12.8 0.0 copy-start
  12.9 0.0 copy-start.1
  12.9 11.5 %all-to-all-start = ((bf16[128,8,1152]{2,1,0:T(8,128)(2,1)}), bf16[128,8,1152]{2,1,0:T(8,128)(2,1)S(1)}, u32[]{:S(2)}, u32[]{:S(2)}) async-start(bf16[128,8,1152]{2,1,0:T(8,128)(2,1)} %bitcast.8), calls=%async_computation | async-start | bytes 4718592 | tf_op jit(solution)/shard_map/all_to_all | solution.py:353
  24.4 0.0 copy-done
  24.4 0.0 copy-done.1
  24.4 1.4 %prepare.1 = (f32[328,128]{1,0:T(8,128)S(1)}, bf16[512,216]{1,0:T(8,128)(2,1)S(1)}) custom-call(s32[16,16]{1,0:T(8,128)S(1)} %copy-done, bf16[16,27]{1,0:T(8,128)(2,1)S(1)} %copy-done.1), custom_call_target="tpu_custom_call" | custom-call | tf_op jit(solution)/shard_map/prepare/pallas_call | solution.py:345
  25.8 31.0 %all-to-all-done = bf16[128,8,1152]{2,1,0:T(8,128)(2,1)S(1)} async-done(((bf16[128,8,1152]{2,1,0:T(8,128)(2,1)}), bf16[128,8,1152]{2,1,0:T(8,128)(2,1)S(1)}, u32[]{:S(2)}, u32[]{:S(2)}) %all-to-all-start) | async-done | bytes 2359328 | tf_op jit(solution)/shard_map/all_to_all | solution.py:353
  56.8 0.9 %stack.1 = (f32[9,328,128]{2,1,0:T(8,128)S(1)}, bf16[48,1152]{1,0:T(8,128)(2,1)S(1)}, bf16[48,1152]{1,0:T(8,128)(2,1)S(1)}) custom-call(bf16[1024,1152]{1,0:T(8,128)(2,1)S(1)} %bitcast.7, f32[328,128]{1,0:T(8,128)S(1)} %get-tuple-element.12.fold_ref), custom_call_target="tpu_custom_call" | custom-call | tf_op jit(solution)/shard_map/stack/pallas_call | solution.py:358
  57.8 0.8 %collective-permute-start = (bf16[48,1152]{1,0:T(8,128)(2,1)S(1)}, bf16[48,1152]{1,0:T(8,128)(2,1)S(1)}, u32[]{:S(2)}, u32[]{:S(2)}) collective-permute-start(bf16[48,1152]{1,0:T(8,128)(2,1)S(1)} %get-tuple-element.14), channel_id=1, source_target_pairs={{0,1},{1,2},{2,3},{3,4},{4,5},{5,6},{6,7},{7,8},{8,9},{9,10},{10,1... | collective-permute-start | bytes 331784 | tf_op jit(solution)/shard_map/ppermute | solution.py:299
  58.5 4.1 %collective-permute-start.1 = (bf16[48,1152]{1,0:T(8,128)(2,1)S(1)}, bf16[48,1152]{1,0:T(8,128)(2,1)S(1)}, u32[]{:S(2)}, u32[]{:S(2)}) collective-permute-start(bf16[48,1152]{1,0:T(8,128)(2,1)S(1)} %get-tuple-element.15), channel_id=1, source_target_pairs={{1,0},{2,1},{3,2},{4,3},{5,4},{6,5},{7,6},{8,7},{9,8},{10,9},{11,1... | collective-permute-start | bytes 331784 | tf_op jit(solution)/shard_map/ppermute | solution.py:299
  62.6 2.1 %collective-permute-done.left_ref = bf16[48,1152]{1,0:T(8,128)(2,1)S(1)} collective-permute-done((bf16[48,1152]{1,0:T(8,128)(2,1)S(1)}, bf16[48,1152]{1,0:T(8,128)(2,1)S(1)}, u32[]{:S(2)}, u32[]{:S(2)}) %collective-permute-start) | collective-permute-done | bytes 110624 | tf_op jit(solution)/shard_map/ppermute | solution.py:299
  64.8 0.0 collective-permute-done.1.right_ref
  64.8 0.1 edges.1
  64.9 2.4 %collective-permute-start.2 = (bf16[40,1152]{1,0:T(8,128)(2,1)S(1)}, bf16[40,1152]{1,0:T(8,128)(2,1)S(1)}, u32[]{:S(2)}, u32[]{:S(2)}) collective-permute-start(bf16[40,1152]{1,0:T(8,128)(2,1)S(1)} %get-tuple-element.16), channel_id=1, source_target_pairs={{0,16},{16,32},{32,48},{48,64},{64,80},{80,96},{96,112},{112,0},{1... | collective-permute-start | bytes 276488 | tf_op jit(solution)/shard_map/ppermute | solution.py:299
  67.2 0.0 collective-permute-start.3
  67.2 3.9 %inner.1._ = bf16[16,16,16,1024]{3,2,1,0:T(8,128)(2,1)} custom-call(f32[9,328,128]{2,1,0:T(8,128)S(1)} %get-tuple-element.13.main_ref, bf16[48,1152]{1,0:T(8,128)(2,1)S(1)} %collective-permute-done.left_ref, bf16[48,1152]{1,0:T(8,128)(2,1)S(1)} %collective-permute-done.1.right_ref, bf16[512,216]{1,0:T(8,128)(2,1)S(1)} %get-tuple-element.18.w_ref), custom_call_target="tpu_custom_call" | custom-call | flops 4294967296 | bytes 8388608 | tf_op jit(solution)/shard_map/inner/pallas_call | solution.py:387
  71.2 0.0 collective-permute-done.2.above_ref
  71.2 0.3 collective-permute-done.3.below_ref
  71.5 2.0 %outer.1 = bf16[16,16,16,1024]{3,2,1,0:T(8,128)(2,1)} custom-call(f32[9,328,128]{2,1,0:T(8,128)S(1)} %get-tuple-element.13.main_ref, bf16[48,1152]{1,0:T(8,128)(2,1)S(1)} %collective-permute-done.left_ref, bf16[48,1152]{1,0:T(8,128)(2,1)S(1)} %collective-permute-done.1.right_ref, ...), custom_call_target="tpu_custom_call", output_to_operand_aliasing={{}: (6, {})} | custom-call | tf_op jit(solution)/shard_map/outer/pallas_call | solution.py:397
Async XLA Ops:
  12.8 11.5 %copy-start = (s32[16,16]{1,0:T(8,128)S(1)}, s32[16,16]{1,0:T(8,128)}, u32[]{:S(2)}) copy-start(s32[16,16]{1,0:T(8,128)} %fold_ref.1) | copy-start | bytes 3076
  12.9 11.5 %copy-start.1 = (bf16[16,27]{1,0:T(8,128)(2,1)S(1)}, bf16[16,27]{1,0:T(8,128)(2,1)}, u32[]{:S(2)}) copy-start(bf16[16,27]{1,0:T(8,128)(2,1)} %wv_ref.1) | copy-start | bytes 2596
  12.9 44.0 %all-to-all-start = ((bf16[128,8,1152]{2,1,0:T(8,128)(2,1)}), bf16[128,8,1152]{2,1,0:T(8,128)(2,1)S(1)}, u32[]{:S(2)}, u32[]{:S(2)}) async-start(bf16[128,8,1152]{2,1,0:T(8,128)(2,1)} %bitcast.8), calls=%async_computation | async-start | bytes 4718592 | tf_op jit(solution)/shard_map/all_to_all | solution.py:353
  57.8 7.0 %collective-permute-start = (bf16[48,1152]{1,0:T(8,128)(2,1)S(1)}, bf16[48,1152]{1,0:T(8,128)(2,1)S(1)}, u32[]{:S(2)}, u32[]{:S(2)}) collective-permute-start(bf16[48,1152]{1,0:T(8,128)(2,1)S(1)} %get-tuple-element.14), channel_id=1, source_target_pairs={{0,1},{1,2},{2,3},{3,4},{4,5},{5,6},{6,7},{7,8},{8,9},{9,10},{10,1... | collective-permute-start | bytes 331784 | tf_op jit(solution)/shard_map/ppermute | solution.py:299
  58.5 6.2 %collective-permute-start.1 = (bf16[48,1152]{1,0:T(8,128)(2,1)S(1)}, bf16[48,1152]{1,0:T(8,128)(2,1)S(1)}, u32[]{:S(2)}, u32[]{:S(2)}) collective-permute-start(bf16[48,1152]{1,0:T(8,128)(2,1)S(1)} %get-tuple-element.15), channel_id=1, source_target_pairs={{1,0},{2,1},{3,2},{4,3},{5,4},{6,5},{7,6},{8,7},{9,8},{10,9},{11,1... | collective-permute-start | bytes 331784 | tf_op jit(solution)/shard_map/ppermute | solution.py:299
  64.9 6.3 %collective-permute-start.2 = (bf16[40,1152]{1,0:T(8,128)(2,1)S(1)}, bf16[40,1152]{1,0:T(8,128)(2,1)S(1)}, u32[]{:S(2)}, u32[]{:S(2)}) collective-permute-start(bf16[40,1152]{1,0:T(8,128)(2,1)S(1)} %get-tuple-element.16), channel_id=1, source_target_pairs={{0,16},{16,32},{32,48},{48,64},{64,80},{80,96},{96,112},{112,0},{1... | collective-permute-start | bytes 276488 | tf_op jit(solution)/shard_map/ppermute | solution.py:299
  67.2 4.3 %collective-permute-start.3 = (bf16[40,1152]{1,0:T(8,128)(2,1)S(1)}, bf16[40,1152]{1,0:T(8,128)(2,1)S(1)}, u32[]{:S(2)}, u32[]{:S(2)}) collective-permute-start(bf16[40,1152]{1,0:T(8,128)(2,1)S(1)} %get-tuple-element.17), channel_id=1, source_target_pairs={{16,0},{32,16},{48,32},{64,48},{80,64},{96,80},{112,96},{0,112},{1... | collective-permute-start | bytes 276488 | tf_op jit(solution)/shard_map/ppermute | solution.py:299

commit v6 on v5

--- a/solution.py
+++ b/solution.py
@@ -42,7 +42,7 @@
     windows = -(-samples // WIN)
     hidden_bufs = (ha, hb)
 
-    for load in loads[1:]:
+    for load in loads:
         load.wait()
 
     own = own_ref[...]
@@ -61,11 +61,6 @@
         )
         store.start()
         stores.append(store)
-
-    which = iota((TAIL, traces), 0)
-    row, col = bins_ref[...] // 18 + 1, bins_ref[...] % 18 + 1
-    tail = jnp.where(which == 0, row, jnp.where(which == 1, col, 0)).astype(F32).astype(BF16)
-    place(samples, TAIL, tail)
 
     wf = wf_ref[...].astype(F32)
     taps = [jnp.broadcast_to(column(wf[k : k + 1], 32), (32, 32)) for k in range(3)]
@@ -92,7 +87,6 @@
     of_row = jnp.where(row // 8 * 4 + row % 4 == iota((64, 32), 1), wn_ref[...].astype(F32), 0.0)
     wn[...] = jnp.broadcast_to(jnp.sum(of_row, axis=1, keepdims=True), wn.shape)
 
-    loads[0].wait()
     xt[0:PAD, :] = jnp.zeros((PAD, traces), F32)
     xt[PAD + samples : rows, :] = jnp.zeros((rows - PAD - samples, traces), F32)
     for k in range(samples // 128):
@@ -133,6 +127,11 @@
             jnp.dot(w1[192 * p + 160 : 192 * (p + 1), :], xs, preferred_element_type=F32)
         )
     hidden(0, ha, hb)
+    placed = 0
+    which = iota((TAIL, traces), 0)
+    row, col = bins_ref[...] // 18 + 1, bins_ref[...] % 18 + 1
+    tail = jnp.where(which == 0, row, jnp.where(which == 1, col, 0)).astype(F32).astype(BF16)
+    place(samples, TAIL, tail)
     for j in range(windows):
         this, other = hidden_bufs[j % 2], hidden_bufs[1 - j % 2]
         if j + 1 < windows:
@@ -142,9 +141,10 @@
             for p in range(4):
                 this[p, inside:, :] = jnp.zeros((256 - inside, traces), BF16)
         second(j, this)
-        while len(stores) - 1 < min(WIN * (j + 1), samples) // 256:
-            start = 256 * (len(stores) - 1)
-            place(start, 256, dt[start : start + 256, :].astype(BF16))
+        ready = min(WIN * (j + 1), samples)
+        while placed < samples and placed + 256 <= ready:
+            place(placed, 256, dt[placed : placed + 256, :].astype(BF16))
+            placed += 256
     for store in stores:
         store.wait()
 
@@ -190,14 +190,14 @@
         main_ref[c] = both[:, :128]
         main_ref[c + 1] = both[:, 128:]
     main_ref[blocks - 1] = fold_ref[...]
-    pad = jnp.zeros((24 - SIDE, 128), F32)
+    pad = jnp.zeros((STRIP - EDGE, 128), F32)
     at = lax.axis_index("xline")
     sides = ((left_ref, 0, at > 0), (right_ref, 16, at < lax.axis_size("xline") - 1))
     for c in range(blocks):
         lanes = slice(128 * c, 128 * (c + 1))
         for ref, first, wanted in sides:
             cols = [main_ref[c, pl.ds(first + k, SIDE, stride=SIDE), :] for k in range(2)]
-            strip = jnp.concatenate([cols[0], pad, cols[1], pad], axis=0)
+            strip = jnp.concatenate([cols[0], cols[1], pad], axis=0)
             ref[:, lanes] = jnp.where(wanted, strip, 0.0).astype(BF16)
 
 
@@ -212,8 +212,8 @@
         for k in range(2):
             for r in range(2):
                 at = r * SIDE + first + k
-                up[at : at + 1, :] += strip[24 * k + r : 24 * k + r + 1, :]
-                down[at : at + 1, :] += strip[24 * k + 16 + r : 24 * k + 17 + r, :]
+                up[at : at + 1, :] += strip[SIDE * k + r : SIDE * k + r + 1, :]
+                down[at : at + 1, :] += strip[SIDE * k + 16 + r : SIDE * k + 17 + r, :]
     at = lax.axis_index("inline")
     wanted = (iota(up.shape, 0) < EDGE) & (at > 0)
     up_ref[...] = jnp.where(wanted, up[...], 0.0).astype(BF16)
@@ -227,7 +227,7 @@
             strip = ref[:, lanes].astype(F32)
             for k in range(2):
                 rows = pl.ds(start * SIDE + first + k, count, stride=SIDE)
-                acc[c, rows, :] += strip[24 * k + start : 24 * k + start + count, :]
+                acc[c, rows, :] += strip[SIDE * k + start : SIDE * k + start + count, :]
 
 
 def make_taps(acc, vs, start, stop):
@@ -254,17 +254,17 @@
 def inner_kernel(main_ref, left_ref, right_ref, w_ref, out_hbm, acc, vs, out, sems):
     acc[...] = main_ref[...]
     add_sides(acc, left_ref, right_ref, 2, 14)
-    done, slots = EDGE // 8 * 8, out.shape[0]
+    slots = out.shape[0]
     stores = []
-    for m in range(1, 7):
-        needed = EDGE * (m + 2) // 8 * 8 + 8 * (EDGE * (m + 2) % 8 > 0)
-        make_taps(acc, vs, done, needed)
-        done = needed
-        k = m - 1
+    ends = [EDGE // 8 * 8] + [-(-EDGE * (m + 2) // 8) * 8 for m in range(1, 7)]
+    make_taps(acc, vs, ends[0], ends[1])
+    for k in range(6):
         if k >= slots:
             stores[k - slots].wait()
-        convolve(m, vs, w_ref, out.at[k % slots])
-        store = pltpu.make_async_copy(out.at[k % slots], out_hbm.at[pl.ds(2 * m, 2)], sems.at[k % slots])
+        if k < 5:
+            make_taps(acc, vs, ends[k + 1], ends[k + 2])
+        convolve(k + 1, vs, w_ref, out.at[k % slots])
+        store = pltpu.make_async_copy(out.at[k % slots], out_hbm.at[pl.ds(2 * k + 2, 2)], sems.at[k % slots])
         store.start()
         stores.append(store)
     for store in stores[6 - slots :]:
@@ -353,11 +353,10 @@
     received = lax.all_to_all(
         outgoing.reshape(devices, 8, width), ("inline", "xline"), split_axis=0, concat_axis=0, tiled=True
     ).reshape(slots, width)
-    strip = jax.ShapeDtypeStruct((48, width), BF16)
     edge = jax.ShapeDtypeStruct((STRIP, width), BF16)
     main, left, right = pl.pallas_call(
         stack_kernel,
-        out_shape=[jax.ShapeDtypeStruct((width // 128, bins, 128), F32), strip, strip],
+        out_shape=[jax.ShapeDtypeStruct((width // 128, bins, 128), F32), edge, edge],
         in_specs=[vmem] * 2,
         out_specs=[vmem] * 3,
         compiler_params=params,

time: 75.1 us -> 74.7 us (level)
  no operation moved by 1% of the time
where the time goes in v6:
time: 74.7 us; the launch traced here: 73.3 us
  waiting for transfers between devices  33.2 us (44%)
  Pallas kernels  21.1 us (28%)
  starting transfers between devices  18.7 us (25%)
    all_to_all x1, waiting for transfers between devices, body(): lax.all_to_all(outgoing.reshape(devices, 8, width), ('inline', 'xline'),...  31 us
    pallas_call x1, Pallas kernels, body(): pl.pallas_call(denoise_kernel, out_shape=jax.ShapeDtypeStruct((slots, wid...  12.7 us
    all_to_all x1, starting transfers between devices, body(): lax.all_to_all(outgoing.reshape(devices, 8, width), ('inline', 'xline'),...  11.5 us
    ppermute x4, starting transfers between devices, neighbours(): return (lax.ppermute(last, axis, up), lax.ppermute(first, axis, down))  7.22 us
    pallas_call x1, Pallas kernels, body(): pl.pallas_call(inner_kernel, out_shape=features, in_specs=[vmem] * 4, out...  3.96 us
    ppermute x4, waiting for transfers between devices, neighbours(): return (lax.ppermute(last, axis, up), lax.ppermute(first, axis, down))  2.23 us
    pallas_call x1, Pallas kernels, body(): pl.pallas_call(outer_kernel, out_shape=features, in_specs=[vmem] * 6 + [h...  2.01 us
  transfers between devices with their start and end apart: 5, of which 3 were waited for; matrix products, arithmetic and copies ran while one was open for 0% of the time, Pallas kernels for 7%

profile of v6, /device:TPU:1, one launch (start us, length us, event | category | flops | bytes accessed | tf_op | source)
XLA Modules:
  0.0 73.3 jit_solution(15049271164134793597)
XLA Ops:
  0.0 12.7 %denoise.1 = bf16[1024,1152]{1,0:T(8,128)(2,1)} custom-call(bf16[256,1024]{1,0:T(8,128)(2,1)} %refs_0_.1, s32[1,256]{1,0:T(1,128)} %bitcast.10, s32[1,256]{1,0:T(1,128)} %bitcast.11, bf16[3,32]{1,0:T(4,128)(2,1)} %bitcast.12, bf16[96,32]{1,0:T(8,128)(2,1)} %bitcast.9, bf16[1,32]{1,0:T(2,128)(2,1)} %bitcast.13), custom_call_target="tpu_custom_call" | custom-call | tf_op jit(solution)/shard_map/denoise/pallas_call | solution.py:311
  12.7 0.0 copy-start
  12.7 0.0 copy-start.1
  12.7 11.5 %all-to-all-start = ((bf16[128,8,1152]{2,1,0:T(8,128)(2,1)}), bf16[128,8,1152]{2,1,0:T(8,128)(2,1)S(1)}, u32[]{:S(2)}, u32[]{:S(2)}) async-start(bf16[128,8,1152]{2,1,0:T(8,128)(2,1)} %bitcast.8), calls=%async_computation | async-start | bytes 4718592 | tf_op jit(solution)/shard_map/all_to_all | solution.py:353
  24.3 0.0 copy-done
  24.3 0.0 copy-done.1
  24.3 1.4 %prepare.1 = (f32[328,128]{1,0:T(8,128)S(1)}, bf16[512,216]{1,0:T(8,128)(2,1)S(1)}) custom-call(s32[16,16]{1,0:T(8,128)S(1)} %copy-done, bf16[16,27]{1,0:T(8,128)(2,1)S(1)} %copy-done.1), custom_call_target="tpu_custom_call" | custom-call | tf_op jit(solution)/shard_map/prepare/pallas_call | solution.py:345
  25.7 31.0 %all-to-all-done = bf16[128,8,1152]{2,1,0:T(8,128)(2,1)S(1)} async-done(((bf16[128,8,1152]{2,1,0:T(8,128)(2,1)}), bf16[128,8,1152]{2,1,0:T(8,128)(2,1)S(1)}, u32[]{:S(2)}, u32[]{:S(2)}) %all-to-all-start) | async-done | bytes 2359328 | tf_op jit(solution)/shard_map/all_to_all | solution.py:353
  56.7 1.0 %stack.1 = (f32[9,328,128]{2,1,0:T(8,128)S(1)}, bf16[40,1152]{1,0:T(8,128)(2,1)S(1)}, bf16[40,1152]{1,0:T(8,128)(2,1)S(1)}) custom-call(bf16[1024,1152]{1,0:T(8,128)(2,1)S(1)} %bitcast.7, f32[328,128]{1,0:T(8,128)S(1)} %get-tuple-element.12.fold_ref), custom_call_target="tpu_custom_call" | custom-call | tf_op jit(solution)/shard_map/stack/pallas_call | solution.py:357
  57.7 0.7 %collective-permute-start = (bf16[40,1152]{1,0:T(8,128)(2,1)S(1)}, bf16[40,1152]{1,0:T(8,128)(2,1)S(1)}, u32[]{:S(2)}, u32[]{:S(2)}) collective-permute-start(bf16[40,1152]{1,0:T(8,128)(2,1)S(1)} %get-tuple-element.14), channel_id=1, source_target_pairs={{0,1},{1,2},{2,3},{3,4},{4,5},{5,6},{6,7},{7,8},{8,9},{9,10},{10,1... | collective-permute-start | bytes 276488 | tf_op jit(solution)/shard_map/ppermute | solution.py:299
  58.4 4.1 %collective-permute-start.1 = (bf16[40,1152]{1,0:T(8,128)(2,1)S(1)}, bf16[40,1152]{1,0:T(8,128)(2,1)S(1)}, u32[]{:S(2)}, u32[]{:S(2)}) collective-permute-start(bf16[40,1152]{1,0:T(8,128)(2,1)S(1)} %get-tuple-element.15), channel_id=1, source_target_pairs={{1,0},{2,1},{3,2},{4,3},{5,4},{6,5},{7,6},{8,7},{9,8},{10,9},{11,1... | collective-permute-start | bytes 276488 | tf_op jit(solution)/shard_map/ppermute | solution.py:299
  62.5 1.9 %collective-permute-done.left_ref = bf16[40,1152]{1,0:T(8,128)(2,1)S(1)} collective-permute-done((bf16[40,1152]{1,0:T(8,128)(2,1)S(1)}, bf16[40,1152]{1,0:T(8,128)(2,1)S(1)}, u32[]{:S(2)}, u32[]{:S(2)}) %collective-permute-start) | collective-permute-done | bytes 92192 | tf_op jit(solution)/shard_map/ppermute | solution.py:299
  64.5 0.0 collective-permute-done.1.right_ref
  64.5 0.1 edges.1
  64.5 2.4 %collective-permute-start.2 = (bf16[40,1152]{1,0:T(8,128)(2,1)S(1)}, bf16[40,1152]{1,0:T(8,128)(2,1)S(1)}, u32[]{:S(2)}, u32[]{:S(2)}) collective-permute-start(bf16[40,1152]{1,0:T(8,128)(2,1)S(1)} %get-tuple-element.16), channel_id=1, source_target_pairs={{0,16},{16,32},{32,48},{48,64},{64,80},{80,96},{96,112},{112,0},{1... | collective-permute-start | bytes 276488 | tf_op jit(solution)/shard_map/ppermute | solution.py:299
  66.9 0.0 collective-permute-start.3
  66.9 4.0 %inner.1._ = bf16[16,16,16,1024]{3,2,1,0:T(8,128)(2,1)} custom-call(f32[9,328,128]{2,1,0:T(8,128)S(1)} %get-tuple-element.13.main_ref, bf16[40,1152]{1,0:T(8,128)(2,1)S(1)} %collective-permute-done.left_ref, bf16[40,1152]{1,0:T(8,128)(2,1)S(1)} %collective-permute-done.1.right_ref, bf16[512,216]{1,0:T(8,128)(2,1)S(1)} %get-tuple-element.18.w_ref), custom_call_target="tpu_custom_call" | custom-call | flops 4294967296 | bytes 8388608 | tf_op jit(solution)/shard_map/inner/pallas_call | solution.py:386
  70.9 0.0 collective-permute-done.2.above_ref
  70.9 0.3 collective-permute-done.3.below_ref
  71.2 2.0 %outer.1 = bf16[16,16,16,1024]{3,2,1,0:T(8,128)(2,1)} custom-call(f32[9,328,128]{2,1,0:T(8,128)S(1)} %get-tuple-element.13.main_ref, bf16[40,1152]{1,0:T(8,128)(2,1)S(1)} %collective-permute-done.left_ref, bf16[40,1152]{1,0:T(8,128)(2,1)S(1)} %collective-permute-done.1.right_ref, ...), custom_call_target="tpu_custom_call", output_to_operand_aliasing={{}: (6, {})} | custom-call | tf_op jit(solution)/shard_map/outer/pallas_call | solution.py:396
Async XLA Ops:
  12.7 11.5 %copy-start = (s32[16,16]{1,0:T(8,128)S(1)}, s32[16,16]{1,0:T(8,128)}, u32[]{:S(2)}) copy-start(s32[16,16]{1,0:T(8,128)} %fold_ref.1) | copy-start | bytes 3076
  12.7 11.5 %copy-start.1 = (bf16[16,27]{1,0:T(8,128)(2,1)S(1)}, bf16[16,27]{1,0:T(8,128)(2,1)}, u32[]{:S(2)}) copy-start(bf16[16,27]{1,0:T(8,128)(2,1)} %wv_ref.1) | copy-start | bytes 2596
  12.7 44.0 %all-to-all-start = ((bf16[128,8,1152]{2,1,0:T(8,128)(2,1)}), bf16[128,8,1152]{2,1,0:T(8,128)(2,1)S(1)}, u32[]{:S(2)}, u32[]{:S(2)}) async-start(bf16[128,8,1152]{2,1,0:T(8,128)(2,1)} %bitcast.8), calls=%async_computation | async-start | bytes 4718592 | tf_op jit(solution)/shard_map/all_to_all | solution.py:353
  57.7 6.8 %collective-permute-start = (bf16[40,1152]{1,0:T(8,128)(2,1)S(1)}, bf16[40,1152]{1,0:T(8,128)(2,1)S(1)}, u32[]{:S(2)}, u32[]{:S(2)}) collective-permute-start(bf16[40,1152]{1,0:T(8,128)(2,1)S(1)} %get-tuple-element.14), channel_id=1, source_target_pairs={{0,1},{1,2},{2,3},{3,4},{4,5},{5,6},{6,7},{7,8},{8,9},{9,10},{10,1... | collective-permute-start | bytes 276488 | tf_op jit(solution)/shard_map/ppermute | solution.py:299
  58.4 6.0 %collective-permute-start.1 = (bf16[40,1152]{1,0:T(8,128)(2,1)S(1)}, bf16[40,1152]{1,0:T(8,128)(2,1)S(1)}, u32[]{:S(2)}, u32[]{:S(2)}) collective-permute-start(bf16[40,1152]{1,0:T(8,128)(2,1)S(1)} %get-tuple-element.15), channel_id=1, source_target_pairs={{1,0},{2,1},{3,2},{4,3},{5,4},{6,5},{7,6},{8,7},{9,8},{10,9},{11,1... | collective-permute-start | bytes 276488 | tf_op jit(solution)/shard_map/ppermute | solution.py:299
  64.5 6.3 %collective-permute-start.2 = (bf16[40,1152]{1,0:T(8,128)(2,1)S(1)}, bf16[40,1152]{1,0:T(8,128)(2,1)S(1)}, u32[]{:S(2)}, u32[]{:S(2)}) collective-permute-start(bf16[40,1152]{1,0:T(8,128)(2,1)S(1)} %get-tuple-element.16), channel_id=1, source_target_pairs={{0,16},{16,32},{32,48},{48,64},{64,80},{80,96},{96,112},{112,0},{1... | collective-permute-start | bytes 276488 | tf_op jit(solution)/shard_map/ppermute | solution.py:299
  66.9 4.3 %collective-permute-start.3 = (bf16[40,1152]{1,0:T(8,128)(2,1)S(1)}, bf16[40,1152]{1,0:T(8,128)(2,1)S(1)}, u32[]{:S(2)}, u32[]{:S(2)}) collective-permute-start(bf16[40,1152]{1,0:T(8,128)(2,1)S(1)} %get-tuple-element.17), channel_id=1, source_target_pairs={{16,0},{32,16},{48,32},{64,48},{80,64},{96,80},{112,96},{0,112},{1... | collective-permute-start | bytes 276488 | tf_op jit(solution)/shard_map/ppermute | solution.py:299

commit v7 on v6

--- a/solution.py
+++ b/solution.py
@@ -178,27 +178,40 @@
     w_out[...] = total.astype(BF16)
 
 
-def stack_kernel(recv_ref, fold_ref, main_ref, left_ref, right_ref):
+def bins_of(recv_ref):
+    tail = recv_ref[:, recv_ref.shape[1] - TAIL :].astype(F32).T
+    return ((tail[0:1] - 1.0) * SIDE + (tail[1:2] - 1.0)).astype(jnp.int32)
+
+
+def sides_kernel(recv_ref, fold_ref, left_ref, right_ref):
+    slots, width = recv_ref.shape
+    row = iota((2 * STRIP, slots), 0)
+    at = row % STRIP
+    wanted_bin = at % SIDE * SIDE + at // SIDE + row // STRIP * 16
+    wanted_bin = jnp.where(at < EDGE, wanted_bin, -1000)
+    select = picks((2 * STRIP, slots), wanted_bin, bins_of(recv_ref))
+    at = lax.axis_index("xline")
+    sides = ((left_ref, 0, at > 0), (right_ref, 16, at < lax.axis_size("xline") - 1))
+    for c in range(0, width - TAIL, 256):
+        part = jnp.dot(select, recv_ref[:, c : c + 256], preferred_element_type=F32)
+        for k, (ref, _, wanted) in enumerate(sides):
+            ref[:, c : c + 256] = jnp.where(wanted, part[STRIP * k : STRIP * (k + 1)], 0.0).astype(BF16)
+    pad = jnp.zeros((STRIP - EDGE, TAIL), F32)
+    for ref, first, wanted in sides:
+        cols = [fold_ref[pl.ds(first + k, SIDE, stride=SIDE), :] for k in range(2)]
+        strip = jnp.concatenate([cols[0], cols[1], pad], axis=0)
+        ref[:, width - TAIL :] = jnp.where(wanted, strip, 0.0).astype(BF16)
+
+
+def stack_kernel(recv_ref, fold_ref, main_ref):
     slots = recv_ref.shape[0]
     blocks, bins, _ = main_ref.shape
-    samples = recv_ref.shape[1] - TAIL
-    tail = recv_ref[:, samples:].astype(F32).T
-    place = ((tail[0:1] - 1.0) * SIDE + (tail[1:2] - 1.0)).astype(jnp.int32)
-    select = picks((bins, slots), iota((bins, slots), 0), place)
+    select = picks((bins, slots), iota((bins, slots), 0), bins_of(recv_ref))
     for c in range(0, blocks - 1, 2):
         both = jnp.dot(select, recv_ref[:, 128 * c : 128 * (c + 2)], preferred_element_type=F32)
         main_ref[c] = both[:, :128]
         main_ref[c + 1] = both[:, 128:]
     main_ref[blocks - 1] = fold_ref[...]
-    pad = jnp.zeros((STRIP - EDGE, 128), F32)
-    at = lax.axis_index("xline")
-    sides = ((left_ref, 0, at > 0), (right_ref, 16, at < lax.axis_size("xline") - 1))
-    for c in range(blocks):
-        lanes = slice(128 * c, 128 * (c + 1))
-        for ref, first, wanted in sides:
-            cols = [main_ref[c, pl.ds(first + k, SIDE, stride=SIDE), :] for k in range(2)]
-            strip = jnp.concatenate([cols[0], cols[1], pad], axis=0)
-            ref[:, lanes] = jnp.where(wanted, strip, 0.0).astype(BF16)
 
 
 def edges_kernel(main_ref, left_ref, right_ref, up_ref, down_ref, up, down):
@@ -244,30 +257,33 @@
     vs[2, start:stop, :] = jnp.where(lane == samples - 1, 0.0, pltpu.roll(v, samples - 1, 1))
 
 
-def convolve(m, vs, w_ref, block):
+def convolve(m, vs, w_ref, block, out_hbm, sem, width):
     taps = jnp.concatenate([vs[dt, EDGE * m : EDGE * (m + 2), :] for dt in range(3)], axis=0).astype(BF16)
+    stores = []
     for c in range(0, vs.shape[2], 256):
         part = jnp.dot(w_ref[...], taps[:, c : c + 256], preferred_element_type=F32)
         block[:, :, :, c : c + 256] = part.astype(BF16).reshape(2, 16, 16, 256)
+        if (c + 256) % width == 0:
+            lanes = pl.ds(c + 256 - width, width)
+            store = pltpu.make_async_copy(
+                block.at[:, :, :, lanes], out_hbm.at[pl.ds(2 * m, 2), :, :, lanes], sem.at[len(stores)]
+            )
+            store.start()
+            stores.append(store)
+    return stores
 
 
 def inner_kernel(main_ref, left_ref, right_ref, w_ref, out_hbm, acc, vs, out, sems):
     acc[...] = main_ref[...]
     add_sides(acc, left_ref, right_ref, 2, 14)
-    slots = out.shape[0]
     stores = []
     ends = [EDGE // 8 * 8] + [-(-EDGE * (m + 2) // 8) * 8 for m in range(1, 7)]
     make_taps(acc, vs, ends[0], ends[1])
     for k in range(6):
-        if k >= slots:
-            stores[k - slots].wait()
         if k < 5:
             make_taps(acc, vs, ends[k + 1], ends[k + 2])
-        convolve(k + 1, vs, w_ref, out.at[k % slots])
-        store = pltpu.make_async_copy(out.at[k % slots], out_hbm.at[pl.ds(2 * k + 2, 2)], sems.at[k % slots])
-        store.start()
-        stores.append(store)
-    for store in stores[6 - slots :]:
+        stores += convolve(k + 1, vs, w_ref, out.at[k], out_hbm, sems.at[k], 1024 if k < 5 else 512)
+    for store in stores:
         store.wait()
 
 
@@ -280,14 +296,11 @@
         acc[c, bottom:bins, :] = main_ref[c, bottom:bins, :]
         acc[c, 0:STRIP, :] += above_ref[:, lanes].astype(F32)
         acc[c, bins - STRIP : bins, :] += below_ref[:, lanes].astype(F32)
-    stores = []
-    for k, (m, start, stop, row) in enumerate(((0, 0, top, 0), (7, bottom, bins, 14))):
+    for start, stop, row in ((0, top, 0), (bottom, bins, 14)):
         add_sides(acc, left_ref, right_ref, row, 4)
         make_taps(acc, vs, start, stop)
-        convolve(m, vs, w_ref, out.at[k])
-        store = pltpu.make_async_copy(out.at[k], out_hbm.at[pl.ds(2 * m, 2)], sems.at[k])
-        store.start()
-        stores.append(store)
+    stores = convolve(0, vs, w_ref, out.at[0], out_hbm, sems.at[0], 512)
+    stores += convolve(7, vs, w_ref, out.at[1], out_hbm, sems.at[1], 512)
     for store in stores:
         store.wait()
 
@@ -354,15 +367,24 @@
         outgoing.reshape(devices, 8, width), ("inline", "xline"), split_axis=0, concat_axis=0, tiled=True
     ).reshape(slots, width)
     edge = jax.ShapeDtypeStruct((STRIP, width), BF16)
-    main, left, right = pl.pallas_call(
+    left, right = pl.pallas_call(
+        sides_kernel,
+        out_shape=[edge, edge],
+        in_specs=[vmem] * 2,
+        out_specs=[vmem] * 2,
+        compiler_params=params,
+        name="sides",
+    )(received, folds)
+    from_left, from_right = neighbours(left, right, "xline")
+    main = pl.pallas_call(
         stack_kernel,
-        out_shape=[jax.ShapeDtypeStruct((width // 128, bins, 128), F32), edge, edge],
+        out_shape=jax.ShapeDtypeStruct((width // 128, bins, 128), F32),
         in_specs=[vmem] * 2,
-        out_specs=[vmem] * 3,
-        compiler_params=params,
+        out_specs=vmem,
+        compiler_params=params,
+        cost_estimate=pl.CostEstimate(flops=1 << 30, transcendentals=0, bytes_accessed=4 << 20),
         name="stack",
     )(received, folds)
-    from_left, from_right = neighbours(left, right, "xline")
     up, down = pl.pallas_call(
         edges_kernel,
         out_shape=[edge, edge],
@@ -379,7 +401,7 @@
             pltpu.VMEM((width // 128, bins, 128), F32),
             pltpu.VMEM((3, bins, samples), F32),
             pltpu.VMEM((slots, 2, 16, 16, samples), BF16),
-            pltpu.SemaphoreType.DMA((slots,)),
+            pltpu.SemaphoreType.DMA((slots, samples // 256)),
         ]
 
     features = jax.ShapeDtypeStruct((16, 16, 16, samples), BF16)
@@ -388,7 +410,7 @@
         out_shape=features,
         in_specs=[vmem] * 4,
         out_specs=hbm,
-        scratch_shapes=scratch(3),
+        scratch_shapes=scratch(6),
         compiler_params=params,
         cost_estimate=pl.CostEstimate(flops=1 << 32, transcendentals=0, bytes_accessed=8 << 20),
         name="inner",

time: 74.7 us -> 73.8 us (0.988)
  transfers between devices with their start and end apart: 5 -> 5, of which waited for: 3 -> 3; matrix products, arithmetic and copies ran while one was open for 0% -> 0% of each run, Pallas kernels for 7% -> 8%
where the time goes in v7:
time: 73.8 us; the launch traced here: 72.8 us
  waiting for transfers between devices  32.7 us (44%)
  Pallas kernels  21.1 us (29%)
  starting transfers between devices  18.7 us (25%)
    all_to_all x1, waiting for transfers between devices, body(): lax.all_to_all(outgoing.reshape(devices, 8, width), ('inline', 'xline'),...  31 us
    pallas_call x1, Pallas kernels, body(): pl.pallas_call(denoise_kernel, out_shape=jax.ShapeDtypeStruct((slots, wid...  12.7 us
    all_to_all x1, starting transfers between devices, body(): lax.all_to_all(outgoing.reshape(devices, 8, width), ('inline', 'xline'),...  11.5 us
    ppermute x4, starting transfers between devices, neighbours(): return (lax.ppermute(last, axis, up), lax.ppermute(first, axis, down))  7.22 us
    pallas_call x1, Pallas kernels, body(): pl.pallas_call(inner_kernel, out_shape=features, in_specs=[vmem] * 4, out...  3.55 us
    pallas_call x1, Pallas kernels, body(): pl.pallas_call(outer_kernel, out_shape=features, in_specs=[vmem] * 6 + [h...  1.92 us
    ppermute x4, waiting for transfers between devices, neighbours(): return (lax.ppermute(last, axis, up), lax.ppermute(first, axis, down))  1.71 us
  transfers between devices with their start and end apart: 5, of which 3 were waited for; matrix products, arithmetic and copies ran while one was open for 0% of the time, Pallas kernels for 8%

profile of v7, /device:TPU:1, one launch (start us, length us, event | category | flops | bytes accessed | tf_op | source)
XLA Modules:
  0.0 72.8 jit_solution(3151587642976159393)
XLA Ops:
  0.0 12.7 %denoise.1 = bf16[1024,1152]{1,0:T(8,128)(2,1)} custom-call(bf16[256,1024]{1,0:T(8,128)(2,1)} %refs_0_.1, s32[1,256]{1,0:T(1,128)} %bitcast.11, s32[1,256]{1,0:T(1,128)} %bitcast.12, bf16[3,32]{1,0:T(4,128)(2,1)} %bitcast.13, bf16[96,32]{1,0:T(8,128)(2,1)} %bitcast.10, bf16[1,32]{1,0:T(2,128)(2,1)} %bitcast.14), custom_call_target="tpu_custom_call" | custom-call | tf_op jit(solution)/shard_map/denoise/pallas_call | solution.py:324
  12.7 0.0 copy-start
  12.7 0.0 copy-start.1
  12.7 11.5 %all-to-all-start = ((bf16[128,8,1152]{2,1,0:T(8,128)(2,1)}), bf16[128,8,1152]{2,1,0:T(8,128)(2,1)S(1)}, u32[]{:S(2)}, u32[]{:S(2)}) async-start(bf16[128,8,1152]{2,1,0:T(8,128)(2,1)} %bitcast.9), calls=%async_computation | async-start | bytes 4718592 | tf_op jit(solution)/shard_map/all_to_all | solution.py:366
  24.3 0.0 copy-done
  24.3 0.0 copy-done.1
  24.3 1.4 %prepare.1 = (f32[328,128]{1,0:T(8,128)S(1)}, bf16[512,216]{1,0:T(8,128)(2,1)S(1)}) custom-call(s32[16,16]{1,0:T(8,128)S(1)} %copy-done, bf16[16,27]{1,0:T(8,128)(2,1)S(1)} %copy-done.1), custom_call_target="tpu_custom_call" | custom-call | tf_op jit(solution)/shard_map/prepare/pallas_call | solution.py:358
  25.7 31.0 %all-to-all-done = bf16[128,8,1152]{2,1,0:T(8,128)(2,1)S(1)} async-done(((bf16[128,8,1152]{2,1,0:T(8,128)(2,1)}), bf16[128,8,1152]{2,1,0:T(8,128)(2,1)S(1)}, u32[]{:S(2)}, u32[]{:S(2)}) %all-to-all-start) | async-done | bytes 2359328 | tf_op jit(solution)/shard_map/all_to_all | solution.py:366
  56.7 0.5 sides.1
  57.2 0.7 %collective-permute-start = (bf16[40,1152]{1,0:T(8,128)(2,1)S(1)}, bf16[40,1152]{1,0:T(8,128)(2,1)S(1)}, u32[]{:S(2)}, u32[]{:S(2)}) collective-permute-start(bf16[40,1152]{1,0:T(8,128)(2,1)S(1)} %get-tuple-element.12), channel_id=1, source_target_pairs={{0,1},{1,2},{2,3},{3,4},{4,5},{5,6},{6,7},{7,8},{8,9},{9,10},{10,1... | collective-permute-start | bytes 276488 | tf_op jit(solution)/shard_map/ppermute | solution.py:312
  58.0 4.1 %collective-permute-start.1 = (bf16[40,1152]{1,0:T(8,128)(2,1)S(1)}, bf16[40,1152]{1,0:T(8,128)(2,1)S(1)}, u32[]{:S(2)}, u32[]{:S(2)}) collective-permute-start(bf16[40,1152]{1,0:T(8,128)(2,1)S(1)} %get-tuple-element.13), channel_id=1, source_target_pairs={{1,0},{2,1},{3,2},{4,3},{5,4},{6,5},{7,6},{8,7},{9,8},{10,9},{11,1... | collective-permute-start | bytes 276488 | tf_op jit(solution)/shard_map/ppermute | solution.py:312
  62.1 0.9 %stack.1.main_ref = f32[9,328,128]{2,1,0:T(8,128)S(1)} custom-call(bf16[1024,1152]{1,0:T(8,128)(2,1)S(1)} %bitcast.8, f32[328,128]{1,0:T(8,128)S(1)} %get-tuple-element.11.fold_ref), custom_call_target="tpu_custom_call" | custom-call | flops 1073741824 | bytes 4194304 | tf_op jit(solution)/shard_map/stack/pallas_call | solution.py:379
  63.0 1.0 %collective-permute-done.left_ref = bf16[40,1152]{1,0:T(8,128)(2,1)S(1)} collective-permute-done((bf16[40,1152]{1,0:T(8,128)(2,1)S(1)}, bf16[40,1152]{1,0:T(8,128)(2,1)S(1)}, u32[]{:S(2)}, u32[]{:S(2)}) %collective-permute-start) | collective-permute-done | bytes 92192 | tf_op jit(solution)/shard_map/ppermute | solution.py:312
  64.0 0.0 collective-permute-done.1.right_ref
  64.0 0.1 edges.1
  64.1 2.4 %collective-permute-start.2 = (bf16[40,1152]{1,0:T(8,128)(2,1)S(1)}, bf16[40,1152]{1,0:T(8,128)(2,1)S(1)}, u32[]{:S(2)}, u32[]{:S(2)}) collective-permute-start(bf16[40,1152]{1,0:T(8,128)(2,1)S(1)} %get-tuple-element.14), channel_id=1, source_target_pairs={{0,16},{16,32},{32,48},{48,64},{64,80},{80,96},{96,112},{112,0},{1... | collective-permute-start | bytes 276488 | tf_op jit(solution)/shard_map/ppermute | solution.py:312
  66.5 0.0 collective-permute-start.3
  66.5 3.6 %inner.1._ = bf16[16,16,16,1024]{3,2,1,0:T(8,128)(2,1)} custom-call(f32[9,328,128]{2,1,0:T(8,128)S(1)} %stack.1.main_ref, bf16[40,1152]{1,0:T(8,128)(2,1)S(1)} %collective-permute-done.left_ref, bf16[40,1152]{1,0:T(8,128)(2,1)S(1)} %collective-permute-done.1.right_ref, bf16[512,216]{1,0:T(8,128)(2,1)S(1)} %get-tuple-element.16.w_ref), custom_call_target="tpu_custom_call" | custom-call | flops 4294967296 | bytes 8388608 | tf_op jit(solution)/shard_map/inner/pallas_call | solution.py:408
  70.0 0.0 collective-permute-done.2.above_ref
  70.0 0.7 collective-permute-done.3.below_ref
  70.7 1.9 %outer.1 = bf16[16,16,16,1024]{3,2,1,0:T(8,128)(2,1)} custom-call(f32[9,328,128]{2,1,0:T(8,128)S(1)} %stack.1.main_ref, bf16[40,1152]{1,0:T(8,128)(2,1)S(1)} %collective-permute-done.left_ref, bf16[40,1152]{1,0:T(8,128)(2,1)S(1)} %collective-permute-done.1.right_ref, ...), custom_call_target="tpu_custom_call", output_to_operand_aliasing={{}: (6, {})} | custom-call | tf_op jit(solution)/shard_map/outer/pallas_call | solution.py:418
Async XLA Ops:
  12.7 11.5 %copy-start = (s32[16,16]{1,0:T(8,128)S(1)}, s32[16,16]{1,0:T(8,128)}, u32[]{:S(2)}) copy-start(s32[16,16]{1,0:T(8,128)} %fold_ref.1) | copy-start | bytes 3076
  12.7 11.5 %copy-start.1 = (bf16[16,27]{1,0:T(8,128)(2,1)S(1)}, bf16[16,27]{1,0:T(8,128)(2,1)}, u32[]{:S(2)}) copy-start(bf16[16,27]{1,0:T(8,128)(2,1)} %wv_ref.1) | copy-start | bytes 2596
  12.7 44.0 %all-to-all-start = ((bf16[128,8,1152]{2,1,0:T(8,128)(2,1)}), bf16[128,8,1152]{2,1,0:T(8,128)(2,1)S(1)}, u32[]{:S(2)}, u32[]{:S(2)}) async-start(bf16[128,8,1152]{2,1,0:T(8,128)(2,1)} %bitcast.9), calls=%async_computation | async-start | bytes 4718592 | tf_op jit(solution)/shard_map/all_to_all | solution.py:366
  57.2 6.8 %collective-permute-start = (bf16[40,1152]{1,0:T(8,128)(2,1)S(1)}, bf16[40,1152]{1,0:T(8,128)(2,1)S(1)}, u32[]{:S(2)}, u32[]{:S(2)}) collective-permute-start(bf16[40,1152]{1,0:T(8,128)(2,1)S(1)} %get-tuple-element.12), channel_id=1, source_target_pairs={{0,1},{1,2},{2,3},{3,4},{4,5},{5,6},{6,7},{7,8},{8,9},{9,10},{10,1... | collective-permute-start | bytes 276488 | tf_op jit(solution)/shard_map/ppermute | solution.py:312
  58.0 6.0 %collective-permute-start.1 = (bf16[40,1152]{1,0:T(8,128)(2,1)S(1)}, bf16[40,1152]{1,0:T(8,128)(2,1)S(1)}, u32[]{:S(2)}, u32[]{:S(2)}) collective-permute-start(bf16[40,1152]{1,0:T(8,128)(2,1)S(1)} %get-tuple-element.13), channel_id=1, source_target_pairs={{1,0},{2,1},{3,2},{4,3},{5,4},{6,5},{7,6},{8,7},{9,8},{10,9},{11,1... | collective-permute-start | bytes 276488 | tf_op jit(solution)/shard_map/ppermute | solution.py:312
  64.1 5.9 %collective-permute-start.2 = (bf16[40,1152]{1,0:T(8,128)(2,1)S(1)}, bf16[40,1152]{1,0:T(8,128)(2,1)S(1)}, u32[]{:S(2)}, u32[]{:S(2)}) collective-permute-start(bf16[40,1152]{1,0:T(8,128)(2,1)S(1)} %get-tuple-element.14), channel_id=1, source_target_pairs={{0,16},{16,32},{32,48},{48,64},{64,80},{80,96},{96,112},{112,0},{1... | collective-permute-start | bytes 276488 | tf_op jit(solution)/shard_map/ppermute | solution.py:312
  66.5 4.3 %collective-permute-start.3 = (bf16[40,1152]{1,0:T(8,128)(2,1)S(1)}, bf16[40,1152]{1,0:T(8,128)(2,1)S(1)}, u32[]{:S(2)}, u32[]{:S(2)}) collective-permute-start(bf16[40,1152]{1,0:T(8,128)(2,1)S(1)} %get-tuple-element.15), channel_id=1, source_target_pairs={{16,0},{32,16},{48,32},{64,48},{80,64},{96,80},{112,96},{0,112},{1... | collective-permute-start | bytes 276488 | tf_op jit(solution)/shard_map/ppermute | solution.py:312

commit v8 on v7

--- a/solution.py
+++ b/solution.py
@@ -31,7 +31,7 @@
 
 def denoise_kernel(*refs):
     ins, out_hbm, bufs = refs[:6], refs[6], refs[7:13]
-    xt, dt, ha, hb, w1, w2, wn, out_ref, in_sems, out_sems = refs[13:]
+    xt, dt, ha, hb, w1, w2, wn, wv, out_ref, in_sems, out_sems = refs[13:]
     x_ref, own_ref, bins_ref, wf_ref, ws_ref, wn_ref = bufs
     loads = [pltpu.make_async_copy(src, dst, in_sems.at[k]) for k, (src, dst) in enumerate(zip(ins, bufs))]
     for load in loads:
@@ -64,6 +64,8 @@
 
     wf = wf_ref[...].astype(F32)
     taps = [jnp.broadcast_to(column(wf[k : k + 1], 32), (32, 32)) for k in range(3)]
+    for k in range(3):
+        wv[k] = jnp.broadcast_to(taps[k][:, 0:1], (32, traces))
     lane = iota((32, 32), 1)
     for p in range(4):
         for u in range(6):
@@ -96,9 +98,17 @@
         return jnp.maximum(value.astype(BF16), jnp.zeros((), BF16))
 
     def hidden(j, h_ref, before):
-        xs = xt[PAD + WIN * j : PAD + WIN * j + 32, :].astype(BF16)
+        first = PAD + WIN * j
+        xs = xt[first : first + 32, :].astype(BF16)
         for p in range(4):
             h_ref[p, 0:64, :] = before[p, 192:256, :]
+        for u in range(6):
+            at = first + 4 * u + 3
+            value = wv[0] * xt[at : at + 1, :]
+            for k in range(1, 3):
+                value = value + wv[k] * xt[at + k : at + k + 1, :]
+            h_ref[0, 64 + 32 * u : 96 + 32 * u, :] = relu(value)
+        for p in range(1, 4):
             h_ref[p, 64:256, :] = relu(
                 jnp.dot(w1[192 * p : 192 * (p + 1), :], xs, preferred_element_type=F32)
             )
@@ -142,9 +152,12 @@
                 this[p, inside:, :] = jnp.zeros((256 - inside, traces), BF16)
         second(j, this)
         ready = min(WIN * (j + 1), samples)
-        while placed < samples and placed + 256 <= ready:
-            place(placed, 256, dt[placed : placed + 256, :].astype(BF16))
-            placed += 256
+        while placed < samples:
+            size = 128 if placed >= samples - 256 else 256
+            if placed + size > ready:
+                break
+            place(placed, size, dt[placed : placed + size, :].astype(BF16))
+            placed += size
     for store in stores:
         store.wait()
 
@@ -340,9 +353,10 @@
             pltpu.VMEM((768, 32), BF16),
             pltpu.VMEM((192, 256), BF16),
             pltpu.VMEM((64, count), F32),
+            pltpu.VMEM((3, 32, count), F32),
             pltpu.VMEM((slots, width), BF16),
             pltpu.SemaphoreType.DMA((6,)),
-            pltpu.SemaphoreType.DMA((samples // 256 + 1,)),
+            pltpu.SemaphoreType.DMA((samples // 256 + 2,)),
         ],
         compiler_params=pltpu.CompilerParams(vmem_limit_bytes=60 << 20),
         name="denoise",

time: 73.8 us -> 73.1 us (level)
    pallas_call x1, Pallas kernels: 12.7 us -> 12 us  [body(): pl.pallas_call(denoise_kernel, out_shape=jax.ShapeDtypeStruct((slots, wid...]
where the time goes in v8:
time: 73.1 us; the launch traced here: 72.1 us
  waiting for transfers between devices  32.7 us (45%)
  Pallas kernels  20.4 us (28%)
  starting transfers between devices  18.7 us (26%)
    all_to_all x1, waiting for transfers between devices, body(): lax.all_to_all(outgoing.reshape(devices, 8, width), ('inline', 'xline'),...  31 us
    pallas_call x1, Pallas kernels, body(): pl.pallas_call(denoise_kernel, out_shape=jax.ShapeDtypeStruct((slots, wid...  12 us
    all_to_all x1, starting transfers between devices, body(): lax.all_to_all(outgoing.reshape(devices, 8, width), ('inline', 'xline'),...  11.5 us
    ppermute x4, starting transfers between devices, neighbours(): return (lax.ppermute(last, axis, up), lax.ppermute(first, axis, down))  7.21 us
    pallas_call x1, Pallas kernels, body(): pl.pallas_call(inner_kernel, out_shape=features, in_specs=[vmem] * 4, out...  3.55 us
    pallas_call x1, Pallas kernels, body(): pl.pallas_call(outer_kernel, out_shape=features, in_specs=[vmem] * 6 + [h...  1.92 us
    ppermute x4, waiting for transfers between devices, neighbours(): return (lax.ppermute(last, axis, up), lax.ppermute(first, axis, down))  1.71 us
  transfers between devices with their start and end apart: 5, of which 3 were waited for; matrix products, arithmetic and copies ran while one was open for 0% of the time, Pallas kernels for 8%

profile of v8, /device:TPU:1, one launch (start us, length us, event | category | flops | bytes accessed | tf_op | source)
XLA Modules:
  0.0 72.1 jit_solution(718414006679519526)
XLA Ops:
  0.0 12.0 %denoise.1 = bf16[1024,1152]{1,0:T(8,128)(2,1)} custom-call(bf16[256,1024]{1,0:T(8,128)(2,1)} %refs_0_.1, s32[1,256]{1,0:T(1,128)} %bitcast.11, s32[1,256]{1,0:T(1,128)} %bitcast.12, bf16[3,32]{1,0:T(4,128)(2,1)} %bitcast.13, bf16[96,32]{1,0:T(8,128)(2,1)} %bitcast.10, bf16[1,32]{1,0:T(2,128)(2,1)} %bitcast.14), custom_call_target="tpu_custom_call" | custom-call | tf_op jit(solution)/shard_map/denoise/pallas_call | solution.py:337
  12.0 0.0 copy-start
  12.0 0.0 copy-start.1
  12.0 11.5 %all-to-all-start = ((bf16[128,8,1152]{2,1,0:T(8,128)(2,1)}), bf16[128,8,1152]{2,1,0:T(8,128)(2,1)S(1)}, u32[]{:S(2)}, u32[]{:S(2)}) async-start(bf16[128,8,1152]{2,1,0:T(8,128)(2,1)} %bitcast.9), calls=%async_computation | async-start | bytes 4718592 | tf_op jit(solution)/shard_map/all_to_all | solution.py:380
  23.5 0.0 copy-done
  23.5 0.0 copy-done.1
  23.5 1.4 %prepare.1 = (f32[328,128]{1,0:T(8,128)S(1)}, bf16[512,216]{1,0:T(8,128)(2,1)S(1)}) custom-call(s32[16,16]{1,0:T(8,128)S(1)} %copy-done, bf16[16,27]{1,0:T(8,128)(2,1)S(1)} %copy-done.1), custom_call_target="tpu_custom_call" | custom-call | tf_op jit(solution)/shard_map/prepare/pallas_call | solution.py:372
  24.9 31.0 %all-to-all-done = bf16[128,8,1152]{2,1,0:T(8,128)(2,1)S(1)} async-done(((bf16[128,8,1152]{2,1,0:T(8,128)(2,1)}), bf16[128,8,1152]{2,1,0:T(8,128)(2,1)S(1)}, u32[]{:S(2)}, u32[]{:S(2)}) %all-to-all-start) | async-done | bytes 2359328 | tf_op jit(solution)/shard_map/all_to_all | solution.py:380
  56.0 0.5 sides.1
  56.5 0.7 %collective-permute-start = (bf16[40,1152]{1,0:T(8,128)(2,1)S(1)}, bf16[40,1152]{1,0:T(8,128)(2,1)S(1)}, u32[]{:S(2)}, u32[]{:S(2)}) collective-permute-start(bf16[40,1152]{1,0:T(8,128)(2,1)S(1)} %get-tuple-element.12), channel_id=1, source_target_pairs={{0,1},{1,2},{2,3},{3,4},{4,5},{5,6},{6,7},{7,8},{8,9},{9,10},{10,1... | collective-permute-start | bytes 276488 | tf_op jit(solution)/shard_map/ppermute | solution.py:325
  57.2 4.1 %collective-permute-start.1 = (bf16[40,1152]{1,0:T(8,128)(2,1)S(1)}, bf16[40,1152]{1,0:T(8,128)(2,1)S(1)}, u32[]{:S(2)}, u32[]{:S(2)}) collective-permute-start(bf16[40,1152]{1,0:T(8,128)(2,1)S(1)} %get-tuple-element.13), channel_id=1, source_target_pairs={{1,0},{2,1},{3,2},{4,3},{5,4},{6,5},{7,6},{8,7},{9,8},{10,9},{11,1... | collective-permute-start | bytes 276488 | tf_op jit(solution)/shard_map/ppermute | solution.py:325
  61.4 0.9 %stack.1.main_ref = f32[9,328,128]{2,1,0:T(8,128)S(1)} custom-call(bf16[1024,1152]{1,0:T(8,128)(2,1)S(1)} %bitcast.8, f32[328,128]{1,0:T(8,128)S(1)} %get-tuple-element.11.fold_ref), custom_call_target="tpu_custom_call" | custom-call | flops 1073741824 | bytes 4194304 | tf_op jit(solution)/shard_map/stack/pallas_call | solution.py:393
  62.3 1.0 %collective-permute-done.left_ref = bf16[40,1152]{1,0:T(8,128)(2,1)S(1)} collective-permute-done((bf16[40,1152]{1,0:T(8,128)(2,1)S(1)}, bf16[40,1152]{1,0:T(8,128)(2,1)S(1)}, u32[]{:S(2)}, u32[]{:S(2)}) %collective-permute-start) | collective-permute-done | bytes 92192 | tf_op jit(solution)/shard_map/ppermute | solution.py:325
  63.3 0.0 collective-permute-done.1.right_ref
  63.3 0.1 edges.1
  63.4 2.4 %collective-permute-start.2 = (bf16[40,1152]{1,0:T(8,128)(2,1)S(1)}, bf16[40,1152]{1,0:T(8,128)(2,1)S(1)}, u32[]{:S(2)}, u32[]{:S(2)}) collective-permute-start(bf16[40,1152]{1,0:T(8,128)(2,1)S(1)} %get-tuple-element.14), channel_id=1, source_target_pairs={{0,16},{16,32},{32,48},{48,64},{64,80},{80,96},{96,112},{112,0},{1... | collective-permute-start | bytes 276488 | tf_op jit(solution)/shard_map/ppermute | solution.py:325
  65.7 0.0 collective-permute-start.3
  65.7 3.6 %inner.1._ = bf16[16,16,16,1024]{3,2,1,0:T(8,128)(2,1)} custom-call(f32[9,328,128]{2,1,0:T(8,128)S(1)} %stack.1.main_ref, bf16[40,1152]{1,0:T(8,128)(2,1)S(1)} %collective-permute-done.left_ref, bf16[40,1152]{1,0:T(8,128)(2,1)S(1)} %collective-permute-done.1.right_ref, bf16[512,216]{1,0:T(8,128)(2,1)S(1)} %get-tuple-element.16.w_ref), custom_call_target="tpu_custom_call" | custom-call | flops 4294967296 | bytes 8388608 | tf_op jit(solution)/shard_map/inner/pallas_call | solution.py:422
  69.3 0.0 collective-permute-done.2.above_ref
  69.3 0.7 collective-permute-done.3.below_ref
  70.0 1.9 %outer.1 = bf16[16,16,16,1024]{3,2,1,0:T(8,128)(2,1)} custom-call(f32[9,328,128]{2,1,0:T(8,128)S(1)} %stack.1.main_ref, bf16[40,1152]{1,0:T(8,128)(2,1)S(1)} %collective-permute-done.left_ref, bf16[40,1152]{1,0:T(8,128)(2,1)S(1)} %collective-permute-done.1.right_ref, ...), custom_call_target="tpu_custom_call", output_to_operand_aliasing={{}: (6, {})} | custom-call | tf_op jit(solution)/shard_map/outer/pallas_call | solution.py:432
Async XLA Ops:
  12.0 11.6 %copy-start = (s32[16,16]{1,0:T(8,128)S(1)}, s32[16,16]{1,0:T(8,128)}, u32[]{:S(2)}) copy-start(s32[16,16]{1,0:T(8,128)} %fold_ref.1) | copy-start | bytes 3076
  12.0 11.5 %copy-start.1 = (bf16[16,27]{1,0:T(8,128)(2,1)S(1)}, bf16[16,27]{1,0:T(8,128)(2,1)}, u32[]{:S(2)}) copy-start(bf16[16,27]{1,0:T(8,128)(2,1)} %wv_ref.1) | copy-start | bytes 2596
  12.0 44.0 %all-to-all-start = ((bf16[128,8,1152]{2,1,0:T(8,128)(2,1)}), bf16[128,8,1152]{2,1,0:T(8,128)(2,1)S(1)}, u32[]{:S(2)}, u32[]{:S(2)}) async-start(bf16[128,8,1152]{2,1,0:T(8,128)(2,1)} %bitcast.9), calls=%async_computation | async-start | bytes 4718592 | tf_op jit(solution)/shard_map/all_to_all | solution.py:380
  56.5 6.8 %collective-permute-start = (bf16[40,1152]{1,0:T(8,128)(2,1)S(1)}, bf16[40,1152]{1,0:T(8,128)(2,1)S(1)}, u32[]{:S(2)}, u32[]{:S(2)}) collective-permute-start(bf16[40,1152]{1,0:T(8,128)(2,1)S(1)} %get-tuple-element.12), channel_id=1, source_target_pairs={{0,1},{1,2},{2,3},{3,4},{4,5},{5,6},{6,7},{7,8},{8,9},{9,10},{10,1... | collective-permute-start | bytes 276488 | tf_op jit(solution)/shard_map/ppermute | solution.py:325
  57.2 6.0 %collective-permute-start.1 = (bf16[40,1152]{1,0:T(8,128)(2,1)S(1)}, bf16[40,1152]{1,0:T(8,128)(2,1)S(1)}, u32[]{:S(2)}, u32[]{:S(2)}) collective-permute-start(bf16[40,1152]{1,0:T(8,128)(2,1)S(1)} %get-tuple-element.13), channel_id=1, source_target_pairs={{1,0},{2,1},{3,2},{4,3},{5,4},{6,5},{7,6},{8,7},{9,8},{10,9},{11,1... | collective-permute-start | bytes 276488 | tf_op jit(solution)/shard_map/ppermute | solution.py:325
  63.4 5.9 %collective-permute-start.2 = (bf16[40,1152]{1,0:T(8,128)(2,1)S(1)}, bf16[40,1152]{1,0:T(8,128)(2,1)S(1)}, u32[]{:S(2)}, u32[]{:S(2)}) collective-permute-start(bf16[40,1152]{1,0:T(8,128)(2,1)S(1)} %get-tuple-element.14), channel_id=1, source_target_pairs={{0,16},{16,32},{32,48},{48,64},{64,80},{80,96},{96,112},{112,0},{1... | collective-permute-start | bytes 276488 | tf_op jit(solution)/shard_map/ppermute | solution.py:325
  65.7 4.3 %collective-permute-start.3 = (bf16[40,1152]{1,0:T(8,128)(2,1)S(1)}, bf16[40,1152]{1,0:T(8,128)(2,1)S(1)}, u32[]{:S(2)}, u32[]{:S(2)}) collective-permute-start(bf16[40,1152]{1,0:T(8,128)(2,1)S(1)} %get-tuple-element.15), channel_id=1, source_target_pairs={{16,0},{32,16},{48,32},{64,48},{80,64},{96,80},{112,96},{0,112},{1... | collective-permute-start | bytes 276488 | tf_op jit(solution)/shard_map/ppermute | solution.py:325

commit v9 on v8

--- a/solution.py
+++ b/solution.py
@@ -97,38 +97,37 @@
     def relu(value):
         return jnp.maximum(value.astype(BF16), jnp.zeros((), BF16))
 
-    def hidden(j, h_ref, before):
+    def hidden(j, h_ref, before, steps=6):
         first = PAD + WIN * j
         xs = xt[first : first + 32, :].astype(BF16)
         for p in range(4):
             h_ref[p, 0:64, :] = before[p, 192:256, :]
-        for u in range(6):
+        for u in range(steps):
             at = first + 4 * u + 3
             value = wv[0] * xt[at : at + 1, :]
             for k in range(1, 3):
                 value = value + wv[k] * xt[at + k : at + k + 1, :]
             h_ref[0, 64 + 32 * u : 96 + 32 * u, :] = relu(value)
         for p in range(1, 4):
-            h_ref[p, 64:256, :] = relu(
-                jnp.dot(w1[192 * p : 192 * (p + 1), :], xs, preferred_element_type=F32)
+            h_ref[p, 64 : 64 + 32 * steps, :] = relu(
+                jnp.dot(w1[192 * p : 192 * p + 32 * steps, :], xs, preferred_element_type=F32)
             )
-
-    sub = iota((3, 8, traces), 1)
-    even = (sub & 1) == 0
-    low = (sub & 2) == 0
 
     def pair(a, b, shift, mask):
         return jnp.where(mask, a + pltpu.roll(a, 8 - shift, 1), b + pltpu.roll(b, shift, 1))
 
-    def second(j, h_ref):
+    def second(j, h_ref, tiles=3):
+        sub = iota((tiles, 8, traces), 1)
+        even, low = (sub & 1) == 0, (sub & 2) == 0
         parts = []
         for p in range(4):
-            o = jnp.dot(w2[...], h_ref[p], preferred_element_type=F32)
-            o = jnp.maximum(o, 0.0).reshape(3, 64, traces) * wn[...][None]
-            parts.append(jnp.sum(o.reshape(3, 8, 8, traces), axis=1))
+            o = jnp.dot(w2[0 : 64 * tiles, :], h_ref[p], preferred_element_type=F32)
+            o = jnp.maximum(o, 0.0).reshape(tiles, 64, traces) * wn[...][None]
+            parts.append(jnp.sum(o.reshape(tiles, 8, 8, traces), axis=1))
         noise = pair(pair(parts[0], parts[1], 1, even), pair(parts[2], parts[3], 1, even), 2, low)
-        x = xt[PAD + WIN * j : PAD + WIN * (j + 1), :]
-        dt[WIN * j : WIN * (j + 1), :] = x - noise.reshape(WIN, traces)
+        size = 8 * tiles
+        x = xt[PAD + WIN * j : PAD + WIN * j + size, :]
+        dt[WIN * j : WIN * j + size, :] = x - noise.reshape(size, traces)
 
     xs = xt[PAD - WIN : PAD - WIN + 32, :].astype(BF16)
     for p in range(4):
@@ -138,6 +137,8 @@
         )
     hidden(0, ha, hb)
     placed = 0
+    tiles = -(-(samples - WIN * (windows - 1)) // 8)
+    steps = (samples - WIN * (windows - 1) + 4) // 4
     which = iota((TAIL, traces), 0)
     row, col = bins_ref[...] // 18 + 1, bins_ref[...] % 18 + 1
     tail = jnp.where(which == 0, row, jnp.where(which == 1, col, 0)).astype(F32).astype(BF16)
@@ -145,12 +146,12 @@
     for j in range(windows):
         this, other = hidden_bufs[j % 2], hidden_bufs[1 - j % 2]
         if j + 1 < windows:
-            hidden(j + 1, other, this)
+            hidden(j + 1, other, this, 6 if j + 2 < windows else steps - 2)
         else:
-            inside = 32 * ((samples - WIN * j + 4) // 4)
+            inside = 32 * steps
             for p in range(4):
                 this[p, inside:, :] = jnp.zeros((256 - inside, traces), BF16)
-        second(j, this)
+        second(j, this, 3 if j + 1 < windows else tiles)
         ready = min(WIN * (j + 1), samples)
         while placed < samples:
             size = 128 if placed >= samples - 256 else 256
@@ -287,14 +288,23 @@
 
 
 def inner_kernel(main_ref, left_ref, right_ref, w_ref, out_hbm, acc, vs, out, sems):
-    acc[...] = main_ref[...]
-    add_sides(acc, left_ref, right_ref, 2, 14)
-    stores = []
-    ends = [EDGE // 8 * 8] + [-(-EDGE * (m + 2) // 8) * 8 for m in range(1, 7)]
+    first, last = EDGE // 8 * 8, -(-16 * SIDE // 8) * 8
+    cut = -(-EDGE * 3 // 8) * 8
+
+    def assemble(start, stop, row, count):
+        for c in range(acc.shape[0]):
+            acc[c, start:stop, :] = main_ref[c, start:stop, :]
+        add_sides(acc, left_ref, right_ref, row, count)
+
+    assemble(first, cut, 2, 4)
+    make_taps(acc, vs, first, cut)
+    stores = convolve(1, vs, w_ref, out.at[0], out_hbm, sems.at[0], 512)
+    assemble(cut - 8, last, 5, 11)
+    ends = [cut - 8] + [-(-EDGE * (m + 2) // 8) * 8 for m in range(2, 7)]
     make_taps(acc, vs, ends[0], ends[1])
-    for k in range(6):
+    for k in range(1, 6):
         if k < 5:
-            make_taps(acc, vs, ends[k + 1], ends[k + 2])
+            make_taps(acc, vs, ends[k], ends[k + 1])
         stores += convolve(k + 1, vs, w_ref, out.at[k], out_hbm, sems.at[k], 1024 if k < 5 else 512)
     for store in stores:
         store.wait()

time: 73.1 us -> 73 us (level)
  no operation moved by 1% of the time
where the time goes in v9:
time: 73 us; the launch traced here: 72 us
  waiting for transfers between devices  32.8 us (45%)
  Pallas kernels  20.3 us (28%)
  starting transfers between devices  18.7 us (26%)
    all_to_all x1, waiting for transfers between devices, body(): lax.all_to_all(outgoing.reshape(devices, 8, width), ('inline', 'xline'),...  31 us
    pallas_call x1, Pallas kernels, body(): pl.pallas_call(denoise_kernel, out_shape=jax.ShapeDtypeStruct((slots, wid...  11.9 us
    all_to_all x1, starting transfers between devices, body(): lax.all_to_all(outgoing.reshape(devices, 8, width), ('inline', 'xline'),...  11.5 us
    ppermute x4, starting transfers between devices, neighbours(): return (lax.ppermute(last, axis, up), lax.ppermute(first, axis, down))  7.22 us
    pallas_call x1, Pallas kernels, body(): pl.pallas_call(inner_kernel, out_shape=features, in_specs=[vmem] * 4, out...  3.49 us
    pallas_call x1, Pallas kernels, body(): pl.pallas_call(outer_kernel, out_shape=features, in_specs=[vmem] * 6 + [h...  1.92 us
    ppermute x4, waiting for transfers between devices, neighbours(): return (lax.ppermute(last, axis, up), lax.ppermute(first, axis, down))  1.77 us
  transfers between devices with their start and end apart: 5, of which 3 were waited for; matrix products, arithmetic and copies ran while one was open for 0% of the time, Pallas kernels for 8%

profile of v9, /device:TPU:1, one launch (start us, length us, event | category | flops | bytes accessed | tf_op | source)
XLA Modules:
  0.0 72.0 jit_solution(3597310411275442989)
XLA Ops:
  0.0 11.9 %denoise.1 = bf16[1024,1152]{1,0:T(8,128)(2,1)} custom-call(bf16[256,1024]{1,0:T(8,128)(2,1)} %refs_0_.1, s32[1,256]{1,0:T(1,128)} %bitcast.11, s32[1,256]{1,0:T(1,128)} %bitcast.12, bf16[3,32]{1,0:T(4,128)(2,1)} %bitcast.13, bf16[96,32]{1,0:T(8,128)(2,1)} %bitcast.10, bf16[1,32]{1,0:T(2,128)(2,1)} %bitcast.14), custom_call_target="tpu_custom_call" | custom-call | tf_op jit(solution)/shard_map/denoise/pallas_call | solution.py:347
  11.9 0.0 copy-start
  12.0 0.0 copy-start.1
  12.0 11.5 %all-to-all-start = ((bf16[128,8,1152]{2,1,0:T(8,128)(2,1)}), bf16[128,8,1152]{2,1,0:T(8,128)(2,1)S(1)}, u32[]{:S(2)}, u32[]{:S(2)}) async-start(bf16[128,8,1152]{2,1,0:T(8,128)(2,1)} %bitcast.9), calls=%async_computation | async-start | bytes 4718592 | tf_op jit(solution)/shard_map/all_to_all | solution.py:390
  23.5 0.0 copy-done
  23.5 0.0 copy-done.1
  23.5 1.4 %prepare.1 = (f32[328,128]{1,0:T(8,128)S(1)}, bf16[512,216]{1,0:T(8,128)(2,1)S(1)}) custom-call(s32[16,16]{1,0:T(8,128)S(1)} %copy-done, bf16[16,27]{1,0:T(8,128)(2,1)S(1)} %copy-done.1), custom_call_target="tpu_custom_call" | custom-call | tf_op jit(solution)/shard_map/prepare/pallas_call | solution.py:382
  24.9 31.0 %all-to-all-done = bf16[128,8,1152]{2,1,0:T(8,128)(2,1)S(1)} async-done(((bf16[128,8,1152]{2,1,0:T(8,128)(2,1)}), bf16[128,8,1152]{2,1,0:T(8,128)(2,1)S(1)}, u32[]{:S(2)}, u32[]{:S(2)}) %all-to-all-start) | async-done | bytes 2359328 | tf_op jit(solution)/shard_map/all_to_all | solution.py:390
  55.9 0.5 sides.1
  56.5 0.7 %collective-permute-start = (bf16[40,1152]{1,0:T(8,128)(2,1)S(1)}, bf16[40,1152]{1,0:T(8,128)(2,1)S(1)}, u32[]{:S(2)}, u32[]{:S(2)}) collective-permute-start(bf16[40,1152]{1,0:T(8,128)(2,1)S(1)} %get-tuple-element.12), channel_id=1, source_target_pairs={{0,1},{1,2},{2,3},{3,4},{4,5},{5,6},{6,7},{7,8},{8,9},{9,10},{10,1... | collective-permute-start | bytes 276488 | tf_op jit(solution)/shard_map/ppermute | solution.py:335
  57.2 4.1 %collective-permute-start.1 = (bf16[40,1152]{1,0:T(8,128)(2,1)S(1)}, bf16[40,1152]{1,0:T(8,128)(2,1)S(1)}, u32[]{:S(2)}, u32[]{:S(2)}) collective-permute-start(bf16[40,1152]{1,0:T(8,128)(2,1)S(1)} %get-tuple-element.13), channel_id=1, source_target_pairs={{1,0},{2,1},{3,2},{4,3},{5,4},{6,5},{7,6},{8,7},{9,8},{10,9},{11,1... | collective-permute-start | bytes 276488 | tf_op jit(solution)/shard_map/ppermute | solution.py:335
  61.3 0.9 %stack.1.main_ref = f32[9,328,128]{2,1,0:T(8,128)S(1)} custom-call(bf16[1024,1152]{1,0:T(8,128)(2,1)S(1)} %bitcast.8, f32[328,128]{1,0:T(8,128)S(1)} %get-tuple-element.11.fold_ref), custom_call_target="tpu_custom_call" | custom-call | flops 1073741824 | bytes 4194304 | tf_op jit(solution)/shard_map/stack/pallas_call | solution.py:403
  62.2 1.0 %collective-permute-done.left_ref = bf16[40,1152]{1,0:T(8,128)(2,1)S(1)} collective-permute-done((bf16[40,1152]{1,0:T(8,128)(2,1)S(1)}, bf16[40,1152]{1,0:T(8,128)(2,1)S(1)}, u32[]{:S(2)}, u32[]{:S(2)}) %collective-permute-start) | collective-permute-done | bytes 92192 | tf_op jit(solution)/shard_map/ppermute | solution.py:335
  63.2 0.0 collective-permute-done.1.right_ref
  63.3 0.1 edges.1
  63.3 2.4 %collective-permute-start.2 = (bf16[40,1152]{1,0:T(8,128)(2,1)S(1)}, bf16[40,1152]{1,0:T(8,128)(2,1)S(1)}, u32[]{:S(2)}, u32[]{:S(2)}) collective-permute-start(bf16[40,1152]{1,0:T(8,128)(2,1)S(1)} %get-tuple-element.14), channel_id=1, source_target_pairs={{0,16},{16,32},{32,48},{48,64},{64,80},{80,96},{96,112},{112,0},{1... | collective-permute-start | bytes 276488 | tf_op jit(solution)/shard_map/ppermute | solution.py:335
  65.7 0.0 collective-permute-start.3
  65.7 3.5 %inner.1._ = bf16[16,16,16,1024]{3,2,1,0:T(8,128)(2,1)} custom-call(f32[9,328,128]{2,1,0:T(8,128)S(1)} %stack.1.main_ref, bf16[40,1152]{1,0:T(8,128)(2,1)S(1)} %collective-permute-done.left_ref, bf16[40,1152]{1,0:T(8,128)(2,1)S(1)} %collective-permute-done.1.right_ref, bf16[512,216]{1,0:T(8,128)(2,1)S(1)} %get-tuple-element.16.w_ref), custom_call_target="tpu_custom_call" | custom-call | flops 4294967296 | bytes 8388608 | tf_op jit(solution)/shard_map/inner/pallas_call | solution.py:432
  69.2 0.0 collective-permute-done.2.above_ref
  69.2 0.8 %collective-permute-done.3.below_ref = bf16[40,1152]{1,0:T(8,128)(2,1)S(1)} collective-permute-done((bf16[40,1152]{1,0:T(8,128)(2,1)S(1)}, bf16[40,1152]{1,0:T(8,128)(2,1)S(1)}, u32[]{:S(2)}, u32[]{:S(2)}) %collective-permute-start.3) | collective-permute-done | bytes 92192 | tf_op jit(solution)/shard_map/ppermute | solution.py:335
  70.0 1.9 %outer.1 = bf16[16,16,16,1024]{3,2,1,0:T(8,128)(2,1)} custom-call(f32[9,328,128]{2,1,0:T(8,128)S(1)} %stack.1.main_ref, bf16[40,1152]{1,0:T(8,128)(2,1)S(1)} %collective-permute-done.left_ref, bf16[40,1152]{1,0:T(8,128)(2,1)S(1)} %collective-permute-done.1.right_ref, ...), custom_call_target="tpu_custom_call", output_to_operand_aliasing={{}: (6, {})} | custom-call | tf_op jit(solution)/shard_map/outer/pallas_call | solution.py:442
Async XLA Ops:
  11.9 11.5 %copy-start = (s32[16,16]{1,0:T(8,128)S(1)}, s32[16,16]{1,0:T(8,128)}, u32[]{:S(2)}) copy-start(s32[16,16]{1,0:T(8,128)} %fold_ref.1) | copy-start | bytes 3076
  12.0 11.5 %copy-start.1 = (bf16[16,27]{1,0:T(8,128)(2,1)S(1)}, bf16[16,27]{1,0:T(8,128)(2,1)}, u32[]{:S(2)}) copy-start(bf16[16,27]{1,0:T(8,128)(2,1)} %wv_ref.1) | copy-start | bytes 2596
  12.0 44.0 %all-to-all-start = ((bf16[128,8,1152]{2,1,0:T(8,128)(2,1)}), bf16[128,8,1152]{2,1,0:T(8,128)(2,1)S(1)}, u32[]{:S(2)}, u32[]{:S(2)}) async-start(bf16[128,8,1152]{2,1,0:T(8,128)(2,1)} %bitcast.9), calls=%async_computation | async-start | bytes 4718592 | tf_op jit(solution)/shard_map/all_to_all | solution.py:390
  56.5 6.8 %collective-permute-start = (bf16[40,1152]{1,0:T(8,128)(2,1)S(1)}, bf16[40,1152]{1,0:T(8,128)(2,1)S(1)}, u32[]{:S(2)}, u32[]{:S(2)}) collective-permute-start(bf16[40,1152]{1,0:T(8,128)(2,1)S(1)} %get-tuple-element.12), channel_id=1, source_target_pairs={{0,1},{1,2},{2,3},{3,4},{4,5},{5,6},{6,7},{7,8},{8,9},{9,10},{10,1... | collective-permute-start | bytes 276488 | tf_op jit(solution)/shard_map/ppermute | solution.py:335
  57.2 6.0 %collective-permute-start.1 = (bf16[40,1152]{1,0:T(8,128)(2,1)S(1)}, bf16[40,1152]{1,0:T(8,128)(2,1)S(1)}, u32[]{:S(2)}, u32[]{:S(2)}) collective-permute-start(bf16[40,1152]{1,0:T(8,128)(2,1)S(1)} %get-tuple-element.13), channel_id=1, source_target_pairs={{1,0},{2,1},{3,2},{4,3},{5,4},{6,5},{7,6},{8,7},{9,8},{10,9},{11,1... | collective-permute-start | bytes 276488 | tf_op jit(solution)/shard_map/ppermute | solution.py:335
  63.3 5.9 %collective-permute-start.2 = (bf16[40,1152]{1,0:T(8,128)(2,1)S(1)}, bf16[40,1152]{1,0:T(8,128)(2,1)S(1)}, u32[]{:S(2)}, u32[]{:S(2)}) collective-permute-start(bf16[40,1152]{1,0:T(8,128)(2,1)S(1)} %get-tuple-element.14), channel_id=1, source_target_pairs={{0,16},{16,32},{32,48},{48,64},{64,80},{80,96},{96,112},{112,0},{1... | collective-permute-start | bytes 276488 | tf_op jit(solution)/shard_map/ppermute | solution.py:335
  65.7 4.3 %collective-permute-start.3 = (bf16[40,1152]{1,0:T(8,128)(2,1)S(1)}, bf16[40,1152]{1,0:T(8,128)(2,1)S(1)}, u32[]{:S(2)}, u32[]{:S(2)}) collective-permute-start(bf16[40,1152]{1,0:T(8,128)(2,1)S(1)} %get-tuple-element.15), channel_id=1, source_target_pairs={{16,0},{32,16},{48,32},{64,48},{80,64},{96,80},{112,96},{0,112},{1... | collective-permute-start | bytes 276488 | tf_op jit(solution)/shard_map/ppermute | solution.py:335
